TPU v7x, 256 devices: a whole 4x4x8 slice. The times are simulated.
256 devices in a mesh: comp: 4 (over y), horiz: 16 (over x_lo, z), trc: 4 (over x_hi, core).
Axes of the slice: x: 4 (x_hi: 2, x_lo: 2; x = x_hi * 2 + x_lo), y: 4, z: 8, core: 2. Of those that a mesh axis runs over, the one named last changes fastest.
Arguments:
- tracers: float32 [16, 64, 512, 256], P(('comp', 'trc'), None, 'horiz'), may hold values from -6 to 6
- eastward: float32 [64, 512, 256], P(('comp', 'trc'), 'horiz'), may hold values from -1.2 to 1.2
- northward: float32 [64, 512, 256], P(('comp', 'trc'), 'horiz'), may hold values from -1.2 to 1.2
- surface_height: float32 [512, 256], P('horiz'), may hold values from -6 to 6
- sea_mask: int32 [512, 256], P('horiz'), may hold values 0 or 1
- mixing: float32 [64, 512, 256], P(('comp', 'trc'), 'horiz'), may hold values from 0.02 to 0.15
- sunlight: float32 [512, 256], P('horiz'), may hold values from 0.5 to 4
- reaction: float32 [16, 16], replicated, may hold values from -1.5 to 1.5
Outputs:
- east_out: float32 [64, 512, 256], P(('comp', 'trc'), 'horiz')
- north_out: float32 [64, 512, 256], P(('comp', 'trc'), 'horiz')
- tracers_out: float32 [16, 64, 512, 256], P(None, ('comp', 'trc'), 'horiz')
- heating: float32 [64, 512, 256], P(('comp', 'trc'), 'horiz')
All inputs are finite; a program needn't handle non-finite values. No bound on the sum of `sea_mask` on one device may be relied on, other than what follows from the above.
Results may differ from a plain program's by a relative error of at most 0.00017.
Values sent between devices are 32-bit elements; how exact they have to be, the bound alone decides.
No kernel may reach another device: no remote copies, remote signals or barrier semaphores. Data moves between devices by JAX's collectives and lax.ppermute only.
A program may use at most 64 MiB of HBM per device.

v0:
```python
import jax
import jax.numpy as jnp
from jax import lax
from jax.sharding import PartitionSpec as P

SUBSTEPS = 4


TIME_STEP = 0.25
GRAVITY = 1.0
VISCOSITY = 0.05
COURANT = 0.2
HALF_LIGHT = 0.3


def with_halo(block, sides, width):
    for axis, dim in sides:
        count = lax.axis_size(axis)
        forward = [(i, i + 1) for i in range(count - 1)]
        backward = [(target, source) for source, target in forward]
        low = lax.ppermute(
            lax.slice_in_dim(block, block.shape[dim] - width, None, axis=dim), axis, forward
        )
        high = lax.ppermute(lax.slice_in_dim(block, 0, width, axis=dim), axis, backward)
        block = jnp.concatenate([low, block, high], axis=dim)
    return block


def entering(shard, axis, combine, identity):
    length, position = (lax.axis_size(axis), lax.axis_index(axis))
    everything = lax.all_gather(shard, axis)
    start = jnp.broadcast_to(jnp.asarray(identity, shard.dtype), shard.shape)

    def lap(k, before):
        reached = k < position
        new = combine(before, everything[k])
        return jnp.where(reached, new, before)

    return lax.fori_loop(0, length, lap, start)


def pad_rows(array):
    return jnp.pad(array, [(0, 0)] * (array.ndim - 1) + [(1, 1)])


def ocean_step(east_ext, north_ext, height_ext, wet_ext, mixing, bottom_keep):
    width = east_ext.shape[1] - 4
    rows = east_ext.shape[2]
    coriolis = 0.5 + 0.5 * jnp.arange(rows, dtype=jnp.float32) / rows
    east_pad = pad_rows(east_ext)
    north_pad = pad_rows(north_ext)
    height_pad = pad_rows(height_ext)
    wet_pad = pad_rows(wet_ext)
    east_mid = east_ext[:, 1 : width + 2]
    east_lap = (
        east_ext[:, 2 : width + 3]
        + east_ext[:, 0 : width + 1]
        + east_pad[:, 1 : width + 2, 2:]
        + east_pad[:, 1 : width + 2, :-2]
        - 4.0 * east_mid
    )
    north_avg = 0.25 * (
        north_pad[:, 1 : width + 2, 1:-1]
        + north_pad[:, 2 : width + 3, 1:-1]
        + north_pad[:, 1 : width + 2, :-2]
        + north_pad[:, 2 : width + 3, :-2]
    )
    slope_x = height_ext[2 : width + 3] - height_ext[1 : width + 2]
    open_x = wet_ext[1 : width + 2] * wet_ext[2 : width + 3]
    east_new = open_x * (
        east_mid + TIME_STEP * (coriolis * north_avg - GRAVITY * slope_x + VISCOSITY * east_lap)
    )
    north_mid = north_ext[:, 2 : width + 2]
    north_lap = (
        north_ext[:, 3 : width + 3]
        + north_ext[:, 1 : width + 1]
        + north_pad[:, 2 : width + 2, 2:]
        + north_pad[:, 2 : width + 2, :-2]
        - 4.0 * north_mid
    )
    east_avg = 0.25 * (
        east_pad[:, 2 : width + 2, 1:-1]
        + east_pad[:, 1 : width + 1, 1:-1]
        + east_pad[:, 2 : width + 2, 2:]
        + east_pad[:, 1 : width + 1, 2:]
    )
    slope_y = height_pad[2 : width + 2, 2:] - height_pad[2 : width + 2, 1:-1]
    open_y = wet_pad[2 : width + 2, 1:-1] * wet_pad[2 : width + 2, 2:]
    north_new = open_y * (
        north_mid + TIME_STEP * (-coriolis * east_avg - GRAVITY * slope_y + VISCOSITY * north_lap)
    )
    east_out = east_new[:, 1:]
    speed = jnp.minimum(east_out * east_out + north_new * north_new, 1.0)
    kappa = wet_ext[2 : width + 2] * mixing * (1.0 + speed) * bottom_keep
    return (east_out, north_new, COURANT * east_new, COURANT * north_new, kappa)


def advance(padded, flux_x, flux_y, kappa, kappa_up):
    inner = padded[..., 1:-1, 1:-1, :]
    level_mid = padded[..., 1:-1, :, :]
    width = inner.shape[-2]
    east_flux = (
        jnp.maximum(flux_x, 0.0) * level_mid[..., 0 : width + 1, :]
        + jnp.minimum(flux_x, 0.0) * level_mid[..., 1 : width + 2, :]
    )
    across_x = east_flux[..., :-1, :] - east_flux[..., 1:, :]
    north_cells = jnp.pad(inner[..., 1:], [(0, 0)] * (inner.ndim - 1) + [(0, 1)])
    north_flux = jnp.maximum(flux_y, 0.0) * inner + jnp.minimum(flux_y, 0.0) * north_cells
    south_flux = jnp.pad(north_flux[..., :-1], [(0, 0)] * (inner.ndim - 1) + [(1, 0)])
    across_y = south_flux - north_flux
    below = kappa * (padded[..., 2:, 1:-1, :] - inner)
    above = kappa_up * (inner - padded[..., :-2, 1:-1, :])
    return inner + across_x + across_y + below - above


def add_terms(earlier, later):
    return earlier + later


def per_device(tracers, eastward, northward, surface_height, sea_mask, mixing, sunlight, reaction):
    depth_dev = eastward.shape[0]
    groups = lax.axis_size(("comp", "trc"))
    levels = depth_dev * groups
    first_level = lax.axis_index(("comp", "trc")) * depth_dev
    keep = (first_level + jnp.arange(depth_dev) < levels - 1).astype(jnp.float32)[:, None, None]
    wet_local = sea_mask.astype(jnp.float32)
    stacked = jnp.concatenate([eastward, northward, surface_height[None], wet_local[None]], 0)
    edges = with_halo(stacked, (("horiz", 1),), 2)
    east_out, north_out, flux_x, flux_y, kappa = ocean_step(
        edges[:depth_dev],
        edges[depth_dev : 2 * depth_dev],
        edges[2 * depth_dev],
        edges[2 * depth_dev + 1],
        mixing,
        keep,
    )
    flux_all, north_all, kappa_all = (
        lax.all_gather(flux_x, ("comp", "trc"), axis=0, tiled=True),
        lax.all_gather(flux_y, ("comp", "trc"), axis=0, tiled=True),
        lax.all_gather(kappa, ("comp", "trc"), axis=0, tiled=True),
    )
    kappa_up = jnp.pad(kappa_all[:-1], ((1, 0), (0, 0), (0, 0)))
    field = tracers
    for step in range(SUBSTEPS):
        sides = with_halo(field, (("horiz", 2),), 1)
        padded = jnp.pad(sides, ((0, 0), (1, 1), (0, 0), (0, 0)))
        field = advance(padded, flux_all, north_all, kappa_all, kappa_up)
    moved = lax.all_to_all(field, ("comp", "trc"), split_axis=1, concat_axis=0, tiled=True)
    tau = (0.5 + moved[0] * moved[0]) / levels
    total = jnp.sum(tau, 0)
    above = entering(total, ("comp", "trc"), add_terms, jnp.zeros_like(total))
    depth_top = above + (jnp.cumsum(tau, 0) - tau)
    light_top = sunlight * jnp.exp(-depth_top)
    heating = levels * light_top * (1.0 - jnp.exp(-tau))
    light_mid = light_top * jnp.exp(-0.5 * tau)
    limit = light_mid / (light_mid + HALF_LIGHT)
    growth = jnp.einsum("ij,jlxy->ilxy", reaction, moved, precision=lax.Precision.HIGHEST)
    tracers_out = moved + limit * growth
    return (east_out, north_out, tracers_out, heating)


def solution(mesh):
    return jax.shard_map(
        per_device,
        mesh=mesh,
        in_specs=(
            P(("comp", "trc"), None, "horiz", None),
            P(("comp", "trc"), "horiz", None),
            P(("comp", "trc"), "horiz", None),
            P("horiz", None),
            P("horiz", None),
            P(("comp", "trc"), "horiz", None),
            P("horiz", None),
            P(),
        ),
        out_specs=(
            P(("comp", "trc"), "horiz", None),
            P(("comp", "trc"), "horiz", None),
            P(None, ("comp", "trc"), "horiz", None),
            P(("comp", "trc"), "horiz", None),
        ),
        check_vma=False,
    )
```

profile of v0, /device:TPU:7, one launch (start us, length us, event | category | flops | bytes accessed | tf_op | source)
XLA Modules:
  0.0 338.1 jit_solution(2410745276192525370)
XLA Ops:
  9.0 7.8 %collective-permute-start.1 = (f32[10,2,256]{2,1,0:T(2,128)S(1)}, f32[10,2,256]{2,1,0:T(2,128)S(1)}, u32[]{:S(2)}, u32[]{:S(2)}) collective-permute-start(f32[10,2,256]{2,1,0:T(2,128)S(1)} %get-tuple-element.140), channel_id=1, source_target_pairs={{4,0},{8,4},{12,8},{16,12},{20,16},{24,20},{28,24},{32,28},{36,32}... | collective-permute-start | bytes 61448 | tf_op jit(solution)/shard_map/ppermute | solution.py:24
  18.7 4.7 %collective-permute-done = f32[10,2,256]{2,1,0:T(2,128)S(1)} collective-permute-done((f32[10,2,256]{2,1,0:T(2,128)S(1)}, f32[10,2,256]{2,1,0:T(2,128)S(1)}, u32[]{:S(2)}, u32[]{:S(2)}) %collective-permute-start) | collective-permute-done | bytes 20512 | tf_op jit(solution)/shard_map/ppermute | solution.py:21
  31.6 5.5 %collective-permute-start.3 = (f32[1,64,1,256]{3,2,1,0:T(1,128)S(1)}, f32[1,64,1,256]{3,2,1,0:T(1,128)S(1)}, u32[]{:S(2)}, u32[]{:S(2)}) collective-permute-start(f32[1,64,1,256]{3,2,1,0:T(1,128)S(1)} %get-tuple-element.132), channel_id=1, source_target_pairs={{4,0},{8,4},{12,8},{16,12},{20,16},{24,20},{28,24},{32,28},{36,32}... | collective-permute-start | bytes 196616 | tf_op jit(solution)/shard_map/ppermute | solution.py:24
  41.0 36.2 %all-gather.9.cloned.1.call-done = f32[64,32,256]{2,1,0:T(8,128)} async-done(((f32[4,32,256]{2,1,0:T(8,128)}), f32[64,32,256]{2,1,0:T(8,128)}) %all-gather.9.cloned.1.call-update) | async-done | bytes 2097168 | tf_op jit(solution)/shard_map/all_gather | solution.py:140
  77.1 3.1 slice.348
  80.2 51.7 %all-gather.7.cloned.1.call-done = f32[64,32,256]{2,1,0:T(8,128)} async-done(((f32[4,32,256]{2,1,0:T(8,128)}), f32[64,32,256]{2,1,0:T(8,128)}) %all-gather.7.cloned.1.call-update) | async-done | bytes 2097168 | tf_op jit(solution)/shard_map/all_gather | solution.py:139
  131.9 4.3 %fusion.34 = f32[1,64,32,256]{3,2,1,0:T(8,128)} fusion(f32[1,64,32,256]{3,2,1,0:T(8,128)S(1)} %copy-done.1, f32[1,64,32,255]{3,2,1,0:T(8,128)} %slice.304, f32[64,32,256]{2,1,0:T(8,128)} %all-gather.7.cloned.1.call-done), kind=kLoop, calls=%fused_computation.70 | loop fusion | flops 2621440 | bytes 8380416 | tf_op jit(solution)/shard_map/add | solution.py:108
  136.3 51.4 %all-gather.5.cloned.1.call-done = f32[64,33,256]{2,1,0:T(8,128)} async-done(((f32[4,33,256]{2,1,0:T(8,128)}), f32[64,33,256]{2,1,0:T(8,128)}) %all-gather.5.cloned.1.call-update) | async-done | bytes 2162704 | tf_op jit(solution)/shard_map/all_gather | solution.py:138
  187.6 4.2 %fusion.2 = f32[1,64,33,256]{3,2,1,0:T(8,128)} fusion(f32[64,32,256]{2,1,0:T(8,128)S(1)} %bitcast.131, f32[64,1,256]{2,1,0:T(1,128)S(1)} %bitcast.148, f32[64,1,256]{2,1,0:T(1,128)S(1)} %bitcast.149, f32[64,33,256]{2,1,0:T(8,128)} %all-gather.5.cloned.1.call-done), kind=kLoop, calls=%fused_computation.14 | loop fusion | flops 3784704 | bytes 6553600 | tf_op jit(solution)/shard_map/add | solution.py:103
  191.8 7.1 %fusion.29 = f32[1,64,32,256]{3,2,1,0:T(8,128)S(1)} fusion(f32[1,64,32,256]{3,2,1,0:T(8,128)S(1)} %copy-done.1, f32[1,66,34,256]{3,2,1,0:T(8,128)} %select_maximum_fusion.6, f32[1,64,33,256]{3,2,1,0:T(8,128)} %fusion.2, f32[64,32,256]{2,1,0:T(8,128)S(1)} %copy-done.2, f32[1,64,32,256]{3,2,1,0:T(8,128)} %fusion.34, f32[1,64,32,255]{3,2,1,0:T(8,128)} %bitcast.135, ...), kind=kLoop, calls=%fused_computation.58 | loop fusion | flops 5242880 | bytes 20930560 | tf_op jit(solution)/shard_map/sub | solution.py:113
  199.6 3.2 collective-permute-start.4
  202.8 4.2 %collective-permute-start.5 = (f32[1,64,1,256]{3,2,1,0:T(1,128)S(1)}, f32[1,64,1,256]{3,2,1,0:T(1,128)S(1)}, u32[]{:S(2)}, u32[]{:S(2)}) collective-permute-start(f32[1,64,1,256]{3,2,1,0:T(1,128)S(1)} %get-tuple-element.130), channel_id=1, source_target_pairs={{4,0},{8,4},{12,8},{16,12},{20,16},{24,20},{28,24},{32,28},{36,32}... | collective-permute-start | bytes 196616 | tf_op jit(solution)/shard_map/ppermute | solution.py:24
  211.8 2.2 fusion.4
  213.9 6.9 %fusion.23 = f32[1,64,32,256]{3,2,1,0:T(8,128)S(1)} fusion(f32[1,64,32,256]{3,2,1,0:T(8,128)S(1)} %fusion.29, f32[1,66,34,256]{3,2,1,0:T(8,128)} %select_maximum_fusion.4, f32[1,64,33,256]{3,2,1,0:T(8,128)} %fusion.4, f32[64,32,256]{2,1,0:T(8,128)S(1)} %copy-done.2, f32[1,64,32,256]{3,2,1,0:T(8,128)} %fusion.35, f32[1,64,32,255]{3,2,1,0:T(8,128)} %bitcast.133, ...), kind=kLoop, calls=%fused_computation.49 | loop fusion | flops 5242880 | bytes 20930560 | tf_op jit(solution)/shard_map/sub | solution.py:113
  223.4 5.7 %collective-permute-start.7 = (f32[1,64,1,256]{3,2,1,0:T(1,128)S(1)}, f32[1,64,1,256]{3,2,1,0:T(1,128)S(1)}, u32[]{:S(2)}, u32[]{:S(2)}) collective-permute-start(f32[1,64,1,256]{3,2,1,0:T(1,128)S(1)} %get-tuple-element.128), channel_id=1, source_target_pairs={{4,0},{8,4},{12,8},{16,12},{20,16},{24,20},{28,24},{32,28},{36,32}... | collective-permute-start | bytes 196616 | tf_op jit(solution)/shard_map/ppermute | solution.py:24
  233.8 2.2 fusion.6
  236.0 6.9 %fusion.17 = f32[1,64,32,256]{3,2,1,0:T(8,128)S(1)} fusion(f32[1,64,32,256]{3,2,1,0:T(8,128)S(1)} %fusion.23, f32[1,66,34,256]{3,2,1,0:T(8,128)} %select_maximum_fusion.2, f32[1,64,33,256]{3,2,1,0:T(8,128)} %fusion.6, f32[64,32,256]{2,1,0:T(8,128)S(1)} %copy-done.2, f32[1,64,32,256]{3,2,1,0:T(8,128)} %fusion.36, f32[1,64,32,255]{3,2,1,0:T(8,128)} %bitcast.134, ...), kind=kLoop, calls=%fused_computation.40 | loop fusion | flops 5242880 | bytes 20930560 | tf_op jit(solution)/shard_map/sub | solution.py:113
  245.5 5.5 %collective-permute-start.9 = (f32[1,64,1,256]{3,2,1,0:T(1,128)S(1)}, f32[1,64,1,256]{3,2,1,0:T(1,128)S(1)}, u32[]{:S(2)}, u32[]{:S(2)}) collective-permute-start(f32[1,64,1,256]{3,2,1,0:T(1,128)S(1)} %get-tuple-element.126), channel_id=1, source_target_pairs={{4,0},{8,4},{12,8},{16,12},{20,16},{24,20},{28,24},{32,28},{36,32}... | collective-permute-start | bytes 196616 | tf_op jit(solution)/shard_map/ppermute | solution.py:24
  256.4 7.2 %fusion.11 = f32[1,64,32,256]{3,2,0,1:T(8,128)} fusion(f32[1,64,32,256]{3,2,1,0:T(8,128)S(1)} %fusion.17, f32[1,66,34,256]{3,2,1,0:T(8,128)} %select_maximum_fusion, f32[1,64,33,256]{3,2,1,0:T(8,128)} %fusion.8, f32[64,32,256]{2,1,0:T(8,128)S(1)} %copy-done.2, f32[1,64,32,256]{3,2,1,0:T(8,128)S(1)} %fusion.37, f32[1,64,32,255]{3,2,1,0:T(8,128)S(1)} %bitcast.132, ...), kind=kLoop, calls=%fused_computation.31 | loop fusion | flops 5242880 | bytes 20930560 | tf_op jit(solution)/shard_map/sub | solution.py:113
  263.6 8.9 %all-to-all-start = ((f32[1,64,32,256]{3,2,0,1:T(8,128)}), f32[1,64,32,256]{3,2,0,1:T(8,128)S(1)}, u32[]{:S(2)}, u32[]{:S(2)}) async-start(f32[1,64,32,256]{3,2,0,1:T(8,128)} %fusion.11), calls=%async_computation | async-start | bytes 4194304 | tf_op jit(solution)/shard_map/all_to_all | solution.py:148
  272.5 26.6 %all-to-all-done = f32[1,64,32,256]{3,2,0,1:T(8,128)S(1)} async-done(((f32[1,64,32,256]{3,2,0,1:T(8,128)}), f32[1,64,32,256]{3,2,0,1:T(8,128)S(1)}, u32[]{:S(2)}, u32[]{:S(2)}) %all-to-all-start) | async-done | bytes 2097184 | tf_op jit(solution)/shard_map/all_to_all | solution.py:148
  299.1 24.2 %all-gather = f32[512,256]{1,0:T(8,128)S(1)} all-gather(f32[32,256]{1,0:T(8,128)S(1)} %fusion.87), channel_id=2, replica_groups=mesh['comp'=4,'horiz'=16,'trc'=4] {'comp','trc'}, dimensions={0}, use_global_device_ids=true | all-gather | bytes 557056 | tf_op jit(solution)/shard_map/all_gather | solution.py:31
  324.8 4.3 %bitcast_add_fusion = f32[16,4,32,256]{3,0,2,1:T(8,128)S(1)} fusion(f32[16,4,32,256]{3,2,1,0:T(8,128)S(1)} %bitcast.139, f32[4,32,256]{2,1,0:T(8,128)S(1)} %fusion.54, f32[16,16]{1,0:T(8,128)S(1)} %copy-done), kind=kOutput, calls=%fused_computation.65 | convolution fusion | flops 101711872 | bytes 4326400 | tf_op jit(solution)/shard_map/ij,jlxy->ilxy/dot_general | solution.py:157
  329.1 2.5 copy.20
  (107 shorter events, 38.0 us)
Async XLA Ops:
  7.2 317.6 %copy-start = (f32[16,16]{1,0:T(8,128)S(1)}, f32[16,16]{1,0:T(8,128)}, u32[]{:S(2)}) copy-start(f32[16,16]{1,0:T(8,128)} %param.17) | copy-start | bytes 3076
  7.2 18.0 %copy-start.16 = (s32[32,256]{1,0:T(8,128)S(1)}, s32[32,256]{1,0:T(8,128)}, u32[]{:S(2)}) copy-start(s32[32,256]{1,0:T(8,128)} %param.14) | copy-start | bytes 98308
  7.2 18.0 %copy-start.13 = (f32[32,256]{1,0:T(8,128)S(1)}, f32[32,256]{1,0:T(8,128)}, u32[]{:S(2)}) copy-start(f32[32,256]{1,0:T(8,128)} %param.13) | copy-start | bytes 98308
  7.2 18.1 %copy-start.12 = (f32[4,32,256]{2,1,0:T(8,128)S(1)}, f32[4,32,256]{2,1,0:T(8,128)}, u32[]{:S(2)}) copy-start(f32[4,32,256]{2,1,0:T(8,128)} %param.11) | copy-start | bytes 393220
  7.2 18.1 %copy-start.11 = (f32[4,32,256]{2,1,0:T(8,128)S(1)}, f32[4,32,256]{2,1,0:T(8,128)}, u32[]{:S(2)}) copy-start(f32[4,32,256]{2,1,0:T(8,128)} %param.12) | copy-start | bytes 393220
  7.2 69.9 %all-gather.9.cloned.1.call-start = ((), (), s32[]{:S(2)}) async-start(), calls=%async_computation.3 | async-start | bytes 2228224 | tf_op jit(solution)/shard_map/all_gather | solution.py:140
  9.0 9.7 %collective-permute-start.1 = (f32[10,2,256]{2,1,0:T(2,128)S(1)}, f32[10,2,256]{2,1,0:T(2,128)S(1)}, u32[]{:S(2)}, u32[]{:S(2)}) collective-permute-start(f32[10,2,256]{2,1,0:T(2,128)S(1)} %get-tuple-element.140), channel_id=1, source_target_pairs={{4,0},{8,4},{12,8},{16,12},{20,16},{24,20},{28,24},{32,28},{36,32}... | collective-permute-start | bytes 61448 | tf_op jit(solution)/shard_map/ppermute | solution.py:24
  16.7 6.6 %collective-permute-start = (f32[10,2,256]{2,1,0:T(2,128)S(1)}, f32[10,2,256]{2,1,0:T(2,128)S(1)}, u32[]{:S(2)}, u32[]{:S(2)}) collective-permute-start(f32[10,2,256]{2,1,0:T(2,128)S(1)} %get-tuple-element.139), channel_id=1, source_target_pairs={{0,4},{4,8},{8,12},{12,16},{16,20},{20,24},{24,28},{28,32},{32,36}... | collective-permute-start | bytes 61448 | tf_op jit(solution)/shard_map/ppermute | solution.py:21
  27.3 11.7 %copy-start.14 = (f32[4,32,256]{2,1,0:T(8,128)}, f32[4,32,256]{2,1,0:T(8,128)S(1)}, u32[]{:S(2)}) copy-start(f32[4,32,256]{2,1,0:T(8,128)S(1)} %get-tuple-element.120) | copy-start | bytes 393220
  28.1 103.9 %all-gather.7.cloned.1.call-start = ((), (), s32[]{:S(2)}) async-start(), calls=%async_computation.2 | async-start | bytes 2228224 | tf_op jit(solution)/shard_map/all_gather | solution.py:139
  28.8 158.8 %all-gather.5.cloned.1.call-start = ((), (), s32[]{:S(2)}) async-start(), calls=%async_computation.1 | async-start | bytes 2785280 | tf_op jit(solution)/shard_map/all_gather | solution.py:138
  29.7 9.3 %collective-permute-start.2 = (f32[1,64,1,256]{3,2,1,0:T(1,128)S(1)}, f32[1,64,1,256]{3,2,1,0:T(1,128)S(1)}, u32[]{:S(2)}, u32[]{:S(2)}) collective-permute-start(f32[1,64,1,256]{3,2,1,0:T(1,128)S(1)} %get-tuple-element.131), channel_id=1, source_target_pairs={{0,4},{4,8},{8,12},{12,16},{16,20},{20,24},{24,28},{28,32},{32,36}... | collective-permute-start | bytes 196616 | tf_op jit(solution)/shard_map/ppermute | solution.py:21
  31.6 7.4 %collective-permute-start.3 = (f32[1,64,1,256]{3,2,1,0:T(1,128)S(1)}, f32[1,64,1,256]{3,2,1,0:T(1,128)S(1)}, u32[]{:S(2)}, u32[]{:S(2)}) collective-permute-start(f32[1,64,1,256]{3,2,1,0:T(1,128)S(1)} %get-tuple-element.132), channel_id=1, source_target_pairs={{4,0},{8,4},{12,8},{16,12},{20,16},{24,20},{28,24},{32,28},{36,32}... | collective-permute-start | bytes 196616 | tf_op jit(solution)/shard_map/ppermute | solution.py:24
  198.9 8.1 %copy-start.8 = (f32[64,32,256]{2,1,0:T(8,128)S(1)}, f32[64,32,256]{2,1,0:T(8,128)}, u32[]{:S(2)}) copy-start(f32[64,32,256]{2,1,0:T(8,128)} %all-gather.7.cloned.1.call-done) | copy-start | bytes 6291460
  199.6 9.5 %collective-permute-start.4 = (f32[1,64,1,256]{3,2,1,0:T(1,128)S(1)}, f32[1,64,1,256]{3,2,1,0:T(1,128)S(1)}, u32[]{:S(2)}, u32[]{:S(2)}) collective-permute-start(f32[1,64,1,256]{3,2,1,0:T(1,128)S(1)} %get-tuple-element.129), channel_id=1, source_target_pairs={{0,4},{4,8},{8,12},{12,16},{16,20},{20,24},{24,28},{28,32},{32,36}... | collective-permute-start | bytes 196616 | tf_op jit(solution)/shard_map/ppermute | solution.py:21
  202.8 6.3 %collective-permute-start.5 = (f32[1,64,1,256]{3,2,1,0:T(1,128)S(1)}, f32[1,64,1,256]{3,2,1,0:T(1,128)S(1)}, u32[]{:S(2)}, u32[]{:S(2)}) collective-permute-start(f32[1,64,1,256]{3,2,1,0:T(1,128)S(1)} %get-tuple-element.130), channel_id=1, source_target_pairs={{4,0},{8,4},{12,8},{16,12},{20,16},{24,20},{28,24},{32,28},{36,32}... | collective-permute-start | bytes 196616 | tf_op jit(solution)/shard_map/ppermute | solution.py:24
  220.8 8.3 %copy-start.9 = (f32[64,32,256]{2,1,0:T(8,128)S(1)}, f32[64,32,256]{2,1,0:T(8,128)}, u32[]{:S(2)}) copy-start(f32[64,32,256]{2,1,0:T(8,128)} %all-gather.7.cloned.1.call-done) | copy-start | bytes 6291460
  221.5 9.7 %collective-permute-start.6 = (f32[1,64,1,256]{3,2,1,0:T(1,128)S(1)}, f32[1,64,1,256]{3,2,1,0:T(1,128)S(1)}, u32[]{:S(2)}, u32[]{:S(2)}) collective-permute-start(f32[1,64,1,256]{3,2,1,0:T(1,128)S(1)} %get-tuple-element.127), channel_id=1, source_target_pairs={{0,4},{4,8},{8,12},{12,16},{16,20},{20,24},{24,28},{28,32},{32,36}... | collective-permute-start | bytes 196616 | tf_op jit(solution)/shard_map/ppermute | solution.py:21
  223.4 7.7 %collective-permute-start.7 = (f32[1,64,1,256]{3,2,1,0:T(1,128)S(1)}, f32[1,64,1,256]{3,2,1,0:T(1,128)S(1)}, u32[]{:S(2)}, u32[]{:S(2)}) collective-permute-start(f32[1,64,1,256]{3,2,1,0:T(1,128)S(1)} %get-tuple-element.128), channel_id=1, source_target_pairs={{4,0},{8,4},{12,8},{16,12},{20,16},{24,20},{28,24},{32,28},{36,32}... | collective-permute-start | bytes 196616 | tf_op jit(solution)/shard_map/ppermute | solution.py:24
  242.9 8.1 %copy-start.10 = (f32[64,32,256]{2,1,0:T(8,128)S(1)}, f32[64,32,256]{2,1,0:T(8,128)}, u32[]{:S(2)}) copy-start(f32[64,32,256]{2,1,0:T(8,128)} %all-gather.7.cloned.1.call-done) | copy-start | bytes 6291460
  243.6 8.2 %collective-permute-start.8 = (f32[1,64,1,256]{3,2,1,0:T(1,128)S(1)}, f32[1,64,1,256]{3,2,1,0:T(1,128)S(1)}, u32[]{:S(2)}, u32[]{:S(2)}) collective-permute-start(f32[1,64,1,256]{3,2,1,0:T(1,128)S(1)} %get-tuple-element.125), channel_id=1, source_target_pairs={{0,4},{4,8},{8,12},{12,16},{16,20},{20,24},{24,28},{28,32},{32,36}... | collective-permute-start | bytes 196616 | tf_op jit(solution)/shard_map/ppermute | solution.py:21
  245.5 6.8 %collective-permute-start.9 = (f32[1,64,1,256]{3,2,1,0:T(1,128)S(1)}, f32[1,64,1,256]{3,2,1,0:T(1,128)S(1)}, u32[]{:S(2)}, u32[]{:S(2)}) collective-permute-start(f32[1,64,1,256]{3,2,1,0:T(1,128)S(1)} %get-tuple-element.126), channel_id=1, source_target_pairs={{4,0},{8,4},{12,8},{16,12},{20,16},{24,20},{28,24},{32,28},{36,32}... | collective-permute-start | bytes 196616 | tf_op jit(solution)/shard_map/ppermute | solution.py:24
  263.6 60.4 %copy-start.15 = (f32[32,256]{1,0:T(8,128)S(1)}, f32[32,256]{1,0:T(8,128)}, u32[]{:S(2)}) copy-start(f32[32,256]{1,0:T(8,128)} %param.16) | copy-start | bytes 98308
  263.6 35.5 %all-to-all-start = ((f32[1,64,32,256]{3,2,0,1:T(8,128)}), f32[1,64,32,256]{3,2,0,1:T(8,128)S(1)}, u32[]{:S(2)}, u32[]{:S(2)}) async-start(f32[1,64,32,256]{3,2,0,1:T(8,128)} %fusion.11), calls=%async_computation | async-start | bytes 4194304 | tf_op jit(solution)/shard_map/all_to_all | solution.py:148
  (8 other events, 24.2 us)
Sparse Core Ops, SparseCore 0:
  28.2 48.8 all-gather.8
  80.4 51.4 all-gather.6
  134.7 52.8 all-gather.4
where the time goes:
time: 339 us; the launch traced here: 338 us
  waiting for transfers between devices  172 us (51%)
  other arithmetic  62.9 us (19%)
  starting transfers between devices  48.5 us (14%)
  blocking collectives  24.2 us (7%)
  between operations  14.2 us (4%)
  local copies, waits for them, and re-layouts  11.3 us (3%)
  matrix products  4.27 us (1%)
    all_gather x1, waiting for transfers between devices, per_device(): lax.all_gather(flux_y, ('comp', 'trc'), axis=0, tiled=True)  51.7 us
    all_gather x1, waiting for transfers between devices, per_device(): lax.all_gather(flux_x, ('comp', 'trc'), axis=0, tiled=True)  51.4 us
    all_gather x1, waiting for transfers between devices, per_device(): lax.all_gather(kappa, ('comp', 'trc'), axis=0, tiled=True)  36.2 us
    ppermute x5, starting transfers between devices, with_halo(): lax.ppermute(lax.slice_in_dim(block, 0, width, axis=dim), axis, backward)  28.6 us
    sub x4, other arithmetic, advance(): return inner + across_x + across_y + below - above  28.1 us
    all_to_all x1, waiting for transfers between devices, per_device(): lax.all_to_all(field, ('comp', 'trc'), split_axis=1, concat_axis=0, tiled...  26.6 us
    all_gather x1, blocking collectives, entering(): everything = lax.all_gather(shard, axis)  24.2 us
    ppermute x5, starting transfers between devices, with_halo(): lax.ppermute(lax.slice_in_dim(block, block.shape[dim] - width, None, axis...  10.9 us
  transfers between devices with their start and end apart: 14, of which 6 were waited for; matrix products, arithmetic and copies ran while one was open for 5% of the time, Pallas kernels for 0%

commit v1 on v0

v1 whole, which is shorter than its diff:
```python
import functools

import jax
import jax.numpy as jnp
from jax import lax
from jax.experimental import pallas as pl
from jax.experimental.pallas import tpu as pltpu
from jax.sharding import PartitionSpec as P

SUBSTEPS = 4
TIME_STEP = 0.25
VISCOSITY = 0.05
COURANT = 0.2
HALF_LIGHT = 0.3

HALO = 4
SHIFTS = (0, 1, 3, 2)

ANY = pl.BlockSpec(memory_space=pl.ANY)
SMEM = pl.BlockSpec(memory_space=pltpu.SMEM)
VMEM = pl.BlockSpec(memory_space=pltpu.VMEM)


def roll(x, shift, axis):
    return pltpu.roll(x, shift % x.shape[axis], axis)


def ocean_kernel(last, levels_ref, u_ref, v_ref, k_ref, h_ref, m_ref, lo_ref, hi_ref, east_ref, north_ref, flux_ref):
    depth, width, rows = u_ref.shape

    def circular(inner, index):
        return jnp.concatenate([inner, hi_ref[index], lo_ref[index]], 0)

    span = width + 16
    lane = lax.broadcasted_iota(jnp.int32, (span, rows), 1)
    first, final = lane == 0, lane == rows - 1
    east = lambda x: roll(x, -1, 0)
    west = lambda x: roll(x, 1, 0)
    north = lambda x: jnp.where(final, 0.0, roll(x, -1, 1))
    south = lambda x: jnp.where(first, 0.0, roll(x, 1, 1))
    coriolis = 0.5 + 0.5 * lane.astype(jnp.float32) / rows
    h = circular(h_ref[...], 3 * depth)
    wet = circular(m_ref[...].astype(jnp.float32), 3 * depth + 1)
    slope_x = east(h) - h
    slope_y = north(h) - h
    open_x = wet * east(wet)
    open_y = wet * north(wet)
    upper = lax.broadcasted_iota(jnp.int32, (8, rows), 0) < HALO

    def emit(index, level, x):
        flux_ref[index, level, :width, :] = x[:width]
        flux_ref[index, level, width:, :] = jnp.where(upper, x[width : width + 8], x[width + 8 :])

    for level in range(depth):
        u = circular(u_ref[level], level)
        v = circular(v_ref[level], depth + level)
        mixing = circular(k_ref[level], 2 * depth + level)
        lap = east(u) + west(u) + north(u) + south(u) - 4.0 * u
        pair = v + east(v)
        avg = 0.25 * (pair + south(pair))
        east_new = open_x * (u + TIME_STEP * (coriolis * avg - slope_x + VISCOSITY * lap))
        lap = east(v) + west(v) + north(v) + south(v) - 4.0 * v
        pair = u + west(u)
        avg = 0.25 * (pair + north(pair))
        north_new = open_y * (v + TIME_STEP * (-coriolis * avg - slope_y + VISCOSITY * lap))
        speed = jnp.minimum(east_new * east_new + north_new * north_new, 1.0)
        keep = jnp.where(levels_ref[0] + level < last, 1.0, 0.0)
        kappa = wet * mixing * (1.0 + speed) * keep
        east_ref[level] = east_new[:width]
        north_ref[level] = north_new[:width]
        emit(0, level, COURANT * east_new)
        emit(1, level, COURANT * north_new)
        emit(2, level, kappa)


def transport_kernel(levels, place_ref, inner_hbm, halo_hbm, flux_hbm, mine_ref, other_ref, send_ref, sums_ref, flux, a, b, sem):
    width = inner_hbm.shape[1]
    copies = [
        pltpu.make_async_copy(flux_hbm.at[place_ref[i]], flux.at[i], sem.at[i]) for i in range(6)
    ]
    copies.append(pltpu.make_async_copy(inner_hbm, a.at[:, :width, :], sem.at[6]))
    copies.append(pltpu.make_async_copy(halo_hbm, a.at[:, width:, :], sem.at[7]))
    for copy in copies:
        copy.start()
    for copy in copies:
        copy.wait()
    total = a.shape[0]

    def down(src, level):
        block, sub = level // HALO, level % HALO
        return flux[block, 2, sub] * (src[level + 1] - src[level])

    for step in range(SUBSTEPS):
        src, dst = (a, b) if step % 2 == 0 else (b, a)
        start, stop = step + 1, total - 1 - step

        def body(level, above, src=src, dst=dst):
            block, sub = level // HALO, level % HALO
            c = src[level]
            fx = flux[block, 0, sub]
            fy = flux[block, 1, sub]
            flow_x = fx * jnp.where(fx > 0.0, c, roll(c, -1, 0))
            flow_y = fy * jnp.where(fy > 0.0, c, roll(c, -1, 1))
            below = flux[block, 2, sub] * (src[level + 1] - c)
            dst[level] = (
                c
                + (roll(flow_x, 1, 0) - flow_x)
                + (roll(flow_y, 1, 1) - flow_y)
                + (below - above)
            )
            return below

        lax.fori_loop(start, stop, body, down(src, start - 1))
    result = b if SUBSTEPS % 2 else a
    own, opposite = place_ref[6], place_ref[7]

    def block_of(index):
        return result[pl.ds(HALO + index * HALO, HALO), :width, :]

    mine_ref[...] = block_of(own)
    other_ref[...] = block_of(own ^ 1)
    send_ref[:HALO] = block_of(opposite)
    send_ref[HALO:] = block_of(opposite ^ 1)
    for index in range(4):
        m = block_of(index)
        sums_ref[index] = jnp.sum((0.5 + m * m) / levels, 0)


def reaction_kernel(levels, order_ref, react_ref, sun_ref, start_ref, *refs):
    mine = refs[0:4]
    across = refs[4:8]
    core_ref, out_ref, heat_ref, depth, field = refs[8:]
    rows = out_ref.shape[2]
    count = out_ref.shape[0]

    @pl.when(pl.program_id(0) == 0)
    def _():
        depth[...] = jnp.sum(start_ref[...], 0)

    for slot in range(4):
        field[order_ref[slot]] = mine[slot][0]
        field[order_ref[4 + slot]] = across[slot][0]
        field[order_ref[8 + slot]] = core_ref[slot, 0]
        field[order_ref[12 + slot]] = core_ref[4 + slot, 0]

    def chunk(index, carry):
        row = pl.ds(pl.multiple_of(index * 8, 8), 8)
        m = [field[j, row, :] for j in range(count)]
        tau = (0.5 + m[0] * m[0]) / levels
        above = depth[row, :]
        light_top = sun_ref[row, :] * jnp.exp(-above)
        heat_ref[0, row, :] = levels * light_top * (1.0 - jnp.exp(-tau))
        depth[row, :] = above + tau
        light_mid = light_top * jnp.exp(-0.5 * tau)
        limit = light_mid / (light_mid + HALF_LIGHT)
        for i in range(count):
            growth = react_ref[i, 0] * m[0]
            for j in range(1, count):
                growth = growth + react_ref[i, j] * m[j]
            out_ref[i, 0, row, :] = m[i] + limit * growth
        return carry

    lax.fori_loop(0, rows // 8, chunk, 0)


def per_device(tracers, eastward, northward, surface_height, sea_mask, mixing, sunlight, reaction):
    f32 = jnp.float32
    depth, width, rows = eastward.shape
    comps, trcs = lax.axis_size("comp"), lax.axis_size("trc")
    tiles = lax.axis_size("horiz")
    levels = depth * comps * trcs
    group = depth * trcs
    c, t = lax.axis_index("comp"), lax.axis_index("trc")
    forward = [(i, i + 1) for i in range(tiles - 1)]
    backward = [(i + 1, i) for i in range(tiles - 1)]
    flip_x = [(i, i ^ 2) for i in range(trcs)]
    flip_core = [(i, i ^ 1) for i in range(trcs)]

    def ring(shift):
        return [(i, (i + shift) % comps) for i in range(comps)]

    field = tracers[0]
    padded = jnp.pad(field, ((HALO, HALO), (0, 0), (0, 0)))

    def segment(array, shift):
        return lax.dynamic_slice_in_dim(array, group * ((c + shift) % comps), group + 2 * HALO, 0)

    inner = {0: segment(padded, 0)}
    for shift in (1, 3):
        inner[shift] = lax.ppermute(segment(padded, shift), "comp", ring(shift))

    edge = jnp.concatenate(
        [eastward, northward, mixing, surface_height[None], sea_mask.astype(f32)[None]], 0
    )
    low = lax.ppermute(edge[:, width - 8 :], "horiz", forward)
    high = lax.ppermute(edge[:, :8], "horiz", backward)
    side_low = lax.ppermute(field[:, width - HALO :], "horiz", forward)
    side_high = lax.ppermute(field[:, :HALO], "horiz", backward)

    first_level = ((c * trcs + t) * depth).astype(jnp.int32)[None]
    span = width + 2 * HALO
    east_out, north_out, flux = pl.pallas_call(
        functools.partial(ocean_kernel, levels - 1),
        out_shape=(
            jax.ShapeDtypeStruct((depth, width, rows), f32),
            jax.ShapeDtypeStruct((depth, width, rows), f32),
            jax.ShapeDtypeStruct((3, depth, span, rows), f32),
        ),
        in_specs=[SMEM] + [VMEM] * 7,
        out_specs=(VMEM,) * 3,
        name="ocean",
        cost_estimate=pl.CostEstimate(flops=8_000_000, bytes_accessed=1_700_000, transcendentals=0),
    )(first_level, eastward, northward, mixing, surface_height, sea_mask, low, high)

    both = ("comp", "trc")
    flux_x = lax.ppermute(flux, "trc", flip_x)
    ups = range(comps - 1)
    near = lax.ppermute(
        flux, both, [(4 * i + 3, 4 * i + 6) for i in ups] + [(4 * i + 4, 4 * i + 1) for i in ups]
    )
    far = lax.ppermute(
        flux, both, [(4 * i + 3, 4 * i + 4) for i in ups] + [(4 * i + 4, 4 * i + 3) for i in ups]
    )
    rim = near + far
    held = jnp.stack([flux, flux_x, rim])
    theirs = lax.ppermute(held, "trc", flip_core)
    flux_all = jnp.concatenate([held, theirs], 0)
    core = t % 2
    block = jnp.arange(4)
    between = (block ^ t).astype(jnp.int32)
    inside = jnp.where(between % 2 == 1, 3, 0) + between // 2
    place = jnp.concatenate(
        [
            jnp.where(core == 0, 2, 5)[None],
            inside,
            jnp.where(core == 0, 5, 2)[None],
            t[None],
            (t ^ 2)[None],
        ]
    ).astype(jnp.int32)

    side = jnp.pad(
        jnp.concatenate([side_high, side_low], 1), ((HALO, HALO), (0, 0), (0, 0))
    )
    sides = {0: segment(side, 0)}
    for shift in (1, 3):
        sides[shift] = lax.ppermute(segment(side, shift), "comp", ring(shift))
    inner[2] = lax.ppermute(segment(padded, 2), "comp", ring(2))
    sides[2] = lax.ppermute(segment(side, 2), "comp", ring(2))

    piece = jax.ShapeDtypeStruct((depth, width, rows), f32)
    transport = pl.pallas_call(
        functools.partial(transport_kernel, levels),
        out_shape=(piece, piece, jax.ShapeDtypeStruct((2 * depth, width, rows), f32), piece),
        in_specs=[SMEM, ANY, ANY, ANY],
        out_specs=(VMEM,) * 4,
        scratch_shapes=[
            pltpu.VMEM((6, 3, depth, span, rows), f32),
            pltpu.VMEM((group + 2 * HALO, span, rows), f32),
            pltpu.VMEM((group + 2 * HALO, span, rows), f32),
            pltpu.SemaphoreType.DMA((8,)),
        ],
        name="transport",
        cost_estimate=pl.CostEstimate(flops=20_000_000, bytes_accessed=5_000_000, transcendentals=0),
    )
    mine, other, across, sums = [], [], [], []
    for shift in SHIFTS:
        m, o, s, total = transport(place, inner[shift], sides[shift], flux_all)
        mine.append(m)
        other.append(o)
        across.append(lax.ppermute(s, "trc", flip_x))
        sums.append(total)
    cross = jnp.stack(other + [a[depth:] for a in across])
    cross = lax.ppermute(cross, "trc", flip_core)

    first = jnp.where(c == 0, sums[0], jnp.where(c == 1, sums[1], jnp.where(c == 3, sums[2], sums[3])))
    first = jnp.where(t == 0, first, 0.0)
    running = [jnp.zeros_like(first[0])]
    for index in range(trcs):
        running.append(running[-1] + first[index])
    whole = running.pop()
    parts = []
    for target in range(comps):
        for index in range(trcs):
            parts.append(jnp.where(c < target, whole, jnp.where(c == target, running[index], 0.0)))
    starts = lax.all_to_all(jnp.stack(parts), both, 0, 0, tiled=True)

    home = [4 * ((c - shift) % comps) for shift in SHIFTS]
    order = jnp.stack([h + (t ^ k) for k in (0, 2, 1, 3) for h in home]).astype(jnp.int32)
    count = reaction.shape[0]
    level_block = pl.BlockSpec((1, width, rows), lambda l: (l, 0, 0))
    tracers_out, heating = pl.pallas_call(
        functools.partial(reaction_kernel, levels),
        grid=(depth,),
        out_shape=(jax.ShapeDtypeStruct((count, depth, width, rows), f32), piece),
        in_specs=[SMEM, SMEM, VMEM, VMEM]
        + [level_block] * 8
        + [pl.BlockSpec((8, 1, width, rows), lambda l: (0, l, 0, 0))],
        out_specs=(pl.BlockSpec((count, 1, width, rows), lambda l: (0, l, 0, 0)), level_block),
        scratch_shapes=[pltpu.VMEM((width, rows), f32), pltpu.VMEM((count, width, rows), f32)],
        name="reaction",
        cost_estimate=pl.CostEstimate(flops=20_000_000, bytes_accessed=5_000_000, transcendentals=100_000),
    )(order, reaction, sunlight, starts, *mine, *across, cross)
    return (east_out, north_out, tracers_out, heating)


def solution(mesh):
    return jax.shard_map(
        per_device,
        mesh=mesh,
        in_specs=(
            P(("comp", "trc"), None, "horiz", None),
            P(("comp", "trc"), "horiz", None),
            P(("comp", "trc"), "horiz", None),
            P("horiz", None),
            P("horiz", None),
            P(("comp", "trc"), "horiz", None),
            P("horiz", None),
            P(),
        ),
        out_specs=(
            P(("comp", "trc"), "horiz", None),
            P(("comp", "trc"), "horiz", None),
            P(None, ("comp", "trc"), "horiz", None),
            P(("comp", "trc"), "horiz", None),
        ),
        check_vma=False,
    )
```

time: 339 us -> 221 us (0.65)
  waiting for transfers between devices: 172 us -> 58.8 us
  Pallas kernels: 0 us -> 71.4 us
  other arithmetic: 62.9 us -> 17.2 us
  blocking collectives: 24.2 us -> 0 us
  between operations: 14.2 us -> 1.03 us
  local copies, waits for them, and re-layouts: 11.3 us -> 18.2 us
  matrix products: 4.27 us -> 0 us
  starting transfers between devices: 48.5 us -> 52.5 us
    all_gather x3 -> x0, waiting for transfers between devices: 139 us -> none  [the longest x1 51.7 us: per_device(): lax.all_gather(flux_y, ('comp', 'trc'), axis=0, tiled=True)]
    pallas_call x0 -> x6, Pallas kernels: none -> 71.4 us  [the longest x4 62.8 us: per_device(): m, o, s, total = transport(place, inner[shift], sides[shift], flux_all)]
    ppermute x10 -> x19, waiting for transfers between devices: 5.22 us -> 49.8 us  [the longest x1 29.8 us: per_device(): sides[2] = lax.ppermute(segment(side, 2), 'comp', ring(2))]
    sub x5 -> x0, other arithmetic: 28.1 us -> none  [the longest x4 28.1 us: advance(): return inner + across_x + across_y + below - above]
    all_gather x1 -> x0, blocking collectives: 24.2 us -> none  [entering(): everything = lax.all_gather(shard, axis)]
    add x8 -> x1, other arithmetic: 19.8 us -> 0.01 us  [per_device(): inside = jnp.where(between % 2 == 1, 3, 0) + between // 2]
    all_to_all x1, waiting for transfers between devices: 26.6 us -> 9.02 us  [per_device(): starts = lax.all_to_all(jnp.stack(parts), both, 0, 0, tiled=True)]
    unnamed x1 -> x15, other arithmetic: 0.01 us -> 9.14 us
  transfers between devices with their start and end apart: 14 -> 20, of which waited for: 6 -> 5; matrix products, arithmetic and copies ran while one was open for 5% -> 11% of each run, Pallas kernels for 0% -> 29%
where the time goes in v1:
time: 221 us; the launch traced here: 219 us
  Pallas kernels  71.4 us (32%)
  waiting for transfers between devices  58.8 us (27%)
  starting transfers between devices  52.5 us (24%)
  local copies, waits for them, and re-layouts  18.2 us (8%)
  other arithmetic  17.2 us (8%)
    pallas_call x4, Pallas kernels, per_device(): m, o, s, total = transport(place, inner[shift], sides[shift], flux_all)  62.8 us
    ppermute x1, waiting for transfers between devices, per_device(): sides[2] = lax.ppermute(segment(side, 2), 'comp', ring(2))  29.8 us
    unnamed x55, local copies, waits for them, and re-layouts  12.6 us
    unnamed x15, other arithmetic  9.14 us
    ppermute x1, waiting for transfers between devices, per_device(): lax.ppermute(flux, both, [(4 * i + 3, 4 * i + 4) for i in ups] + [(4 * i...  9.06 us
    all_to_all x1, waiting for transfers between devices, per_device(): starts = lax.all_to_all(jnp.stack(parts), both, 0, 0, tiled=True)  9.02 us
    all_to_all x1, starting transfers between devices, per_device(): starts = lax.all_to_all(jnp.stack(parts), both, 0, 0, tiled=True)  8.1 us
    ppermute x1, starting transfers between devices, per_device(): high = lax.ppermute(edge[:, :8], 'horiz', backward)  7.75 us
  transfers between devices with their start and end apart: 20, of which 5 were waited for; matrix products, arithmetic and copies ran while one was open for 11% of the time, Pallas kernels for 29%

profile of v1, /device:TPU:7, one launch (start us, length us, event | category | flops | bytes accessed | tf_op | source)
XLA Modules:
  0.0 219.1 jit_solution(2495052788984498541)
XLA Ops:
  4.9 7.8 %collective-permute-start.1 = (f32[14,8,256]{2,1,0:T(8,128)S(1)}, f32[14,8,256]{2,1,0:T(8,128)S(1)}, u32[]{:S(2)}, u32[]{:S(2)}) collective-permute-start(f32[14,8,256]{2,1,0:T(8,128)S(1)} %get-tuple-element.60), channel_id=1, source_target_pairs={{4,0},{8,4},{12,8},{16,12},{20,16},{24,20},{28,24},{32,28},{36,32}... | collective-permute-start | bytes 344072 | tf_op jit(solution)/shard_map/ppermute | solution.py:196
  12.7 1.9 collective-permute-start
  14.6 5.7 %collective-permute-done.lo_ref = f32[14,8,256]{2,1,0:T(8,128)S(1)} collective-permute-done((f32[14,8,256]{2,1,0:T(8,128)S(1)}, f32[14,8,256]{2,1,0:T(8,128)S(1)}, u32[]{:S(2)}, u32[]{:S(2)}) %collective-permute-start) | collective-permute-done | bytes 114720 | tf_op jit(solution)/shard_map/ppermute | solution.py:195
  21.0 2.5 %ocean.1 = (f32[4,32,256]{2,1,0:T(8,128)}, f32[4,32,256]{2,1,0:T(8,128)}, f32[3,4,40,256]{3,2,1,0:T(8,128)}) custom-call(s32[1]{0:T(128)} %bitcast.levels_ref, f32[4,32,256]{2,1,0:T(8,128)} %u_ref.1, f32[4,32,256]{2,1,0:T(8,128)} %v_ref.1, f32[4,32,256]{2,1,0:T(8,128)} %k_ref.1, f32[32,256]{1,0:T(8,128)} %h_ref.1, s32[32,256]{1,0:T(8,128)} %m_ref.1, ...), custom_call_target="tpu_custom_call" | custom-call | flops 8000000 | bytes 1700000 | tf_op jit(solution)/shard_map/ocean/pallas_call | solution.py:202
  23.5 5.9 %collective-permute-start.6 = (f32[3,4,40,256]{3,2,1,0:T(8,128)}, f32[3,4,40,256]{3,2,1,0:T(8,128)S(1)}, u32[]{:S(2)}, u32[]{:S(2)}) collective-permute-start(f32[3,4,40,256]{3,2,1,0:T(8,128)} %get-tuple-element.27), channel_id=1, source_target_pairs={{3,64},{67,128},{131,192},{64,3},{128,67},{192,131},{7,68},{71,132... | collective-permute-start | bytes 1474568 | tf_op jit(solution)/shard_map/ppermute | solution.py:221
  30.8 9.1 %collective-permute-done.6 = f32[3,4,40,256]{3,2,1,0:T(8,128)S(1)} collective-permute-done((f32[3,4,40,256]{3,2,1,0:T(8,128)}, f32[3,4,40,256]{3,2,1,0:T(8,128)S(1)}, u32[]{:S(2)}, u32[]{:S(2)}) %collective-permute-start.6) | collective-permute-done | bytes 491552 | tf_op jit(solution)/shard_map/ppermute | solution.py:221
  39.9 5.2 %collective-permute-done.4 = f32[3,4,40,256]{3,2,1,0:T(8,128)S(1)} collective-permute-done((f32[3,4,40,256]{3,2,1,0:T(8,128)}, f32[3,4,40,256]{3,2,1,0:T(8,128)S(1)}, u32[]{:S(2)}, u32[]{:S(2)}) %collective-permute-start.4) | collective-permute-done | bytes 491552 | tf_op jit(solution)/shard_map/ppermute | solution.py:216
  45.1 2.3 %pad_maximum_fusion.1 = f32[3,3,4,40,256]{4,3,2,1,0:T(8,128)} fusion(f32[1,3,4,40,256]{4,3,2,1,0:T(8,128)S(1)} %add_bitcast_fusion, f32[1,3,4,40,256]{4,3,2,1,0:T(8,128)S(1)} %bitcast.58, f32[1,3,4,40,256]{4,3,2,1,0:T(8,128)} %bitcast.56), kind=kLoop, calls=%fused_computation.5 | loop fusion | flops 737280 | bytes 2949120 | tf_op jit(solution)/shard_map/stack | solution.py:225
  50.2 3.4 %collective-permute-start.3 = (f32[64,4,256]{2,1,0:T(4,128)}, f32[64,4,256]{2,1,0:T(4,128)}, u32[]{:S(2)}, u32[]{:S(2)}) collective-permute-start(f32[64,4,256]{2,1,0:T(4,128)} %get-tuple-element.55), channel_id=1, source_target_pairs={{0,4},{4,8},{8,12},{12,16},{16,20},{20,24},{24,28},{28,32},{32,36}... | collective-permute-start | bytes 786440 | tf_op jit(solution)/shard_map/ppermute | solution.py:197
  55.5 4.4 %collective-permute-start.12 = (f32[24,32,256]{2,1,0:T(8,128)}, f32[24,32,256]{2,1,0:T(8,128)}, u32[]{:S(2)}, u32[]{:S(2)}) collective-permute-start(f32[24,32,256]{2,1,0:T(8,128)} %get-tuple-element.50), channel_id=1, source_target_pairs={{0,128},{64,192},{128,0},{192,64},{1,129},{65,193},{129,1},{193,65... | collective-permute-start | bytes 2359304 | tf_op jit(solution)/shard_map/ppermute | solution.py:248
  59.8 2.7 %collective-permute-start.10 = (f32[24,32,256]{2,1,0:T(8,128)}, f32[24,32,256]{2,1,0:T(8,128)S(1)}, u32[]{:S(2)}, u32[]{:S(2)}) collective-permute-start(f32[24,32,256]{2,1,0:T(8,128)} %get-tuple-element.52), channel_id=1, source_target_pairs={{0,192},{64,0},{128,64},{192,128},{1,193},{65,1},{129,65},{193,129... | collective-permute-start | bytes 2359304 | tf_op jit(solution)/shard_map/ppermute | solution.py:190
  64.5 4.3 %collective-permute-start.13 = (f32[24,8,256]{2,1,0:T(8,128)S(1)}, f32[24,8,256]{2,1,0:T(8,128)S(1)}, u32[]{:S(2)}, u32[]{:S(2)}) collective-permute-start(f32[24,8,256]{2,1,0:T(8,128)S(1)} %get-tuple-element.56), channel_id=1, source_target_pairs={{0,128},{64,192},{128,0},{192,64},{1,129},{65,193},{129,1},{193,65... | collective-permute-start | bytes 589832 | tf_op jit(solution)/shard_map/ppermute | solution.py:249
  68.7 29.8 %collective-permute-done.13.halo_hbm = f32[24,8,256]{2,1,0:T(8,128)S(1)} collective-permute-done((f32[24,8,256]{2,1,0:T(8,128)S(1)}, f32[24,8,256]{2,1,0:T(8,128)S(1)}, u32[]{:S(2)}, u32[]{:S(2)}) %collective-permute-start.13) | collective-permute-done | bytes 196640 | tf_op jit(solution)/shard_map/ppermute | solution.py:249
  101.0 3.2 %pad_maximum_fusion.flux_hbm = f32[6,3,4,40,256]{4,3,2,1,0:T(8,128)} fusion(f32[3,3,4,40,256]{4,3,2,1,0:T(8,128)} %collective-permute-done.7, f32[1,3,4,40,256]{4,3,2,1,0:T(8,128)S(1)} %add_bitcast_fusion, f32[1,3,4,40,256]{4,3,2,1,0:T(8,128)S(1)} %bitcast.59, f32[1,3,4,40,256]{4,3,2,1,0:T(8,128)S(1)} %bitcast.57), kind=kLoop, calls=%fused_computation | loop fusion | flops 2211840 | bytes 5898240 | tf_op jit(solution)/shard_map/concatenate | solution.py:227
  104.2 15.7 %transport.4 = (f32[4,32,256]{2,1,0:T(8,128)}, f32[4,32,256]{2,1,0:T(8,128)}, f32[8,32,256]{2,1,0:T(8,128)}, f32[4,32,256]{2,1,0:T(8,128)}) custom-call(s32[8]{0:T(128)} %concatenate.14.place_ref, f32[24,32,256]{2,1,0:T(8,128)} %get-tuple-element.53.inner_hbm, f32[24,8,256]{2,1,0:T(8,128)} %get-tuple-element.59.halo_hbm, ...), custom_call_target="tpu_custom_call" | custom-call | flops 20000000 | bytes 5000000 | tf_op jit(solution)/shard_map/transport/pallas_call | solution.py:268
  119.9 2.2 %collective-permute-start.14 = (f32[8,32,256]{2,1,0:T(8,128)}, f32[8,32,256]{2,1,0:T(8,128)S(1)}, u32[]{:S(2)}, u32[]{:S(2)}) collective-permute-start(f32[8,32,256]{2,1,0:T(8,128)} %get-tuple-element.36), channel_id=1, source_target_pairs={{0,2},{1,3},{2,0},{3,1},{4,6},{5,7},{6,4},{7,5},{8,10},{9,11},{10,... | collective-permute-start | bytes 786440 | tf_op jit(solution)/shard_map/ppermute | solution.py:271
  122.2 15.7 %transport.7 = (f32[4,32,256]{2,1,0:T(8,128)}, f32[4,32,256]{2,1,0:T(8,128)}, f32[8,32,256]{2,1,0:T(8,128)}, f32[4,32,256]{2,1,0:T(8,128)}) custom-call(s32[8]{0:T(128)} %concatenate.14.place_ref, f32[24,32,256]{2,1,0:T(8,128)} %collective-permute-done.12.inner_hbm, f32[24,8,256]{2,1,0:T(8,128)} %copy-done.12, f32[6,3,4,40,256]{4,3,2,1,0:T(8,128)} %pad_maximum_fusion.flux_hbm), custom_call_target="tpu_custom_call" | custom-call | flops 20000000 | bytes 5000000 | tf_op jit(solution)/shard_map/transport/pallas_call | solution.py:268
  139.6 15.7 %transport.5 = (f32[4,32,256]{2,1,0:T(8,128)}, f32[4,32,256]{2,1,0:T(8,128)}, f32[8,32,256]{2,1,0:T(8,128)}, f32[4,32,256]{2,1,0:T(8,128)}) custom-call(s32[8]{0:T(128)} %concatenate.14.place_ref, f32[24,32,256]{2,1,0:T(8,128)} %copy-done.5, f32[24,8,256]{2,1,0:T(8,128)} %copy-done.11, f32[6,3,4,40,256]{4,3,2,1,0:T(8,128)} %pad_maximum_fusion.flux_hbm), custom_call_target="tpu_custom_call" | custom-call | flops 20000000 | bytes 5000000 | tf_op jit(solution)/shard_map/transport/pallas_call | solution.py:268
  155.4 2.2 %collective-permute-start.15 = (f32[8,32,256]{2,1,0:T(8,128)}, f32[8,32,256]{2,1,0:T(8,128)S(1)}, u32[]{:S(2)}, u32[]{:S(2)}) collective-permute-start(f32[8,32,256]{2,1,0:T(8,128)} %get-tuple-element.37), channel_id=1, source_target_pairs={{0,2},{1,3},{2,0},{3,1},{4,6},{5,7},{6,4},{7,5},{8,10},{9,11},{10,... | collective-permute-start | bytes 786440 | tf_op jit(solution)/shard_map/ppermute | solution.py:271
  159.2 15.8 %transport.6 = (f32[4,32,256]{2,1,0:T(8,128)}, f32[4,32,256]{2,1,0:T(8,128)}, f32[8,32,256]{2,1,0:T(8,128)}, f32[4,32,256]{2,1,0:T(8,128)}) custom-call(s32[8]{0:T(128)} %concatenate.14.place_ref, f32[24,32,256]{2,1,0:T(8,128)} %copy-done.4, f32[24,8,256]{2,1,0:T(8,128)} %copy-done.10, f32[6,3,4,40,256]{4,3,2,1,0:T(8,128)} %pad_maximum_fusion.flux_hbm), custom_call_target="tpu_custom_call" | custom-call | flops 20000000 | bytes 5000000 | tf_op jit(solution)/shard_map/transport/pallas_call | solution.py:268
  189.4 2.8 %collective-permute-start.18 = (f32[8,4,32,256]{3,2,1,0:T(8,128)}, f32[8,4,32,256]{3,2,1,0:T(8,128)S(1)}, u32[]{:S(2)}, u32[]{:S(2)}) collective-permute-start(f32[8,4,32,256]{3,2,1,0:T(8,128)} %fusion.1), channel_id=1, source_target_pairs={{0,1},{1,0},{2,3},{3,2},{4,5},{5,4},{6,7},{7,6},{8,9},{9,8},{10,11... | collective-permute-start | bytes 3145736 | tf_op jit(solution)/shard_map/ppermute | solution.py:274
  194.1 8.1 %all-to-all-start = ((f32[16,32,256]{2,1,0:T(8,128)}), f32[16,32,256]{2,1,0:T(8,128)S(1)}, u32[]{:S(2)}, u32[]{:S(2)}) async-start(f32[16,32,256]{2,1,0:T(8,128)} %constant_dynamic-update-slice_fusion.5), calls=%async_computation | async-start | bytes 1048576 | tf_op jit(solution)/shard_map/all_to_all | solution.py:286
  202.9 9.0 %all-to-all-done.start_ref = f32[16,32,256]{2,1,0:T(8,128)S(1)} async-done(((f32[16,32,256]{2,1,0:T(8,128)}), f32[16,32,256]{2,1,0:T(8,128)S(1)}, u32[]{:S(2)}, u32[]{:S(2)}) %all-to-all-start) | async-done | bytes 524320 | tf_op jit(solution)/shard_map/all_to_all | solution.py:286
  213.0 6.1 %reaction.1 = (f32[16,4,32,256]{3,2,1,0:T(8,128)}, f32[4,32,256]{2,1,0:T(8,128)}) custom-call(s32[16]{0:T(128)} %stack.125.order_ref, f32[16,16]{1,0:T(8,128)} %react_ref.1, f32[32,256]{1,0:T(8,128)} %sun_ref.1, f32[16,32,256]{2,1,0:T(8,128)} %copy-done.1, f32[4,32,256]{2,1,0:T(8,128)} %get-tuple-element.32.refs_0_, ...), custom_call_target="tpu_custom_call" | custom-call | flops 20000000 | bytes 5000000 | tf_op jit(solution)/shard_map/reaction/pallas_call | solution.py:292
  (107 shorter events, 36.8 us)
Async XLA Ops:
  4.9 9.7 %collective-permute-start.1 = (f32[14,8,256]{2,1,0:T(8,128)S(1)}, f32[14,8,256]{2,1,0:T(8,128)S(1)}, u32[]{:S(2)}, u32[]{:S(2)}) collective-permute-start(f32[14,8,256]{2,1,0:T(8,128)S(1)} %get-tuple-element.60), channel_id=1, source_target_pairs={{4,0},{8,4},{12,8},{16,12},{20,16},{24,20},{28,24},{32,28},{36,32}... | collective-permute-start | bytes 344072 | tf_op jit(solution)/shard_map/ppermute | solution.py:196
  12.7 7.6 %collective-permute-start = (f32[14,8,256]{2,1,0:T(8,128)S(1)}, f32[14,8,256]{2,1,0:T(8,128)S(1)}, u32[]{:S(2)}, u32[]{:S(2)}) collective-permute-start(f32[14,8,256]{2,1,0:T(8,128)S(1)} %get-tuple-element.61), channel_id=1, source_target_pairs={{0,4},{4,8},{8,12},{12,16},{16,20},{20,24},{24,28},{28,32},{32,36}... | collective-permute-start | bytes 344072 | tf_op jit(solution)/shard_map/ppermute | solution.py:195
  23.5 16.4 %collective-permute-start.6 = (f32[3,4,40,256]{3,2,1,0:T(8,128)}, f32[3,4,40,256]{3,2,1,0:T(8,128)S(1)}, u32[]{:S(2)}, u32[]{:S(2)}) collective-permute-start(f32[3,4,40,256]{3,2,1,0:T(8,128)} %get-tuple-element.27), channel_id=1, source_target_pairs={{3,64},{67,128},{131,192},{64,3},{128,67},{192,131},{7,68},{71,132... | collective-permute-start | bytes 1474568 | tf_op jit(solution)/shard_map/ppermute | solution.py:221
  29.3 10.5 %collective-permute-start.5 = (f32[3,4,40,256]{3,2,1,0:T(8,128)}, f32[3,4,40,256]{3,2,1,0:T(8,128)S(1)}, u32[]{:S(2)}, u32[]{:S(2)}) collective-permute-start(f32[3,4,40,256]{3,2,1,0:T(8,128)} %get-tuple-element.27), channel_id=1, source_target_pairs={{3,66},{67,130},{131,194},{64,1},{128,65},{192,129},{7,70},{71,134... | collective-permute-start | bytes 1474568 | tf_op jit(solution)/shard_map/ppermute | solution.py:218
  30.7 14.4 %collective-permute-start.4 = (f32[3,4,40,256]{3,2,1,0:T(8,128)}, f32[3,4,40,256]{3,2,1,0:T(8,128)S(1)}, u32[]{:S(2)}, u32[]{:S(2)}) collective-permute-start(f32[3,4,40,256]{3,2,1,0:T(8,128)} %get-tuple-element.27), channel_id=1, source_target_pairs={{0,2},{1,3},{2,0},{3,1},{4,6},{5,7},{6,4},{7,5},{8,10},{9,11},{10,... | collective-permute-start | bytes 1474568 | tf_op jit(solution)/shard_map/ppermute | solution.py:216
  47.4 52.9 %collective-permute-start.7 = (f32[3,3,4,40,256]{4,3,2,1,0:T(8,128)}, f32[3,3,4,40,256]{4,3,2,1,0:T(8,128)}, u32[]{:S(2)}, u32[]{:S(2)}) collective-permute-start(f32[3,3,4,40,256]{4,3,2,1,0:T(8,128)} %pad_maximum_fusion.1), channel_id=1, source_target_pairs={{0,1},{1,0},{2,3},{3,2},{4,5},{5,4},{6,7},{7,6},{8,9},{9,8},{10,11... | collective-permute-start | bytes 4423688 | tf_op jit(solution)/shard_map/ppermute | solution.py:226
  48.3 11.5 %collective-permute-start.2 = (f32[64,4,256]{2,1,0:T(4,128)}, f32[64,4,256]{2,1,0:T(4,128)S(1)}, u32[]{:S(2)}, u32[]{:S(2)}) collective-permute-start(f32[64,4,256]{2,1,0:T(4,128)} %get-tuple-element.54), channel_id=1, source_target_pairs={{4,0},{8,4},{12,8},{16,12},{20,16},{24,20},{28,24},{32,28},{36,32}... | collective-permute-start | bytes 786440 | tf_op jit(solution)/shard_map/ppermute | solution.py:198
  50.2 12.3 %collective-permute-start.3 = (f32[64,4,256]{2,1,0:T(4,128)}, f32[64,4,256]{2,1,0:T(4,128)}, u32[]{:S(2)}, u32[]{:S(2)}) collective-permute-start(f32[64,4,256]{2,1,0:T(4,128)} %get-tuple-element.55), channel_id=1, source_target_pairs={{0,4},{4,8},{8,12},{12,16},{16,20},{20,24},{24,28},{28,32},{32,36}... | collective-permute-start | bytes 786440 | tf_op jit(solution)/shard_map/ppermute | solution.py:197
  55.4 45.5 %copy-start.2 = (f32[3,4,40,256]{3,2,1,0:T(8,128)S(1)}, f32[3,4,40,256]{3,2,1,0:T(8,128)}, u32[]{:S(2)}) copy-start(f32[3,4,40,256]{3,2,1,0:T(8,128)} %get-tuple-element.27) | copy-start | bytes 1474564
  55.5 64.5 %collective-permute-start.12 = (f32[24,32,256]{2,1,0:T(8,128)}, f32[24,32,256]{2,1,0:T(8,128)}, u32[]{:S(2)}, u32[]{:S(2)}) collective-permute-start(f32[24,32,256]{2,1,0:T(8,128)} %get-tuple-element.50), channel_id=1, source_target_pairs={{0,128},{64,192},{128,0},{192,64},{1,129},{65,193},{129,1},{193,65... | collective-permute-start | bytes 2359304 | tf_op jit(solution)/shard_map/ppermute | solution.py:248
  59.8 78.9 %collective-permute-start.8 = (f32[24,32,256]{2,1,0:T(8,128)}, f32[24,32,256]{2,1,0:T(8,128)S(1)}, u32[]{:S(2)}, u32[]{:S(2)}) collective-permute-start(f32[24,32,256]{2,1,0:T(8,128)} %get-tuple-element.51), channel_id=1, source_target_pairs={{0,64},{64,128},{128,192},{192,0},{1,65},{65,129},{129,193},{193,1... | collective-permute-start | bytes 2359304 | tf_op jit(solution)/shard_map/ppermute | solution.py:190
  59.8 97.8 %collective-permute-start.10 = (f32[24,32,256]{2,1,0:T(8,128)}, f32[24,32,256]{2,1,0:T(8,128)S(1)}, u32[]{:S(2)}, u32[]{:S(2)}) collective-permute-start(f32[24,32,256]{2,1,0:T(8,128)} %get-tuple-element.52), channel_id=1, source_target_pairs={{0,192},{64,0},{128,64},{192,128},{1,193},{65,1},{129,65},{193,129... | collective-permute-start | bytes 2359304 | tf_op jit(solution)/shard_map/ppermute | solution.py:190
  64.5 34.0 %collective-permute-start.13 = (f32[24,8,256]{2,1,0:T(8,128)S(1)}, f32[24,8,256]{2,1,0:T(8,128)S(1)}, u32[]{:S(2)}, u32[]{:S(2)}) collective-permute-start(f32[24,8,256]{2,1,0:T(8,128)S(1)} %get-tuple-element.56), channel_id=1, source_target_pairs={{0,128},{64,192},{128,0},{192,64},{1,129},{65,193},{129,1},{193,65... | collective-permute-start | bytes 589832 | tf_op jit(solution)/shard_map/ppermute | solution.py:249
  98.5 59.2 %collective-permute-start.11 = (f32[24,8,256]{2,1,0:T(8,128)}, f32[24,8,256]{2,1,0:T(8,128)S(1)}, u32[]{:S(2)}, u32[]{:S(2)}) collective-permute-start(f32[24,8,256]{2,1,0:T(8,128)} %get-tuple-element.57), channel_id=1, source_target_pairs={{0,192},{64,0},{128,64},{192,128},{1,193},{65,1},{129,65},{193,129... | collective-permute-start | bytes 589832 | tf_op jit(solution)/shard_map/ppermute | solution.py:247
  100.2 37.6 %collective-permute-start.9 = (f32[24,8,256]{2,1,0:T(8,128)}, f32[24,8,256]{2,1,0:T(8,128)S(1)}, u32[]{:S(2)}, u32[]{:S(2)}) collective-permute-start(f32[24,8,256]{2,1,0:T(8,128)} %get-tuple-element.58), channel_id=1, source_target_pairs={{0,64},{64,128},{128,192},{192,0},{1,65},{65,129},{129,193},{193,1... | collective-permute-start | bytes 589832 | tf_op jit(solution)/shard_map/ppermute | solution.py:247
  119.9 66.7 %collective-permute-start.14 = (f32[8,32,256]{2,1,0:T(8,128)}, f32[8,32,256]{2,1,0:T(8,128)S(1)}, u32[]{:S(2)}, u32[]{:S(2)}) collective-permute-start(f32[8,32,256]{2,1,0:T(8,128)} %get-tuple-element.36), channel_id=1, source_target_pairs={{0,2},{1,3},{2,0},{3,1},{4,6},{5,7},{6,4},{7,5},{8,10},{9,11},{10,... | collective-permute-start | bytes 786440 | tf_op jit(solution)/shard_map/ppermute | solution.py:271
  137.9 50.9 %collective-permute-start.17 = (f32[8,32,256]{2,1,0:T(8,128)}, f32[8,32,256]{2,1,0:T(8,128)S(1)}, u32[]{:S(2)}, u32[]{:S(2)}) collective-permute-start(f32[8,32,256]{2,1,0:T(8,128)} %get-tuple-element.39), channel_id=1, source_target_pairs={{0,2},{1,3},{2,0},{3,1},{4,6},{5,7},{6,4},{7,5},{8,10},{9,11},{10,... | collective-permute-start | bytes 786440 | tf_op jit(solution)/shard_map/ppermute | solution.py:271
  155.4 27.3 %copy-start.16 = (f32[4,32,256]{2,1,0:T(8,128)S(1)}, f32[4,32,256]{2,1,0:T(8,128)}, u32[]{:S(2)}) copy-start(f32[4,32,256]{2,1,0:T(8,128)} %get-tuple-element.40) | copy-start | bytes 393220
  155.4 28.0 %copy-start.18 = (f32[4,32,256]{2,1,0:T(8,128)S(1)}, f32[4,32,256]{2,1,0:T(8,128)}, u32[]{:S(2)}) copy-start(f32[4,32,256]{2,1,0:T(8,128)} %get-tuple-element.41) | copy-start | bytes 393220
  155.4 29.3 %copy-start.17 = (f32[4,32,256]{2,1,0:T(8,128)S(1)}, f32[4,32,256]{2,1,0:T(8,128)}, u32[]{:S(2)}) copy-start(f32[4,32,256]{2,1,0:T(8,128)} %get-tuple-element.43) | copy-start | bytes 393220
  155.4 31.9 %collective-permute-start.15 = (f32[8,32,256]{2,1,0:T(8,128)}, f32[8,32,256]{2,1,0:T(8,128)S(1)}, u32[]{:S(2)}, u32[]{:S(2)}) collective-permute-start(f32[8,32,256]{2,1,0:T(8,128)} %get-tuple-element.37), channel_id=1, source_target_pairs={{0,2},{1,3},{2,0},{3,1},{4,6},{5,7},{6,4},{7,5},{8,10},{9,11},{10,... | collective-permute-start | bytes 786440 | tf_op jit(solution)/shard_map/ppermute | solution.py:271
  175.0 13.0 %collective-permute-start.16 = (f32[8,32,256]{2,1,0:T(8,128)}, f32[8,32,256]{2,1,0:T(8,128)S(1)}, u32[]{:S(2)}, u32[]{:S(2)}) collective-permute-start(f32[8,32,256]{2,1,0:T(8,128)} %get-tuple-element.38), channel_id=1, source_target_pairs={{0,2},{1,3},{2,0},{3,1},{4,6},{5,7},{6,4},{7,5},{8,10},{9,11},{10,... | collective-permute-start | bytes 786440 | tf_op jit(solution)/shard_map/ppermute | solution.py:271
  189.4 22.4 %collective-permute-start.18 = (f32[8,4,32,256]{3,2,1,0:T(8,128)}, f32[8,4,32,256]{3,2,1,0:T(8,128)S(1)}, u32[]{:S(2)}, u32[]{:S(2)}) collective-permute-start(f32[8,4,32,256]{3,2,1,0:T(8,128)} %fusion.1), channel_id=1, source_target_pairs={{0,1},{1,0},{2,3},{3,2},{4,5},{5,4},{6,7},{7,6},{8,9},{9,8},{10,11... | collective-permute-start | bytes 3145736 | tf_op jit(solution)/shard_map/ppermute | solution.py:274
  194.1 17.8 %all-to-all-start = ((f32[16,32,256]{2,1,0:T(8,128)}), f32[16,32,256]{2,1,0:T(8,128)S(1)}, u32[]{:S(2)}, u32[]{:S(2)}) async-start(f32[16,32,256]{2,1,0:T(8,128)} %constant_dynamic-update-slice_fusion.5), calls=%async_computation | async-start | bytes 1048576 | tf_op jit(solution)/shard_map/all_to_all | solution.py:286
  (18 other events, 205.0 us)

commit v2 on v1

v2 whole, which is shorter than its diff:
```python
import functools

import jax
import jax.numpy as jnp
from jax import lax
from jax.experimental import pallas as pl
from jax.experimental.pallas import tpu as pltpu
from jax.sharding import PartitionSpec as P


SUBSTEPS = 4
TIME_STEP = 0.25
VISCOSITY = 0.05
COURANT = 0.2
HALF_LIGHT = 0.3

SHIFTS = (0, 1, 3, 2)
HALO = 4


SMEM = pl.BlockSpec(memory_space=pltpu.SMEM)
VMEM = pl.BlockSpec(memory_space=pltpu.VMEM)
ANY = pl.BlockSpec(memory_space=pl.ANY)


def local(*shape):
    return pltpu.VMEM(shape, jnp.float32)


def array(*shape):
    return jax.ShapeDtypeStruct(shape, jnp.float32)


def call(kernel, cost, **kwargs):
    return pl.pallas_call(
        kernel,
        compiler_params=pltpu.CompilerParams(vmem_limit_bytes=12 << 20),
        cost_estimate=pl.CostEstimate(flops=cost * 1_000_000, bytes_accessed=cost * 1_000_000, transcendentals=0),
        **kwargs,
    )


def in_hbm(*arrays):
    return [pltpu.with_memory_space_constraint(x, pltpu.HBM) for x in arrays]


def in_vmem(*arrays):
    return [pltpu.with_memory_space_constraint(x, pltpu.VMEM) for x in arrays]


def position():
    return lax.axis_index("comp").astype(jnp.int32), lax.axis_index("trc").astype(jnp.int32)


def roll(x, shift, axis):
    return pltpu.roll(x, shift % x.shape[axis], axis)


def pack_kernel(field, u, v, k, h, m, *refs):
    segments, (low, high), (west, east, mask, sem) = refs[:4], refs[4:6], refs[6:]
    levels, width = field.shape[0], field.shape[1]
    depth = u.shape[0]
    comps = len(segments)
    group = levels // comps
    copies = []

    def copy(src, dst):
        copies.append(pltpu.make_async_copy(src, dst, sem.at[len(copies)]))
        copies[-1].start()

    place, _ = position()
    for index, source in enumerate((u, v, k)):
        rows = pl.ds(index * depth, depth)
        copy(source.at[:, width - 8 :, :], low.at[rows])
        copy(source.at[:, :8, :], high.at[rows])
    copy(h.at[width - 8 :, :], low.at[3 * depth])
    copy(h.at[:8, :], high.at[3 * depth])
    copy(m.at[width - 8 :, :], mask.at[0])
    copy(m.at[:8, :], mask.at[1])
    copy(field.at[:, :8, :], west)
    copy(field.at[:, width - 8 :, :], east)
    for shift, segment in enumerate(segments):
        target = lax.rem(place + shift, comps)
        start = group * target
        copy(field.at[pl.ds(start, group)], segment.at[pl.ds(HALO, group)])
        copy(field.at[pl.ds(jnp.maximum(start - HALO, 0), HALO)], segment.at[pl.ds(0, HALO)])
        after = jnp.minimum(start + group, levels - HALO)
        copy(field.at[pl.ds(after, HALO)], segment.at[pl.ds(HALO + group, HALO)])
    for item in copies[:12]:
        item.wait()
    low[3 * depth + 1] = mask[0].astype(jnp.float32)
    high[3 * depth + 1] = mask[1].astype(jnp.float32)
    half = levels // 2
    first = 3 * depth + 2
    upper = lax.broadcasted_iota(jnp.int32, west.shape[1:], 0) < HALO

    def body(level, carry):
        a, b = west[level], west[level + half]
        high[first + level] = jnp.where(upper, a, roll(b, HALO, 0))
        a, b = east[level], east[level + half]
        low[first + level] = jnp.where(upper, roll(b, HALO, 0), a)
        return carry

    lax.fori_loop(0, half, body, 0, unroll=4)
    for item in copies[12:]:
        item.wait()


def side_kernel(first, low, high, inner, *refs):
    segments, side = refs[:4], refs[4]
    width = inner.shape[1]
    levels = side.shape[0]
    half = levels // 2
    comps = len(segments)
    group = levels // comps
    c, _ = position()
    upper = lax.broadcasted_iota(jnp.int32, side.shape[1:], 0) < HALO

    def body(level, carry):
        a, b = high[first + level], low[first + level]
        side[level] = jnp.where(upper, a, b)
        side[level + half] = roll(jnp.where(upper, b, a), HALO, 0)
        return carry

    lax.fori_loop(0, half, body, 0, unroll=4)
    for shift, segment in enumerate(segments):
        start = group * lax.rem(c + shift, comps)
        if shift == SHIFTS[-1]:
            segment[:, :width, :] = inner[...]
            segment = segment.at[:, width:, :]
        segment[pl.ds(HALO, group)] = side[pl.ds(start, group)]
        segment[pl.ds(0, HALO)] = side[pl.ds(jnp.maximum(start - HALO, 0), HALO)]
        segment[pl.ds(HALO + group, HALO)] = side[pl.ds(jnp.minimum(start + group, levels - HALO), HALO)]


def ocean_kernel(last, u_ref, v_ref, k_ref, h_ref, m_ref, lo_ref, hi_ref, east_ref, north_ref, flux_ref):
    depth, width, rows = u_ref.shape

    def circular(inner, index):
        return jnp.concatenate([inner, hi_ref[index], lo_ref[index]], 0)

    c, t = position()
    first_level = (c * lax.axis_size("trc") + t) * depth
    span = width + 16
    lane = lax.broadcasted_iota(jnp.int32, (span, rows), 1)
    first, final = lane == 0, lane == rows - 1
    east = lambda x: roll(x, -1, 0)
    west = lambda x: roll(x, 1, 0)
    north = lambda x: jnp.where(final, 0.0, roll(x, -1, 1))
    south = lambda x: jnp.where(first, 0.0, roll(x, 1, 1))
    coriolis = 0.5 + 0.5 * lane.astype(jnp.float32) / rows
    h = circular(h_ref[...], 3 * depth)
    wet = circular(m_ref[...].astype(jnp.float32), 3 * depth + 1)
    slope_x = east(h) - h
    slope_y = north(h) - h
    open_x = wet * east(wet)
    open_y = wet * north(wet)
    upper = lax.broadcasted_iota(jnp.int32, (8, rows), 0) < HALO

    def emit(index, level, x):
        flux_ref[index, level, :width, :] = x[:width]
        flux_ref[index, level, width:, :] = jnp.where(upper, x[width : width + 8], x[width + 8 :])

    for level in range(depth):
        u = circular(u_ref[level], level)
        v = circular(v_ref[level], depth + level)
        mixing = circular(k_ref[level], 2 * depth + level)
        lap = east(u) + west(u) + north(u) + south(u) - 4.0 * u
        pair = v + east(v)
        avg = 0.25 * (pair + south(pair))
        east_new = open_x * (u + TIME_STEP * (coriolis * avg - slope_x + VISCOSITY * lap))
        lap = east(v) + west(v) + north(v) + south(v) - 4.0 * v
        pair = u + west(u)
        avg = 0.25 * (pair + north(pair))
        north_new = open_y * (v + TIME_STEP * (-coriolis * avg - slope_y + VISCOSITY * lap))
        speed = jnp.minimum(east_new * east_new + north_new * north_new, 1.0)
        keep = jnp.where(first_level + level < last, 1.0, 0.0)
        kappa = wet * mixing * (1.0 + speed) * keep
        east_ref[level] = east_new[:width]
        north_ref[level] = north_new[:width]
        emit(0, level, COURANT * east_new)
        emit(1, level, COURANT * north_new)
        emit(2, level, kappa)


def weight_kernel(own, core, pair, core_pair, weight_ref):
    depth = own.shape[1]
    _, t = position()
    odd = t & 1

    def fill(position, piece):
        for level in range(depth):
            fx, fy, kappa = piece(0, level), piece(1, level), piece(2, level)
            fw, fs = roll(fx, 1, 0), roll(fy, 1, 1)
            index = position * depth + level
            weight_ref[0, index] = (
                1.0
                - (jnp.maximum(fx, 0.0) - jnp.minimum(fw, 0.0))
                - (jnp.maximum(fy, 0.0) - jnp.minimum(fs, 0.0))
            )
            weight_ref[1, index] = -jnp.minimum(fx, 0.0)
            weight_ref[2, index] = jnp.maximum(fw, 0.0)
            weight_ref[3, index] = -jnp.minimum(fy, 0.0)
            weight_ref[4, index] = jnp.maximum(fs, 0.0)
            weight_ref[5, index] = kappa

    fill(1 + t, lambda i, l: own[i, l])
    fill(1 + (t ^ 1), lambda i, l: core[i, l])
    fill(1 + (t ^ 2), lambda i, l: pair[0, i, l])
    fill(1 + (t ^ 3), lambda i, l: core_pair[0, i, l])
    fill(5 * odd, lambda i, l: pair[1, i, l])
    fill(5 * (1 - odd), lambda i, l: core_pair[1, i, l])


def pair_kernel(across, near, far, out):
    out[0] = across[...]
    out[1] = near[...] + far[...]


def transport_kernel(levels, weight, *refs):
    parts, (mine_ref, other_ref, send_ref, sums_ref, a, b) = refs[:-6], refs[-6:]
    total, _, _ = parts[0].shape
    width = mine_ref.shape[1]
    _, t = position()
    if len(parts) == 2:
        inner, side = parts

        def fill(level, carry):
            a[level, :width, :] = inner[level]
            a[level, width:, :] = side[level]
            return carry

        lax.fori_loop(0, total, fill, 0, unroll=4)
        whole = a
    else:
        whole = parts[0]

    def edge(src, level):
        return weight[5, level] * (src[level + 1] - src[level])

    def update(src, level, above):
        c = src[level]
        below = weight[5, level] * (src[level + 1] - c)
        value = (
            weight[0, level] * c
            + weight[1, level] * roll(c, -1, 0)
            + weight[2, level] * roll(c, 1, 0)
            + weight[3, level] * roll(c, -1, 1)
            + weight[4, level] * roll(c, 1, 1)
            + (below - above)
        )
        return value, below

    for step in range(SUBSTEPS - 1):
        src, dst = (b, a) if step % 2 else (whole if step == 0 else a, b)
        start, stop = step + 1, total - 1 - step

        def body(index, above, src=src, dst=dst, start=start):
            for sub in range(4):
                level = start + 4 * index + sub
                dst[level], above = update(src, level, above)
            return above

        trips = (stop - start) // 4
        above = lax.fori_loop(0, trips, body, edge(src, start - 1))
        for level in range(start + 4 * trips, stop):
            dst[level], above = update(src, level, above)
    src = b if SUBSTEPS % 2 == 0 else a
    outs = (mine_ref, other_ref, send_ref, send_ref)
    for place, out in enumerate(outs):
        block = t ^ place
        first = HALO + HALO * block
        above = edge(src, first - 1)
        tau = None
        for sub in range(HALO):
            value, above = update(src, first + sub, above)
            m = value[:width]
            out[sub + (HALO if place == 3 else 0)] = m
            part = (0.5 + m * m) / levels
            tau = part if tau is None else tau + part
        sums_ref[block] = tau


def tau_kernel(holder, sums, *refs):
    out = refs[-1]
    c, t = position()
    total = sums[0]
    for index in range(1, sums.shape[0]):
        total = total + sums[index]
    for above in refs[:-1]:
        total = total + above[...]
    out[...] = jnp.where((t == 0) & (c == holder), total, 0.0)


def start_kernel(*refs):
    bases, sums, near, far = refs[:3], refs[3:7], refs[7], refs[8]
    c, _ = position()
    turn = functools.reduce(lambda x, i: jnp.where(c == SHIFTS[i], i, x), range(4), 0)
    running = bases[0][...] + bases[1][...] + bases[2][...]
    for index in range(4):
        out = near if index < 2 else far
        out[index % 2] = running
        for i in range(4):
            running = running + jnp.where(turn == i, sums[i][index], 0.0)


def gather_kernel(near, far, *refs):
    others, across, out = refs[:4], refs[4:8], refs[8]
    depth = others[0].shape[0]
    _, t = position()
    for slot in range(4):
        out[slot * depth : (slot + 1) * depth] = others[slot][...]
        out[(4 + slot) * depth : (5 + slot) * depth] = across[slot][depth:]
    out[8 * depth] = jnp.where(t == 0, near[1], far[1])


def reaction_kernel(levels, react_ref, sun_ref, near_ref, far_ref, *refs):
    mine = refs[0:4]
    across = refs[4:8]
    core_ref, out_ref, heat_ref, depth, field = refs[8:]
    rows = out_ref.shape[2]
    count = out_ref.shape[0]
    level = pl.program_id(0)
    deep = pl.num_programs(0)
    c, t = position()

    @pl.when(level == 0)
    def _():
        inner = jnp.where(t == 0, near_ref[0], far_ref[0])
        depth[...] = jnp.where(t % 2 == 0, inner, core_ref[8 * deep])

    trcs = lax.axis_size("trc")
    comps = lax.axis_size("comp")
    for slot, shift in enumerate(SHIFTS):
        first = trcs * lax.rem(c + comps - shift, comps)
        field[first + t] = mine[slot][level]
        field[first + (t ^ 2)] = across[slot][level]
        field[first + (t ^ 1)] = core_ref[slot * deep + level]
        field[first + (t ^ 3)] = core_ref[(4 + slot) * deep + level]

    def chunk(index, carry):
        row = pl.ds(pl.multiple_of(index * 8, 8), 8)
        m = [field[j, row, :] for j in range(count)]
        tau = (0.5 + m[0] * m[0]) / levels
        above = depth[row, :]
        light_top = sun_ref[row, :] * jnp.exp(-above)
        heat_ref[0, row, :] = levels * light_top * (1.0 - jnp.exp(-tau))
        depth[row, :] = above + tau
        light_mid = light_top * jnp.exp(-0.5 * tau)
        limit = light_mid / (light_mid + HALF_LIGHT)
        for i in range(count):
            growth = react_ref[i, 0] * m[0]
            for j in range(1, count):
                growth = growth + react_ref[i, j] * m[j]
            out_ref[i, 0, row, :] = m[i] + limit * growth
        return carry

    lax.fori_loop(0, rows // 8, chunk, 0)


def per_device(tracers, eastward, northward, surface_height, sea_mask, mixing, sunlight, reaction):
    i32 = jnp.int32
    depth, width, rows = eastward.shape
    comps, trcs = lax.axis_size("comp"), lax.axis_size("trc")
    tiles = lax.axis_size("horiz")
    levels = depth * comps * trcs
    group = depth * trcs
    tall = group + 2 * HALO
    span = width + 2 * HALO
    forward = [(i, i + 1) for i in range(tiles - 1)]
    backward = [(i + 1, i) for i in range(tiles - 1)]
    flip_x = [(i, i ^ 2) for i in range(trcs)]
    flip_core = [(i, i ^ 1) for i in range(trcs)]
    both = ("comp", "trc")
    edges = 3 * depth + 2
    payload = edges + levels // 2

    def ring(shift):
        return [(i, (i + shift) % comps) for i in range(comps)]

    packed = call(
        pack_kernel,
        4,
        out_shape=(local(tall, width, rows),) * comps + (local(payload, 8, rows),) * 2,
        in_specs=[ANY] * 6,
        out_specs=(VMEM,) * (comps + 2),
        scratch_shapes=[
            local(levels, 8, rows),
            local(levels, 8, rows),
            pltpu.VMEM((2, 8, rows), i32),
            pltpu.SemaphoreType.DMA((12 + 3 * comps,)),
        ],
    )(*in_hbm(tracers[0], eastward, northward, mixing, surface_height, sea_mask))
    inner = list(packed[:comps])
    low = lax.ppermute(packed[comps], "horiz", forward)
    high = lax.ppermute(packed[comps + 1], "horiz", backward)
    inner[1] = lax.ppermute(inner[1], "comp", ring(1))
    inner[3] = lax.ppermute(inner[3], "comp", ring(3))

    east_out, north_out, flux = call(
        functools.partial(ocean_kernel, levels - 1),
        4,
        out_shape=(array(depth, width, rows),) * 2 + (local(3, depth, span, rows),),
        in_specs=[VMEM] * 7,
        out_specs=(VMEM,) * 3,
    )(eastward, northward, mixing, surface_height, sea_mask, low, high)

    ups = range(comps - 1)
    last, nxt = trcs - 1, trcs
    near = lax.ppermute(
        flux,
        both,
        [(trcs * i + last, trcs * i + nxt + 2) for i in ups] + [(trcs * i + nxt, trcs * i + 1) for i in ups],
    )
    far = lax.ppermute(
        flux,
        both,
        [(trcs * i + last, trcs * i + nxt) for i in ups] + [(trcs * i + nxt, trcs * i + last) for i in ups],
    )
    across_flux = lax.ppermute(flux, "trc", flip_x)
    core_flux = lax.ppermute(flux, "trc", flip_core)

    sides = list(
        call(
            functools.partial(side_kernel, edges),
            1,
            out_shape=tuple(local(tall, span if i == SHIFTS[-1] else 8, rows) for i in range(comps)),
            in_specs=[VMEM] * 3,
            out_specs=(VMEM,) * comps,
            scratch_shapes=[local(levels, 8, rows)],
        )(*in_vmem(low, high, inner[2]))
    )
    for shift in (1, 3, 2):
        sides[shift] = lax.ppermute(sides[shift], "comp", ring(shift))
    pair = call(
        pair_kernel,
        1,
        out_shape=local(2, 3, depth, span, rows),
        in_specs=[VMEM] * 3,
        out_specs=VMEM,
    )(across_flux, near, far)
    core_pair = lax.ppermute(pair, "trc", flip_core)
    weight = call(
        weight_kernel, 3, out_shape=local(6, tall, span, rows), in_specs=[VMEM] * 4, out_specs=VMEM
    )(*in_vmem(flux, core_flux, pair, core_pair))
    piece = local(depth, width, rows)
    mine, other, across, sums = [], [], [], []
    bases = []

    def pass_tau(turn, holder):
        value = call(
            functools.partial(tau_kernel, holder),
            1,
            out_shape=local(width, rows),
            in_specs=[VMEM] * (1 + len(bases[-1:])),
            out_specs=VMEM,
        )(*in_vmem(sums[turn], *bases[-1:]))
        bases.append(lax.ppermute(value, "comp", [(holder, holder + 1)]))

    for turn, shift in enumerate(SHIFTS):
        inputs = [weight] + ([inner[shift]] if turn < 3 else []) + [sides[shift]]
        m, o, s, total = call(
            functools.partial(transport_kernel, levels),
            6,
            out_shape=(piece, piece, local(2 * depth, width, rows), piece),
            in_specs=[VMEM] * len(inputs),
            out_specs=(VMEM,) * 4,
            scratch_shapes=[local(tall, span, rows)] * 2,
        )(*in_vmem(*inputs))
        mine.append(m)
        other.append(o)
        across.append(lax.ppermute(s, "trc", flip_x))
        sums.append(total)
        if shift < comps - 1:
            pass_tau(turn, shift)
    near, far = call(
        start_kernel,
        1,
        out_shape=(local(2, width, rows),) * 2,
        in_specs=[VMEM] * 7,
        out_specs=(VMEM,) * 2,
    )(*in_vmem(*bases, *sums))
    far = lax.ppermute(far, "trc", flip_x)
    cross = call(
        gather_kernel,
        2,
        out_shape=local(8 * depth + 1, width, rows),
        in_specs=[VMEM] * 10,
        out_specs=VMEM,
    )(*in_vmem(near, far, *other, *across))
    cross = lax.ppermute(cross, "trc", flip_core)

    count = reaction.shape[0]
    tracers_out, heating = call(
        functools.partial(reaction_kernel, levels),
        6,
        grid=(depth,),
        out_shape=(array(count, depth, width, rows), array(depth, width, rows)),
        in_specs=[SMEM] + [VMEM] * 12,
        out_specs=(
            pl.BlockSpec((count, 1, width, rows), lambda l: (0, l, 0, 0)),
            pl.BlockSpec((1, width, rows), lambda l: (l, 0, 0)),
        ),
        scratch_shapes=[local(width, rows), local(count, width, rows)],
    )(reaction, *in_vmem(sunlight, near, far, *mine, *across, cross))
    return (east_out, north_out, tracers_out, heating)


def solution(mesh):
    return jax.shard_map(
        per_device,
        mesh=mesh,
        in_specs=(
            P(("comp", "trc"), None, "horiz", None),
            P(("comp", "trc"), "horiz", None),
            P(("comp", "trc"), "horiz", None),
            P("horiz", None),
            P("horiz", None),
            P(("comp", "trc"), "horiz", None),
            P("horiz", None),
            P(),
        ),
        out_specs=(
            P(("comp", "trc"), "horiz", None),
            P(("comp", "trc"), "horiz", None),
            P(None, ("comp", "trc"), "horiz", None),
            P(("comp", "trc"), "horiz", None),
        ),
        check_vma=False,
    )
```

time: 221 us -> 133 us (0.60)
  the two profiles are of different devices: /device:TPU:7 before, /device:TPU:125 now
where the time goes in v2:
time: 133 us
  waiting for transfers between devices  71.3 us (54%)
  starting transfers between devices  38.9 us (29%)
  Pallas kernels  21.5 us (16%)
    ppermute x3, waiting for transfers between devices, per_device(): sides[shift] = lax.ppermute(sides[shift], 'comp', ring(shift))  31.3 us
    pallas_call x4, Pallas kernels, per_device(): call(functools.partial(transport_kernel, levels), 6, out_shape=(piece, pi...  11.7 us
    ppermute x1, waiting for transfers between devices, per_device(): across_flux = lax.ppermute(flux, 'trc', flip_x)  10.9 us
    ppermute x3, waiting for transfers between devices, pass_tau(): bases.append(lax.ppermute(value, 'comp', [(holder, holder + 1)]))  10.6 us
    ppermute x3, starting transfers between devices, per_device(): sides[shift] = lax.ppermute(sides[shift], 'comp', ring(shift))  9.47 us
    ppermute x4, starting transfers between devices, per_device(): across.append(lax.ppermute(s, 'trc', flip_x))  6.38 us
    ppermute x1, starting transfers between devices, per_device(): cross = lax.ppermute(cross, 'trc', flip_core)  5.99 us
    ppermute x1, waiting for transfers between devices, per_device(): low = lax.ppermute(packed[comps], 'horiz', forward)  5.5 us
  transfers between devices with their start and end apart: 21, of which 8 were waited for; matrix products, arithmetic and copies ran while one was open for 0% of the time, Pallas kernels for 10%

profile of v2, /device:TPU:125, one launch (start us, length us, event | category | flops | bytes accessed | tf_op | source)
XLA Modules:
  0.0 132.6 jit_solution(6323224714668208809)
XLA Ops:
  0.7 2.6 %shard_map.111 = (f32[24,32,256]{2,1,0:T(8,128)S(1)}, f32[24,32,256]{2,1,0:T(8,128)S(1)}, f32[24,32,256]{2,1,0:T(8,128)S(1)}, f32[24,32,256]{2,1,0:T(8,128)S(1)}...) custom-call(f32[64,32,256]{2,1,0:T(8,128)} %bitcast.1, f32[4,32,256]{2,1,0:T(8,128)} %u_ref.1, ...), custom_call_target="tpu_custom_call" | custom-call | flops 4000000 | bytes 4000000 | tf_op jit(solution)/shard_map/pallas_call | solution.py:381
  3.3 4.8 %collective-permute-start = (f32[46,8,256]{2,1,0:T(8,128)S(1)}, f32[46,8,256]{2,1,0:T(8,128)S(1)}, u32[]{:S(2)}, u32[]{:S(2)}) collective-permute-start(f32[46,8,256]{2,1,0:T(8,128)S(1)} %get-tuple-element.37), channel_id=1, source_target_pairs={{0,4},{4,8},{8,12},{12,16},{16,20},{20,24},{24,28},{28,32},{32,36}... | collective-permute-start | bytes 1130504 | tf_op jit(solution)/shard_map/ppermute | solution.py:395
  8.0 1.9 %collective-permute-start.1 = (f32[46,8,256]{2,1,0:T(8,128)S(1)}, f32[46,8,256]{2,1,0:T(8,128)S(1)}, u32[]{:S(2)}, u32[]{:S(2)}) collective-permute-start(f32[46,8,256]{2,1,0:T(8,128)S(1)} %get-tuple-element.38), channel_id=1, source_target_pairs={{4,0},{8,4},{12,8},{16,12},{20,16},{24,20},{28,24},{32,28},{36,32}... | collective-permute-start | bytes 1130504 | tf_op jit(solution)/shard_map/ppermute | solution.py:396
  10.0 5.5 %collective-permute-done.lo_ref.low = f32[46,8,256]{2,1,0:T(8,128)S(1)} collective-permute-done((f32[46,8,256]{2,1,0:T(8,128)S(1)}, f32[46,8,256]{2,1,0:T(8,128)S(1)}, u32[]{:S(2)}, u32[]{:S(2)}) %collective-permute-start) | collective-permute-done | bytes 376864 | tf_op jit(solution)/shard_map/ppermute | solution.py:395
  15.5 5.0 %collective-permute-done.1.hi_ref.high = f32[46,8,256]{2,1,0:T(8,128)S(1)} collective-permute-done((f32[46,8,256]{2,1,0:T(8,128)S(1)}, f32[46,8,256]{2,1,0:T(8,128)S(1)}, u32[]{:S(2)}, u32[]{:S(2)}) %collective-permute-start.1) | collective-permute-done | bytes 376864 | tf_op jit(solution)/shard_map/ppermute | solution.py:396
  23.3 10.9 %collective-permute-done.3.across = f32[3,4,40,256]{3,2,1,0:T(8,128)S(1)} collective-permute-done((f32[3,4,40,256]{3,2,1,0:T(8,128)S(1)}, f32[3,4,40,256]{3,2,1,0:T(8,128)S(1)}, u32[]{:S(2)}, u32[]{:S(2)}) %collective-permute-start.3) | collective-permute-done | bytes 491552 | tf_op jit(solution)/shard_map/ppermute | solution.py:420
  34.3 2.8 %collective-permute-start.6 = (f32[2,3,4,40,256]{4,3,2,1,0:T(8,128)S(1)}, f32[2,3,4,40,256]{4,3,2,1,0:T(8,128)S(1)}, u32[]{:S(2)}, u32[]{:S(2)}) collective-permute-start(f32[2,3,4,40,256]{4,3,2,1,0:T(8,128)S(1)} %shard_map.113.pair), channel_id=1, source_target_pairs={{0,1},{1,0},{2,3},{3,2},{4,5},{5,4},{6,7},{7,6},{8,9},{9,8},{10,11... | collective-permute-start | bytes 2949128 | tf_op jit(solution)/shard_map/ppermute | solution.py:442
  37.2 6.7 %collective-permute-start.11 = (f32[24,40,256]{2,1,0:T(8,128)S(1)}, f32[24,40,256]{2,1,0:T(8,128)S(1)}, u32[]{:S(2)}, u32[]{:S(2)}) collective-permute-start(f32[24,40,256]{2,1,0:T(8,128)S(1)} %get-tuple-element.49), channel_id=1, source_target_pairs={{0,128},{64,192},{128,0},{192,64},{1,129},{65,193},{129,1},{193,65... | collective-permute-start | bytes 2949128 | tf_op jit(solution)/shard_map/ppermute | solution.py:434
  43.9 1.6 %collective-permute-start.8 = (f32[24,32,256]{2,1,0:T(8,128)S(1)}, f32[24,32,256]{2,1,0:T(8,128)S(1)}, u32[]{:S(2)}, u32[]{:S(2)}) collective-permute-start(f32[24,32,256]{2,1,0:T(8,128)S(1)} %get-tuple-element.46), channel_id=1, source_target_pairs={{0,64},{64,128},{128,192},{192,0},{1,65},{65,129},{129,193},{193,1... | collective-permute-start | bytes 2359304 | tf_op jit(solution)/shard_map/ppermute | solution.py:397
  46.6 1.5 %collective-permute-done.2.core = f32[3,4,40,256]{3,2,1,0:T(8,128)S(1)} collective-permute-done((f32[3,4,40,256]{3,2,1,0:T(8,128)S(1)}, f32[3,4,40,256]{3,2,1,0:T(8,128)S(1)}, u32[]{:S(2)}, u32[]{:S(2)}) %collective-permute-start.2) | collective-permute-done | bytes 491552 | tf_op jit(solution)/shard_map/ppermute | solution.py:421
  48.1 2.8 %collective-permute-start.9 = (f32[24,8,256]{2,1,0:T(8,128)S(1)}, f32[24,8,256]{2,1,0:T(8,128)S(1)}, u32[]{:S(2)}, u32[]{:S(2)}) collective-permute-start(f32[24,8,256]{2,1,0:T(8,128)S(1)} %get-tuple-element.47), channel_id=1, source_target_pairs={{0,64},{64,128},{128,192},{192,0},{1,65},{65,129},{129,193},{193,1... | collective-permute-start | bytes 589832 | tf_op jit(solution)/shard_map/ppermute | solution.py:434
  51.7 2.9 %shard_map.116 = (f32[4,32,256]{2,1,0:T(8,128)S(1)}, f32[4,32,256]{2,1,0:T(8,128)S(1)}, f32[8,32,256]{2,1,0:T(8,128)S(1)}, f32[4,32,256]{2,1,0:T(8,128)S(1)}) custom-call(f32[6,24,40,256]{3,2,1,0:T(8,128)S(1)} %shard_map.114.weight, f32[24,32,256]{2,1,0:T(8,128)S(1)} %get-tuple-element.42.refs_0_, f32[24,8,256]{2,1,0:T(8,128)S(1)} %get-tuple-element.44.refs_1_), custom_call_target="tpu_custom_call" | custom-call | flops 6000000 | bytes 6000000 | tf_op jit(solution)/shard_map/pallas_call | solution.py:462
  54.6 31.3 %collective-permute-done.9.refs_1_ = f32[24,8,256]{2,1,0:T(8,128)S(1)} collective-permute-done((f32[24,8,256]{2,1,0:T(8,128)S(1)}, f32[24,8,256]{2,1,0:T(8,128)S(1)}, u32[]{:S(2)}, u32[]{:S(2)}) %collective-permute-start.9) | collective-permute-done | bytes 196640 | tf_op jit(solution)/shard_map/ppermute | solution.py:434
  86.3 2.9 %shard_map.118 = (f32[4,32,256]{2,1,0:T(8,128)S(1)}, f32[4,32,256]{2,1,0:T(8,128)S(1)}, f32[8,32,256]{2,1,0:T(8,128)S(1)}, f32[4,32,256]{2,1,0:T(8,128)S(1)}) custom-call(f32[6,24,40,256]{3,2,1,0:T(8,128)S(1)} %shard_map.114.weight, f32[24,32,256]{2,1,0:T(8,128)S(1)} %collective-permute-done.8.refs_0_, f32[24,8,256]{2,1,0:T(8,128)S(1)} %collective-permute-done.9.refs_1_), custom_call_target="tpu_custom_call" | custom-call | flops 6000000 | bytes 6000000 | tf_op jit(solution)/shard_map/pallas_call | solution.py:462
  89.2 2.6 %collective-permute-start.17 = (f32[8,32,256]{2,1,0:T(8,128)S(1)}, f32[8,32,256]{2,1,0:T(8,128)S(1)}, u32[]{:S(2)}, u32[]{:S(2)}) collective-permute-start(f32[8,32,256]{2,1,0:T(8,128)S(1)} %get-tuple-element.61), channel_id=1, source_target_pairs={{0,2},{1,3},{2,0},{3,1},{4,6},{5,7},{6,4},{7,5},{8,10},{9,11},{10,... | collective-permute-start | bytes 786440 | tf_op jit(solution)/shard_map/ppermute | solution.py:472
  91.9 2.9 %shard_map.122 = (f32[4,32,256]{2,1,0:T(8,128)S(1)}, f32[4,32,256]{2,1,0:T(8,128)S(1)}, f32[8,32,256]{2,1,0:T(8,128)S(1)}, f32[4,32,256]{2,1,0:T(8,128)S(1)}) custom-call(f32[6,24,40,256]{3,2,1,0:T(8,128)S(1)} %shard_map.114.weight, f32[24,32,256]{2,1,0:T(8,128)S(1)} %collective-permute-done.13.refs_0_, f32[24,8,256]{2,1,0:T(8,128)S(1)} %collective-permute-done.14.refs_1_), custom_call_target="tpu_custom_call" | custom-call | flops 6000000 | bytes 6000000 | tf_op jit(solution)/shard_map/pallas_call | solution.py:462
  95.5 2.9 %shard_map.120 = (f32[4,32,256]{2,1,0:T(8,128)S(1)}, f32[4,32,256]{2,1,0:T(8,128)S(1)}, f32[8,32,256]{2,1,0:T(8,128)S(1)}, f32[4,32,256]{2,1,0:T(8,128)S(1)}) custom-call(f32[6,24,40,256]{3,2,1,0:T(8,128)S(1)} %shard_map.114.weight, f32[24,40,256]{2,1,0:T(8,128)S(1)} %collective-permute-done.11.refs_0_), custom_call_target="tpu_custom_call" | custom-call | flops 6000000 | bytes 6000000 | tf_op jit(solution)/shard_map/pallas_call | solution.py:462
  98.4 2.6 %collective-permute-start.19 = (f32[8,32,256]{2,1,0:T(8,128)S(1)}, f32[8,32,256]{2,1,0:T(8,128)S(1)}, u32[]{:S(2)}, u32[]{:S(2)}) collective-permute-start(f32[8,32,256]{2,1,0:T(8,128)S(1)} %get-tuple-element.63), channel_id=1, source_target_pairs={{0,2},{1,3},{2,0},{3,1},{4,6},{5,7},{6,4},{7,5},{8,10},{9,11},{10,... | collective-permute-start | bytes 786440 | tf_op jit(solution)/shard_map/ppermute | solution.py:472
  102.5 1.3 collective-permute-start.12
  103.8 10.6 %collective-permute-done.12.refs_2_ = f32[32,256]{1,0:T(8,128)S(1)} collective-permute-done((f32[32,256]{1,0:T(8,128)S(1)}, f32[32,256]{1,0:T(8,128)S(1)}, u32[]{:S(2)}, u32[]{:S(2)}) %collective-permute-start.12) | collective-permute-done | bytes 32800 | tf_op jit(solution)/shard_map/ppermute | solution.py:458
  115.0 4.1 %collective-permute-done.15.far.far_ref = f32[2,32,256]{2,1,0:T(8,128)S(1)} collective-permute-done((f32[2,32,256]{2,1,0:T(8,128)S(1)}, f32[2,32,256]{2,1,0:T(8,128)S(1)}, u32[]{:S(2)}, u32[]{:S(2)}) %collective-permute-start.15) | collective-permute-done | bytes 65568 | tf_op jit(solution)/shard_map/ppermute | solution.py:483
  119.2 6.0 %collective-permute-start.20 = (f32[33,32,256]{2,1,0:T(8,128)S(1)}, f32[33,32,256]{2,1,0:T(8,128)S(1)}, u32[]{:S(2)}, u32[]{:S(2)}) collective-permute-start(f32[33,32,256]{2,1,0:T(8,128)S(1)} %shard_map.124), channel_id=1, source_target_pairs={{0,1},{1,0},{2,3},{3,2},{4,5},{5,4},{6,7},{7,6},{8,9},{9,8},{10,11... | collective-permute-start | bytes 3244040 | tf_op jit(solution)/shard_map/ppermute | solution.py:491
  125.2 2.3 %collective-permute-done.20.refs_8_ = f32[33,32,256]{2,1,0:T(8,128)S(1)} collective-permute-done((f32[33,32,256]{2,1,0:T(8,128)S(1)}, f32[33,32,256]{2,1,0:T(8,128)S(1)}, u32[]{:S(2)}, u32[]{:S(2)}) %collective-permute-start.20) | collective-permute-done | bytes 1081376 | tf_op jit(solution)/shard_map/ppermute | solution.py:491
  127.6 5.0 %shard_map.125 = (f32[16,4,32,256]{3,2,1,0:T(8,128)}, f32[4,32,256]{2,1,0:T(8,128)}) custom-call(f32[16,16]{1,0:T(8,128)S(1)} %copy-done.6, f32[32,256]{1,0:T(8,128)S(1)} %copy-done.5, f32[2,32,256]{2,1,0:T(8,128)S(1)} %get-tuple-element.54.near.near_ref, f32[2,32,256]{2,1,0:T(8,128)S(1)} %collective-permute-done.15.far.far_ref, ...), custom_call_target="tpu_custom_call" | custom-call | flops 6000000 | bytes 6000000 | tf_op jit(solution)/shard_map/pallas_call | solution.py:494
  (47 shorter events, 8.2 us)
Async XLA Ops:
  0.6 19.9 %copy-start = (f32[4,32,256]{2,1,0:T(8,128)S(1)}, f32[4,32,256]{2,1,0:T(8,128)}, u32[]{:S(2)}) copy-start(f32[4,32,256]{2,1,0:T(8,128)} %u_ref.1) | copy-start | bytes 393220
  3.3 12.2 %collective-permute-start = (f32[46,8,256]{2,1,0:T(8,128)S(1)}, f32[46,8,256]{2,1,0:T(8,128)S(1)}, u32[]{:S(2)}, u32[]{:S(2)}) collective-permute-start(f32[46,8,256]{2,1,0:T(8,128)S(1)} %get-tuple-element.37), channel_id=1, source_target_pairs={{0,4},{4,8},{8,12},{12,16},{16,20},{20,24},{24,28},{28,32},{32,36}... | collective-permute-start | bytes 1130504 | tf_op jit(solution)/shard_map/ppermute | solution.py:395
  8.0 12.5 %collective-permute-start.1 = (f32[46,8,256]{2,1,0:T(8,128)S(1)}, f32[46,8,256]{2,1,0:T(8,128)S(1)}, u32[]{:S(2)}, u32[]{:S(2)}) collective-permute-start(f32[46,8,256]{2,1,0:T(8,128)S(1)} %get-tuple-element.38), channel_id=1, source_target_pairs={{4,0},{8,4},{12,8},{16,12},{20,16},{24,20},{28,24},{32,28},{36,32}... | collective-permute-start | bytes 1130504 | tf_op jit(solution)/shard_map/ppermute | solution.py:396
  21.7 12.5 %collective-permute-start.3 = (f32[3,4,40,256]{3,2,1,0:T(8,128)S(1)}, f32[3,4,40,256]{3,2,1,0:T(8,128)S(1)}, u32[]{:S(2)}, u32[]{:S(2)}) collective-permute-start(f32[3,4,40,256]{3,2,1,0:T(8,128)S(1)} %get-tuple-element.41.own), channel_id=1, source_target_pairs={{0,2},{1,3},{2,0},{3,1},{4,6},{5,7},{6,4},{7,5},{8,10},{9,11},{10,... | collective-permute-start | bytes 1474568 | tf_op jit(solution)/shard_map/ppermute | solution.py:420
  21.9 12.3 %collective-permute-start.4 = (f32[3,4,40,256]{3,2,1,0:T(8,128)S(1)}, f32[3,4,40,256]{3,2,1,0:T(8,128)S(1)}, u32[]{:S(2)}, u32[]{:S(2)}) collective-permute-start(f32[3,4,40,256]{3,2,1,0:T(8,128)S(1)} %get-tuple-element.41.own), channel_id=1, source_target_pairs={{3,66},{67,130},{131,194},{64,1},{128,65},{192,129},{7,70},{71,134... | collective-permute-start | bytes 1474568 | tf_op jit(solution)/shard_map/ppermute | solution.py:410
  22.6 11.6 %collective-permute-start.5 = (f32[3,4,40,256]{3,2,1,0:T(8,128)S(1)}, f32[3,4,40,256]{3,2,1,0:T(8,128)S(1)}, u32[]{:S(2)}, u32[]{:S(2)}) collective-permute-start(f32[3,4,40,256]{3,2,1,0:T(8,128)S(1)} %get-tuple-element.41.own), channel_id=1, source_target_pairs={{3,64},{67,128},{131,192},{64,3},{128,67},{192,131},{7,68},{71,132... | collective-permute-start | bytes 1474568 | tf_op jit(solution)/shard_map/ppermute | solution.py:415
  34.3 16.7 %collective-permute-start.6 = (f32[2,3,4,40,256]{4,3,2,1,0:T(8,128)S(1)}, f32[2,3,4,40,256]{4,3,2,1,0:T(8,128)S(1)}, u32[]{:S(2)}, u32[]{:S(2)}) collective-permute-start(f32[2,3,4,40,256]{4,3,2,1,0:T(8,128)S(1)} %shard_map.113.pair), channel_id=1, source_target_pairs={{0,1},{1,0},{2,3},{3,2},{4,5},{5,4},{6,7},{7,6},{8,9},{9,8},{10,11... | collective-permute-start | bytes 2949128 | tf_op jit(solution)/shard_map/ppermute | solution.py:442
  37.2 58.3 %collective-permute-start.11 = (f32[24,40,256]{2,1,0:T(8,128)S(1)}, f32[24,40,256]{2,1,0:T(8,128)S(1)}, u32[]{:S(2)}, u32[]{:S(2)}) collective-permute-start(f32[24,40,256]{2,1,0:T(8,128)S(1)} %get-tuple-element.49), channel_id=1, source_target_pairs={{0,128},{64,192},{128,0},{192,64},{1,129},{65,193},{129,1},{193,65... | collective-permute-start | bytes 2949128 | tf_op jit(solution)/shard_map/ppermute | solution.py:434
  43.9 42.5 %collective-permute-start.8 = (f32[24,32,256]{2,1,0:T(8,128)S(1)}, f32[24,32,256]{2,1,0:T(8,128)S(1)}, u32[]{:S(2)}, u32[]{:S(2)}) collective-permute-start(f32[24,32,256]{2,1,0:T(8,128)S(1)} %get-tuple-element.46), channel_id=1, source_target_pairs={{0,64},{64,128},{128,192},{192,0},{1,65},{65,129},{129,193},{193,1... | collective-permute-start | bytes 2359304 | tf_op jit(solution)/shard_map/ppermute | solution.py:397
  45.4 46.4 %collective-permute-start.13 = (f32[24,32,256]{2,1,0:T(8,128)S(1)}, f32[24,32,256]{2,1,0:T(8,128)S(1)}, u32[]{:S(2)}, u32[]{:S(2)}) collective-permute-start(f32[24,32,256]{2,1,0:T(8,128)S(1)} %get-tuple-element.51), channel_id=1, source_target_pairs={{0,192},{64,0},{128,64},{192,128},{1,193},{65,1},{129,65},{193,129... | collective-permute-start | bytes 2359304 | tf_op jit(solution)/shard_map/ppermute | solution.py:398
  45.4 2.7 %collective-permute-start.2 = (f32[3,4,40,256]{3,2,1,0:T(8,128)S(1)}, f32[3,4,40,256]{3,2,1,0:T(8,128)S(1)}, u32[]{:S(2)}, u32[]{:S(2)}) collective-permute-start(f32[3,4,40,256]{3,2,1,0:T(8,128)S(1)} %get-tuple-element.41.own), channel_id=1, source_target_pairs={{0,1},{1,0},{2,3},{3,2},{4,5},{5,4},{6,7},{7,6},{8,9},{9,8},{10,11... | collective-permute-start | bytes 1474568 | tf_op jit(solution)/shard_map/ppermute | solution.py:421
  48.1 37.7 %collective-permute-start.9 = (f32[24,8,256]{2,1,0:T(8,128)S(1)}, f32[24,8,256]{2,1,0:T(8,128)S(1)}, u32[]{:S(2)}, u32[]{:S(2)}) collective-permute-start(f32[24,8,256]{2,1,0:T(8,128)S(1)} %get-tuple-element.47), channel_id=1, source_target_pairs={{0,64},{64,128},{128,192},{192,0},{1,65},{65,129},{129,193},{193,1... | collective-permute-start | bytes 589832 | tf_op jit(solution)/shard_map/ppermute | solution.py:434
  50.9 40.9 %collective-permute-start.14 = (f32[24,8,256]{2,1,0:T(8,128)S(1)}, f32[24,8,256]{2,1,0:T(8,128)S(1)}, u32[]{:S(2)}, u32[]{:S(2)}) collective-permute-start(f32[24,8,256]{2,1,0:T(8,128)S(1)} %get-tuple-element.52), channel_id=1, source_target_pairs={{0,192},{64,0},{128,64},{192,128},{1,193},{65,1},{129,65},{193,129... | collective-permute-start | bytes 589832 | tf_op jit(solution)/shard_map/ppermute | solution.py:434
  85.9 33.3 %collective-permute-start.16 = (f32[8,32,256]{2,1,0:T(8,128)S(1)}, f32[8,32,256]{2,1,0:T(8,128)S(1)}, u32[]{:S(2)}, u32[]{:S(2)}) collective-permute-start(f32[8,32,256]{2,1,0:T(8,128)S(1)} %get-tuple-element.60), channel_id=1, source_target_pairs={{0,2},{1,3},{2,0},{3,1},{4,6},{5,7},{6,4},{7,5},{8,10},{9,11},{10,... | collective-permute-start | bytes 786440 | tf_op jit(solution)/shard_map/ppermute | solution.py:472
  89.2 29.9 %collective-permute-start.17 = (f32[8,32,256]{2,1,0:T(8,128)S(1)}, f32[8,32,256]{2,1,0:T(8,128)S(1)}, u32[]{:S(2)}, u32[]{:S(2)}) collective-permute-start(f32[8,32,256]{2,1,0:T(8,128)S(1)} %get-tuple-element.61), channel_id=1, source_target_pairs={{0,2},{1,3},{2,0},{3,1},{4,6},{5,7},{6,4},{7,5},{8,10},{9,11},{10,... | collective-permute-start | bytes 786440 | tf_op jit(solution)/shard_map/ppermute | solution.py:472
  94.8 24.4 %collective-permute-start.18 = (f32[8,32,256]{2,1,0:T(8,128)S(1)}, f32[8,32,256]{2,1,0:T(8,128)S(1)}, u32[]{:S(2)}, u32[]{:S(2)}) collective-permute-start(f32[8,32,256]{2,1,0:T(8,128)S(1)} %get-tuple-element.62), channel_id=1, source_target_pairs={{0,2},{1,3},{2,0},{3,1},{4,6},{5,7},{6,4},{7,5},{8,10},{9,11},{10,... | collective-permute-start | bytes 786440 | tf_op jit(solution)/shard_map/ppermute | solution.py:472
  98.4 29.2 %copy-start.5 = (f32[32,256]{1,0:T(8,128)S(1)}, f32[32,256]{1,0:T(8,128)}, u32[]{:S(2)}) copy-start(f32[32,256]{1,0:T(8,128)} %sun_ref.1) | copy-start | bytes 98308
  98.4 29.2 %copy-start.6 = (f32[16,16]{1,0:T(8,128)S(1)}, f32[16,16]{1,0:T(8,128)}, u32[]{:S(2)}) copy-start(f32[16,16]{1,0:T(8,128)} %react_ref.1) | copy-start | bytes 3076
  98.4 20.7 %collective-permute-start.19 = (f32[8,32,256]{2,1,0:T(8,128)S(1)}, f32[8,32,256]{2,1,0:T(8,128)S(1)}, u32[]{:S(2)}, u32[]{:S(2)}) collective-permute-start(f32[8,32,256]{2,1,0:T(8,128)S(1)} %get-tuple-element.63), channel_id=1, source_target_pairs={{0,2},{1,3},{2,0},{3,1},{4,6},{5,7},{6,4},{7,5},{8,10},{9,11},{10,... | collective-permute-start | bytes 786440 | tf_op jit(solution)/shard_map/ppermute | solution.py:472
  101.0 0.7 collective-permute-start.7
  101.8 0.7 collective-permute-start.10
  102.5 11.9 %collective-permute-start.12 = (f32[32,256]{1,0:T(8,128)S(1)}, f32[32,256]{1,0:T(8,128)S(1)}, u32[]{:S(2)}, u32[]{:S(2)}) collective-permute-start(f32[32,256]{1,0:T(8,128)S(1)} %shard_map.121), channel_id=1, source_target_pairs={{128,192},{129,193},{130,194},{131,195},{132,196},{133,197},{134,1... | collective-permute-start | bytes 98312 | tf_op jit(solution)/shard_map/ppermute | solution.py:458
  114.4 4.7 %collective-permute-start.15 = (f32[2,32,256]{2,1,0:T(8,128)S(1)}, f32[2,32,256]{2,1,0:T(8,128)S(1)}, u32[]{:S(2)}, u32[]{:S(2)}) collective-permute-start(f32[2,32,256]{2,1,0:T(8,128)S(1)} %get-tuple-element.55), channel_id=1, source_target_pairs={{0,2},{1,3},{2,0},{3,1},{4,6},{5,7},{6,4},{7,5},{8,10},{9,11},{10,... | collective-permute-start | bytes 196616 | tf_op jit(solution)/shard_map/ppermute | solution.py:483
  119.2 8.3 %collective-permute-start.20 = (f32[33,32,256]{2,1,0:T(8,128)S(1)}, f32[33,32,256]{2,1,0:T(8,128)S(1)}, u32[]{:S(2)}, u32[]{:S(2)}) collective-permute-start(f32[33,32,256]{2,1,0:T(8,128)S(1)} %shard_map.124), channel_id=1, source_target_pairs={{0,1},{1,0},{2,3},{3,2},{4,5},{5,4},{6,7},{7,6},{8,9},{9,8},{10,11... | collective-permute-start | bytes 3244040 | tf_op jit(solution)/shard_map/ppermute | solution.py:491
  (4 other events, 79.5 us)

commit v3 on v2

--- a/solution.py
+++ b/solution.py
@@ -14,7 +14,6 @@
 COURANT = 0.2
 HALF_LIGHT = 0.3
 
-SHIFTS = (0, 1, 3, 2)
 HALO = 4
 
 
@@ -52,23 +51,39 @@
     return lax.axis_index("comp").astype(jnp.int32), lax.axis_index("trc").astype(jnp.int32)
 
 
+def shift_of(turn, t):
+    if turn < 2:
+        return turn
+    return jnp.where(t == 0, turn, 5 - turn)
+
+
 def roll(x, shift, axis):
     return pltpu.roll(x, shift % x.shape[axis], axis)
 
 
-def pack_kernel(field, u, v, k, h, m, *refs):
-    segments, (low, high), (west, east, mask, sem) = refs[:4], refs[4:6], refs[6:]
+def segment_copies(field, segment, shift):
+    levels = field.shape[0]
+    group = segment.shape[0] - 2 * HALO
+    comps = levels // group
+    c, _ = position()
+    start = group * lax.rem(c + shift, comps)
+    after = jnp.minimum(start + group, levels - HALO)
+    return [
+        (field.at[pl.ds(start, group)], segment.at[pl.ds(HALO, group)]),
+        (field.at[pl.ds(jnp.maximum(start - HALO, 0), HALO)], segment.at[pl.ds(0, HALO)]),
+        (field.at[pl.ds(after, HALO)], segment.at[pl.ds(HALO + group, HALO)]),
+    ]
+
+
+def pack_kernel(field, u, v, k, h, m, one, three, low, high, side_low, side_high, west, east, mask, sem):
     levels, width = field.shape[0], field.shape[1]
     depth = u.shape[0]
-    comps = len(segments)
-    group = levels // comps
     copies = []
 
     def copy(src, dst):
         copies.append(pltpu.make_async_copy(src, dst, sem.at[len(copies)]))
         copies[-1].start()
 
-    place, _ = position()
     for index, source in enumerate((u, v, k)):
         rows = pl.ds(index * depth, depth)
         copy(source.at[:, width - 8 :, :], low.at[rows])
@@ -79,26 +94,22 @@
     copy(m.at[:8, :], mask.at[1])
     copy(field.at[:, :8, :], west)
     copy(field.at[:, width - 8 :, :], east)
-    for shift, segment in enumerate(segments):
-        target = lax.rem(place + shift, comps)
-        start = group * target
-        copy(field.at[pl.ds(start, group)], segment.at[pl.ds(HALO, group)])
-        copy(field.at[pl.ds(jnp.maximum(start - HALO, 0), HALO)], segment.at[pl.ds(0, HALO)])
-        after = jnp.minimum(start + group, levels - HALO)
-        copy(field.at[pl.ds(after, HALO)], segment.at[pl.ds(HALO + group, HALO)])
+    _, t = position()
+    for shift, segment in ((1, one), (shift_of(2, t), three)):
+        for src, dst in segment_copies(field, segment, shift):
+            copy(src, dst)
     for item in copies[:12]:
         item.wait()
     low[3 * depth + 1] = mask[0].astype(jnp.float32)
     high[3 * depth + 1] = mask[1].astype(jnp.float32)
     half = levels // 2
-    first = 3 * depth + 2
     upper = lax.broadcasted_iota(jnp.int32, west.shape[1:], 0) < HALO
 
     def body(level, carry):
         a, b = west[level], west[level + half]
-        high[first + level] = jnp.where(upper, a, roll(b, HALO, 0))
+        side_high[level] = jnp.where(upper, a, roll(b, HALO, 0))
         a, b = east[level], east[level + half]
-        low[first + level] = jnp.where(upper, roll(b, HALO, 0), a)
+        side_low[level] = jnp.where(upper, roll(b, HALO, 0), a)
         return carry
 
     lax.fori_loop(0, half, body, 0, unroll=4)
@@ -106,31 +117,35 @@
         item.wait()
 
 
-def side_kernel(first, low, high, inner, *refs):
-    segments, side = refs[:4], refs[4]
-    width = inner.shape[1]
+def side_kernel(field, low, high, own, one, two, three, side, sem):
     levels = side.shape[0]
     half = levels // 2
-    comps = len(segments)
+    width = field.shape[1]
+    comps = lax.axis_size("comp")
     group = levels // comps
-    c, _ = position()
+    c, t = position()
     upper = lax.broadcasted_iota(jnp.int32, side.shape[1:], 0) < HALO
+    copies = []
+    for shift, segment in ((0, own), (shift_of(3, t), two)):
+        for src, dst in segment_copies(field, segment.at[:, :width, :], shift):
+            copies.append(pltpu.make_async_copy(src, dst, sem.at[len(copies)]))
+            copies[-1].start()
 
     def body(level, carry):
-        a, b = high[first + level], low[first + level]
+        a, b = high[level], low[level]
         side[level] = jnp.where(upper, a, b)
         side[level + half] = roll(jnp.where(upper, b, a), HALO, 0)
         return carry
 
     lax.fori_loop(0, half, body, 0, unroll=4)
-    for shift, segment in enumerate(segments):
-        start = group * lax.rem(c + shift, comps)
-        if shift == SHIFTS[-1]:
-            segment[:, :width, :] = inner[...]
-            segment = segment.at[:, width:, :]
-        segment[pl.ds(HALO, group)] = side[pl.ds(start, group)]
-        segment[pl.ds(0, HALO)] = side[pl.ds(jnp.maximum(start - HALO, 0), HALO)]
-        segment[pl.ds(HALO + group, HALO)] = side[pl.ds(jnp.minimum(start + group, levels - HALO), HALO)]
+    for turn, segment in enumerate((own, one, three, two)):
+        start = group * lax.rem(c + shift_of(turn, t), comps)
+        columns = slice(width if turn in (0, 3) else 0, None)
+        segment[pl.ds(HALO, group), columns, :] = side[pl.ds(start, group)]
+        segment[pl.ds(0, HALO), columns, :] = side[pl.ds(jnp.maximum(start - HALO, 0), HALO)]
+        segment[pl.ds(HALO + group, HALO), columns, :] = side[pl.ds(jnp.minimum(start + group, levels - HALO), HALO)]
+    for item in copies:
+        item.wait()
 
 
 def ocean_kernel(last, u_ref, v_ref, k_ref, h_ref, m_ref, lo_ref, hi_ref, east_ref, north_ref, flux_ref):
@@ -217,11 +232,14 @@
     out[1] = near[...] + far[...]
 
 
-def transport_kernel(levels, weight, *refs):
-    parts, (mine_ref, other_ref, send_ref, sums_ref, a, b) = refs[:-6], refs[-6:]
+def transport_kernel(levels, turn, weight, *refs):
+    parts, refs = refs[: 2 - (turn in (0, 3))], refs[2 - (turn in (0, 3)) :]
+    if turn == 3:
+        earlier, near_ref, refs = refs[:3], refs[3], refs[4:]
+    mine_ref, other_ref, send_ref, sums_ref, a, b = refs
     total, _, _ = parts[0].shape
     width = mine_ref.shape[1]
-    _, t = position()
+    c, t = position()
     if len(parts) == 2:
         inner, side = parts
 
@@ -279,42 +297,47 @@
             part = (0.5 + m * m) / levels
             tau = part if tau is None else tau + part
         sums_ref[block] = tau
-
-
-def tau_kernel(holder, sums, *refs):
-    out = refs[-1]
-    c, t = position()
-    total = sums[0]
-    for index in range(1, sums.shape[0]):
-        total = total + sums[index]
-    for above in refs[:-1]:
-        total = total + above[...]
-    out[...] = jnp.where((t == 0) & (c == holder), total, 0.0)
-
-
-def start_kernel(*refs):
-    bases, sums, near, far = refs[:3], refs[3:7], refs[7], refs[8]
-    c, _ = position()
-    turn = functools.reduce(lambda x, i: jnp.where(c == SHIFTS[i], i, x), range(4), 0)
-    running = bases[0][...] + bases[1][...] + bases[2][...]
-    for index in range(4):
-        out = near if index < 2 else far
-        out[index % 2] = running
-        for i in range(4):
-            running = running + jnp.where(turn == i, sums[i][index], 0.0)
-
-
-def gather_kernel(near, far, *refs):
+    zero = jnp.zeros(sums_ref.shape[1:], jnp.float32)
+
+    def thickness(index, *by_comp):
+        total = zero
+        for holder, part in by_comp:
+            total = total + jnp.where((t == 0) & (c == holder), part[index], 0.0)
+        return total
+
+    if turn < 3:
+        send_ref[2 * HALO] = sum((thickness(index, (turn, sums_ref)) for index in range(4)), zero)
+    else:
+        running = zero
+        for index in range(4):
+            if index < 2:
+                near_ref[index] = running
+            else:
+                send_ref[2 * HALO + index - 2] = running
+            running = running + thickness(index, *enumerate((*earlier, sums_ref)))
+
+
+def tau_kernel(*refs):
+    sent, received, whole = refs[: len(refs) // 2], refs[len(refs) // 2 : -1], refs[-1]
+    _, t = position()
+    total = jnp.zeros(whole.shape, jnp.float32)
+    for here, there in zip(sent, received):
+        total = total + jnp.where(t == 0, here[2 * HALO], jnp.where(t == 2, there[2 * HALO], 0.0))
+    whole[...] = total
+
+
+def gather_kernel(near, one, two, three, *refs):
     others, across, out = refs[:4], refs[4:8], refs[8]
     depth = others[0].shape[0]
     _, t = position()
-    for slot in range(4):
-        out[slot * depth : (slot + 1) * depth] = others[slot][...]
-        out[(4 + slot) * depth : (5 + slot) * depth] = across[slot][depth:]
-    out[8 * depth] = jnp.where(t == 0, near[1], far[1])
-
-
-def reaction_kernel(levels, react_ref, sun_ref, near_ref, far_ref, *refs):
+    for turn in range(4):
+        out[turn * depth : (turn + 1) * depth] = others[turn][...]
+        out[(4 + turn) * depth : (5 + turn) * depth] = across[turn][depth : 2 * depth]
+    base = one[...] + two[...] + three[...]
+    out[8 * depth] = base + jnp.where(t == 0, near[1], across[3][2 * depth + 1])
+
+
+def reaction_kernel(levels, react_ref, sun_ref, near_ref, one, two, three, *refs):
     mine = refs[0:4]
     across = refs[4:8]
     core_ref, out_ref, heat_ref, depth, field = refs[8:]
@@ -326,17 +349,21 @@
 
     @pl.when(level == 0)
     def _():
-        inner = jnp.where(t == 0, near_ref[0], far_ref[0])
+        base = one[...] + two[...] + three[...]
+        inner = base + jnp.where(t == 0, near_ref[0], across[3][2 * HALO])
         depth[...] = jnp.where(t % 2 == 0, inner, core_ref[8 * deep])
 
     trcs = lax.axis_size("trc")
     comps = lax.axis_size("comp")
-    for slot, shift in enumerate(SHIFTS):
-        first = trcs * lax.rem(c + comps - shift, comps)
-        field[first + t] = mine[slot][level]
-        field[first + (t ^ 2)] = across[slot][level]
-        field[first + (t ^ 1)] = core_ref[slot * deep + level]
-        field[first + (t ^ 3)] = core_ref[(4 + slot) * deep + level]
+    for turn in range(4):
+
+        def tracer(holder, turn=turn):
+            return trcs * lax.rem(c + comps - shift_of(turn, holder), comps) + holder
+
+        field[tracer(t)] = mine[turn][level]
+        field[tracer(t ^ 2)] = across[turn][level]
+        field[tracer(t ^ 1)] = core_ref[turn * deep + level]
+        field[tracer(t ^ 3)] = core_ref[(4 + turn) * deep + level]
 
     def chunk(index, carry):
         row = pl.ds(pl.multiple_of(index * 8, 8), 8)
@@ -373,29 +400,36 @@
     flip_core = [(i, i ^ 1) for i in range(trcs)]
     both = ("comp", "trc")
     edges = 3 * depth + 2
-    payload = edges + levels // 2
-
-    def ring(shift):
-        return [(i, (i + shift) % comps) for i in range(comps)]
+
+    def ring(*shifts):
+        return [
+            (trcs * i + j, trcs * ((i + shifts[min(j, len(shifts) - 1)]) % comps) + j)
+            for i in range(comps)
+            for j in range(trcs)
+        ]
 
     packed = call(
         pack_kernel,
         4,
-        out_shape=(local(tall, width, rows),) * comps + (local(payload, 8, rows),) * 2,
+        out_shape=(local(tall, width, rows),) * 2
+        + (local(edges, 8, rows),) * 2
+        + (local(levels // 2, 8, rows),) * 2,
         in_specs=[ANY] * 6,
-        out_specs=(VMEM,) * (comps + 2),
+        out_specs=(VMEM,) * 6,
         scratch_shapes=[
             local(levels, 8, rows),
             local(levels, 8, rows),
             pltpu.VMEM((2, 8, rows), i32),
-            pltpu.SemaphoreType.DMA((12 + 3 * comps,)),
+            pltpu.SemaphoreType.DMA((18,)),
         ],
     )(*in_hbm(tracers[0], eastward, northward, mixing, surface_height, sea_mask))
-    inner = list(packed[:comps])
-    low = lax.ppermute(packed[comps], "horiz", forward)
-    high = lax.ppermute(packed[comps + 1], "horiz", backward)
-    inner[1] = lax.ppermute(inner[1], "comp", ring(1))
-    inner[3] = lax.ppermute(inner[3], "comp", ring(3))
+    one, three, low, high, side_low, side_high = packed
+    one = lax.ppermute(one, both, ring(1))
+    three = lax.ppermute(three, both, ring(2, 3))
+    low = lax.ppermute(low, "horiz", forward)
+    high = lax.ppermute(high, "horiz", backward)
+    side_low = lax.ppermute(side_low, "horiz", forward)
+    side_high = lax.ppermute(side_high, "horiz", backward)
 
     east_out, north_out, flux = call(
         functools.partial(ocean_kernel, levels - 1),
@@ -412,26 +446,24 @@
         both,
         [(trcs * i + last, trcs * i + nxt + 2) for i in ups] + [(trcs * i + nxt, trcs * i + 1) for i in ups],
     )
-    far = lax.ppermute(
-        flux,
-        both,
-        [(trcs * i + last, trcs * i + nxt) for i in ups] + [(trcs * i + nxt, trcs * i + last) for i in ups],
-    )
+    far = lax.ppermute(near, "trc", [(trcs - 2, 0), (1, trcs - 1)])
     across_flux = lax.ppermute(flux, "trc", flip_x)
     core_flux = lax.ppermute(flux, "trc", flip_core)
 
-    sides = list(
-        call(
-            functools.partial(side_kernel, edges),
-            1,
-            out_shape=tuple(local(tall, span if i == SHIFTS[-1] else 8, rows) for i in range(comps)),
-            in_specs=[VMEM] * 3,
-            out_specs=(VMEM,) * comps,
-            scratch_shapes=[local(levels, 8, rows)],
-        )(*in_vmem(low, high, inner[2]))
-    )
-    for shift in (1, 3, 2):
-        sides[shift] = lax.ppermute(sides[shift], "comp", ring(shift))
+    whole = local(tall, span, rows)
+    flank = local(tall, 8, rows)
+    own, side_one, two, side_three = call(
+        side_kernel,
+        1,
+        out_shape=(whole, flank, whole, flank),
+        in_specs=[ANY, VMEM, VMEM],
+        out_specs=(VMEM,) * 4,
+        scratch_shapes=[local(levels, 8, rows), pltpu.SemaphoreType.DMA((6,))],
+    )(*in_hbm(tracers[0]), *in_vmem(side_low, side_high))
+    side_one = lax.ppermute(side_one, both, ring(1))
+    side_three = lax.ppermute(side_three, both, ring(2, 3))
+    two = lax.ppermute(two, both, ring(3, 2))
+    parts = ((own,), (one, side_one), (three, side_three), (two,))
     pair = call(
         pair_kernel,
         1,
@@ -444,50 +476,47 @@
         weight_kernel, 3, out_shape=local(6, tall, span, rows), in_specs=[VMEM] * 4, out_specs=VMEM
     )(*in_vmem(flux, core_flux, pair, core_pair))
     piece = local(depth, width, rows)
-    mine, other, across, sums = [], [], [], []
+    mine, other, sends, across, sums = [], [], [], [], []
+    for turn in range(4):
+        inputs = [weight, *parts[turn]]
+        sent = 2 * depth
+        if turn == 3:
+            inputs += sums
+        sent += 2 if turn == 3 else 1
+        results = call(
+            functools.partial(transport_kernel, levels, turn),
+            6,
+            out_shape=(local(2, width, rows),) * (turn == 3)
+            + (piece, piece, local(sent, width, rows), piece),
+            in_specs=[VMEM] * len(inputs),
+            out_specs=(VMEM,) * (5 if turn == 3 else 4),
+            scratch_shapes=[local(tall, span, rows)] * 2,
+        )(*in_vmem(*inputs))
+        m, o, held, total = results[-4:]
+        mine.append(m)
+        other.append(o)
+        sends.append(held)
+        across.append(lax.ppermute(held, "trc", flip_x))
+        sums.append(total)
+    near = results[0]
     bases = []
-
-    def pass_tau(turn, holder):
-        value = call(
-            functools.partial(tau_kernel, holder),
+    for k in range(1, comps):
+        known = comps - k
+        thick = call(
+            tau_kernel,
             1,
             out_shape=local(width, rows),
-            in_specs=[VMEM] * (1 + len(bases[-1:])),
+            in_specs=[VMEM] * (2 * known),
             out_specs=VMEM,
-        )(*in_vmem(sums[turn], *bases[-1:]))
-        bases.append(lax.ppermute(value, "comp", [(holder, holder + 1)]))
-
-    for turn, shift in enumerate(SHIFTS):
-        inputs = [weight] + ([inner[shift]] if turn < 3 else []) + [sides[shift]]
-        m, o, s, total = call(
-            functools.partial(transport_kernel, levels),
-            6,
-            out_shape=(piece, piece, local(2 * depth, width, rows), piece),
-            in_specs=[VMEM] * len(inputs),
-            out_specs=(VMEM,) * 4,
-            scratch_shapes=[local(tall, span, rows)] * 2,
-        )(*in_vmem(*inputs))
-        mine.append(m)
-        other.append(o)
-        across.append(lax.ppermute(s, "trc", flip_x))
-        sums.append(total)
-        if shift < comps - 1:
-            pass_tau(turn, shift)
-    near, far = call(
-        start_kernel,
-        1,
-        out_shape=(local(2, width, rows),) * 2,
-        in_specs=[VMEM] * 7,
-        out_specs=(VMEM,) * 2,
-    )(*in_vmem(*bases, *sums))
-    far = lax.ppermute(far, "trc", flip_x)
+        )(*in_vmem(*sends[:known], *across[:known]))
+        bases.append(lax.ppermute(thick, "comp", [(i, i + k) for i in range(comps - k)]))
     cross = call(
         gather_kernel,
         2,
         out_shape=local(8 * depth + 1, width, rows),
-        in_specs=[VMEM] * 10,
+        in_specs=[VMEM] * 12,
         out_specs=VMEM,
-    )(*in_vmem(near, far, *other, *across))
+    )(*in_vmem(near, *bases, *other, *across))
     cross = lax.ppermute(cross, "trc", flip_core)
 
     count = reaction.shape[0]
@@ -496,13 +525,13 @@
         6,
         grid=(depth,),
         out_shape=(array(count, depth, width, rows), array(depth, width, rows)),
-        in_specs=[SMEM] + [VMEM] * 12,
+        in_specs=[SMEM] + [VMEM] * 14,
         out_specs=(
             pl.BlockSpec((count, 1, width, rows), lambda l: (0, l, 0, 0)),
             pl.BlockSpec((1, width, rows), lambda l: (l, 0, 0)),
         ),
         scratch_shapes=[local(width, rows), local(count, width, rows)],
-    )(reaction, *in_vmem(sunlight, near, far, *mine, *across, cross))
+    )(reaction, *in_vmem(sunlight, near, *bases, *mine, *across, cross))
     return (east_out, north_out, tracers_out, heating)
 
 

time: 133 us -> 132 us (level)
  the two profiles are of different devices: /device:TPU:125 before, /device:TPU:1 now
where the time goes in v3:
time: 132 us
  waiting for transfers between devices  57.7 us (44%)
  starting transfers between devices  50.4 us (38%)
  Pallas kernels  22.7 us (17%)
    ppermute x1, waiting for transfers between devices, per_device(): side_one = lax.ppermute(side_one, both, ring(1))  30.9 us
    pallas_call x4, Pallas kernels, per_device(): call(functools.partial(transport_kernel, levels, turn), 6, out_shape=(loc...  12.3 us
    ppermute x1, waiting for transfers between devices, per_device(): far = lax.ppermute(near, 'trc', [(trcs - 2, 0), (1, trcs - 1)])  7.52 us
    ppermute x4, starting transfers between devices, per_device(): across.append(lax.ppermute(held, 'trc', flip_x))  7 us
    ppermute x1, starting transfers between devices, per_device(): across_flux = lax.ppermute(flux, 'trc', flip_x)  6.58 us
    ppermute x4, waiting for transfers between devices, per_device(): across.append(lax.ppermute(held, 'trc', flip_x))  6.33 us
    ppermute x3, starting transfers between devices, per_device(): lax.ppermute(thick, 'comp', [(i, i + k) for i in range(comps - k)])  6.28 us
    pallas_call x1, Pallas kernels, per_device(): call(functools.partial(reaction_kernel, levels), 6, grid=(depth,), out_sh...  4.97 us
  transfers between devices with their start and end apart: 22, of which 9 were waited for; matrix products, arithmetic and copies ran while one was open for 0% of the time, Pallas kernels for 11%

profile of v3, /device:TPU:1, one launch (start us, length us, event | category | flops | bytes accessed | tf_op | source)
XLA Modules:
  0.0 131.8 jit_solution(7294833070469985360)
XLA Ops:
  0.7 2.0 %shard_map.111 = (f32[24,32,256]{2,1,0:T(8,128)S(1)}, f32[24,32,256]{2,1,0:T(8,128)S(1)}, f32[14,8,256]{2,1,0:T(8,128)S(1)}, f32[14,8,256]{2,1,0:T(8,128)S(1)}, ...) custom-call(f32[64,32,256]{2,1,0:T(8,128)} %bitcast.1, f32[4,32,256]{2,1,0:T(8,128)} %u_ref.1, f32[4,32,256]{2,1,0:T(8,128)} %v_ref.1, ...), custom_call_target="tpu_custom_call" | custom-call | flops 4000000 | bytes 4000000 | tf_op jit(solution)/shard_map/pallas_call | solution.py:411
  2.7 4.4 %collective-permute-start = (f32[14,8,256]{2,1,0:T(8,128)S(1)}, f32[14,8,256]{2,1,0:T(8,128)S(1)}, u32[]{:S(2)}, u32[]{:S(2)}) collective-permute-start(f32[14,8,256]{2,1,0:T(8,128)S(1)} %get-tuple-element.35), channel_id=1, source_target_pairs={{0,4},{4,8},{8,12},{12,16},{16,20},{20,24},{24,28},{28,32},{32,36}... | collective-permute-start | bytes 344072 | tf_op jit(solution)/shard_map/ppermute | solution.py:429
  8.9 3.9 %collective-permute-done.1.hi_ref = f32[14,8,256]{2,1,0:T(8,128)S(1)} collective-permute-done((f32[14,8,256]{2,1,0:T(8,128)S(1)}, f32[14,8,256]{2,1,0:T(8,128)S(1)}, u32[]{:S(2)}, u32[]{:S(2)}) %collective-permute-start.1) | collective-permute-done | bytes 114720 | tf_op jit(solution)/shard_map/ppermute | solution.py:430
  15.3 6.6 %collective-permute-start.3 = (f32[3,4,40,256]{3,2,1,0:T(8,128)S(1)}, f32[3,4,40,256]{3,2,1,0:T(8,128)S(1)}, u32[]{:S(2)}, u32[]{:S(2)}) collective-permute-start(f32[3,4,40,256]{3,2,1,0:T(8,128)S(1)} %get-tuple-element.39.own), channel_id=1, source_target_pairs={{0,2},{1,3},{2,0},{3,1},{4,6},{5,7},{6,4},{7,5},{8,10},{9,11},{10,... | collective-permute-start | bytes 1474568 | tf_op jit(solution)/shard_map/ppermute | solution.py:450
  21.8 3.3 %collective-permute-done.4.near = f32[3,4,40,256]{3,2,1,0:T(8,128)S(1)} collective-permute-done((f32[3,4,40,256]{3,2,1,0:T(8,128)S(1)}, f32[3,4,40,256]{3,2,1,0:T(8,128)S(1)}, u32[]{:S(2)}, u32[]{:S(2)}) %collective-permute-start.4) | collective-permute-done | bytes 491552 | tf_op jit(solution)/shard_map/ppermute | solution.py:444
  25.2 4.2 %collective-permute-start.5 = (f32[3,4,40,256]{3,2,1,0:T(8,128)S(1)}, f32[3,4,40,256]{3,2,1,0:T(8,128)S(1)}, u32[]{:S(2)}, u32[]{:S(2)}) collective-permute-start(f32[3,4,40,256]{3,2,1,0:T(8,128)S(1)} %collective-permute-done.4.near), channel_id=1, source_target_pairs={{2,0},{1,3},{6,4},{5,7},{10,8},{9,11},{14,12},{13,15},{18,16},{17,... | collective-permute-start | bytes 1474568 | tf_op jit(solution)/shard_map/ppermute | solution.py:449
  29.4 3.6 %collective-permute-start.7 = (f32[32,8,256]{2,1,0:T(8,128)S(1)}, f32[32,8,256]{2,1,0:T(8,128)S(1)}, u32[]{:S(2)}, u32[]{:S(2)}) collective-permute-start(f32[32,8,256]{2,1,0:T(8,128)S(1)} %get-tuple-element.40), channel_id=1, source_target_pairs={{0,4},{4,8},{8,12},{12,16},{16,20},{20,24},{24,28},{28,32},{32,36}... | collective-permute-start | bytes 786440 | tf_op jit(solution)/shard_map/ppermute | solution.py:431
  34.3 7.5 %collective-permute-done.5.far = f32[3,4,40,256]{3,2,1,0:T(8,128)S(1)} collective-permute-done((f32[3,4,40,256]{3,2,1,0:T(8,128)S(1)}, f32[3,4,40,256]{3,2,1,0:T(8,128)S(1)}, u32[]{:S(2)}, u32[]{:S(2)}) %collective-permute-start.5) | collective-permute-done | bytes 491552 | tf_op jit(solution)/shard_map/ppermute | solution.py:449
  44.8 3.6 %collective-permute-start.9 = (f32[24,40,256]{2,1,0:T(8,128)S(1)}, f32[24,40,256]{2,1,0:T(8,128)S(1)}, u32[]{:S(2)}, u32[]{:S(2)}) collective-permute-start(f32[24,40,256]{2,1,0:T(8,128)S(1)} %get-tuple-element.42), channel_id=1, source_target_pairs={{0,192},{1,129},{2,130},{3,131},{64,0},{65,193},{66,194},{67,195},... | collective-permute-start | bytes 2949128 | tf_op jit(solution)/shard_map/ppermute | solution.py:465
  48.4 2.7 %collective-permute-start.12 = (f32[24,32,256]{2,1,0:T(8,128)S(1)}, f32[24,32,256]{2,1,0:T(8,128)S(1)}, u32[]{:S(2)}, u32[]{:S(2)}) collective-permute-start(f32[24,32,256]{2,1,0:T(8,128)S(1)} %get-tuple-element.48), channel_id=1, source_target_pairs={{0,128},{1,193},{2,194},{3,195},{64,192},{65,1},{66,2},{67,3},{128... | collective-permute-start | bytes 2359304 | tf_op jit(solution)/shard_map/ppermute | solution.py:428
  51.0 1.9 %collective-permute-done.2.core = f32[3,4,40,256]{3,2,1,0:T(8,128)S(1)} collective-permute-done((f32[3,4,40,256]{3,2,1,0:T(8,128)S(1)}, f32[3,4,40,256]{3,2,1,0:T(8,128)S(1)}, u32[]{:S(2)}, u32[]{:S(2)}) %collective-permute-start.2) | collective-permute-done | bytes 491552 | tf_op jit(solution)/shard_map/ppermute | solution.py:451
  52.9 2.7 %collective-permute-start.13 = (f32[24,8,256]{2,1,0:T(8,128)S(1)}, f32[24,8,256]{2,1,0:T(8,128)S(1)}, u32[]{:S(2)}, u32[]{:S(2)}) collective-permute-start(f32[24,8,256]{2,1,0:T(8,128)S(1)} %get-tuple-element.49), channel_id=1, source_target_pairs={{0,128},{1,193},{2,194},{3,195},{64,192},{65,1},{66,2},{67,3},{128... | collective-permute-start | bytes 589832 | tf_op jit(solution)/shard_map/ppermute | solution.py:464
  56.3 2.9 %shard_map.116 = (f32[4,32,256]{2,1,0:T(8,128)S(1)}, f32[4,32,256]{2,1,0:T(8,128)S(1)}, f32[9,32,256]{2,1,0:T(8,128)S(1)}, f32[4,32,256]{2,1,0:T(8,128)S(1)}) custom-call(f32[6,24,40,256]{3,2,1,0:T(8,128)S(1)} %shard_map.114.weight, f32[24,40,256]{2,1,0:T(8,128)S(1)} %get-tuple-element.43.refs_0_), custom_call_target="tpu_custom_call" | custom-call | flops 6000000 | bytes 6000000 | tf_op jit(solution)/shard_map/pallas_call | solution.py:486
  59.2 30.9 %collective-permute-done.11.refs_1_ = f32[24,8,256]{2,1,0:T(8,128)S(1)} collective-permute-done((f32[24,8,256]{2,1,0:T(8,128)S(1)}, f32[24,8,256]{2,1,0:T(8,128)S(1)}, u32[]{:S(2)}, u32[]{:S(2)}) %collective-permute-start.11) | collective-permute-done | bytes 196640 | tf_op jit(solution)/shard_map/ppermute | solution.py:463
  90.0 3.7 %collective-permute-start.14 = (f32[9,32,256]{2,1,0:T(8,128)S(1)}, f32[9,32,256]{2,1,0:T(8,128)S(1)}, u32[]{:S(2)}, u32[]{:S(2)}) collective-permute-start(f32[9,32,256]{2,1,0:T(8,128)S(1)} %get-tuple-element.52.refs_0_), channel_id=1, source_target_pairs={{0,2},{1,3},{2,0},{3,1},{4,6},{5,7},{6,4},{7,5},{8,10},{9,11},{10,... | collective-permute-start | bytes 884744 | tf_op jit(solution)/shard_map/ppermute | solution.py:499
  93.7 2.9 %shard_map.117 = (f32[4,32,256]{2,1,0:T(8,128)S(1)}, f32[4,32,256]{2,1,0:T(8,128)S(1)}, f32[9,32,256]{2,1,0:T(8,128)S(1)}, f32[4,32,256]{2,1,0:T(8,128)S(1)}) custom-call(f32[6,24,40,256]{3,2,1,0:T(8,128)S(1)} %shard_map.114.weight, f32[24,32,256]{2,1,0:T(8,128)S(1)} %collective-permute-done.10.refs_0_, f32[24,8,256]{2,1,0:T(8,128)S(1)} %collective-permute-done.11.refs_1_), custom_call_target="tpu_custom_call" | custom-call | flops 6000000 | bytes 6000000 | tf_op jit(solution)/shard_map/pallas_call | solution.py:486
  96.9 2.9 %shard_map.118 = (f32[4,32,256]{2,1,0:T(8,128)S(1)}, f32[4,32,256]{2,1,0:T(8,128)S(1)}, f32[9,32,256]{2,1,0:T(8,128)S(1)}, f32[4,32,256]{2,1,0:T(8,128)S(1)}) custom-call(f32[6,24,40,256]{3,2,1,0:T(8,128)S(1)} %shard_map.114.weight, f32[24,32,256]{2,1,0:T(8,128)S(1)} %collective-permute-done.12.refs_0_, f32[24,8,256]{2,1,0:T(8,128)S(1)} %collective-permute-done.13.refs_1_), custom_call_target="tpu_custom_call" | custom-call | flops 6000000 | bytes 6000000 | tf_op jit(solution)/shard_map/pallas_call | solution.py:486
  99.9 3.0 %collective-permute-start.16 = (f32[9,32,256]{2,1,0:T(8,128)S(1)}, f32[9,32,256]{2,1,0:T(8,128)S(1)}, u32[]{:S(2)}, u32[]{:S(2)}) collective-permute-start(f32[9,32,256]{2,1,0:T(8,128)S(1)} %get-tuple-element.54.refs_2_), channel_id=1, source_target_pairs={{0,2},{1,3},{2,0},{3,1},{4,6},{5,7},{6,4},{7,5},{8,10},{9,11},{10,... | collective-permute-start | bytes 884744 | tf_op jit(solution)/shard_map/ppermute | solution.py:499
  102.9 3.5 %shard_map.119 = (f32[2,32,256]{2,1,0:T(8,128)S(1)}, f32[4,32,256]{2,1,0:T(8,128)S(1)}, f32[4,32,256]{2,1,0:T(8,128)S(1)}, f32[10,32,256]{2,1,0:T(8,128)S(1)}, f32[4,32,256]{2,1,0:T(8,128)}) custom-call(f32[6,24,40,256]{3,2,1,0:T(8,128)S(1)} %shard_map.114.weight, f32[24,40,256]{2,1,0:T(8,128)S(1)} %collective-permute-done.9.refs_0_, ...), custom_call_target="tpu_custom_call" | custom-call | flops 6000000 | bytes 6000000 | tf_op jit(solution)/shard_map/pallas_call | solution.py:486
  106.5 6.3 %collective-permute-done.16.refs_5_.refs_6_ = f32[9,32,256]{2,1,0:T(8,128)S(1)} collective-permute-done((f32[9,32,256]{2,1,0:T(8,128)S(1)}, f32[9,32,256]{2,1,0:T(8,128)S(1)}, u32[]{:S(2)}, u32[]{:S(2)}) %collective-permute-start.16) | collective-permute-done | bytes 294944 | tf_op jit(solution)/shard_map/ppermute | solution.py:499
  112.8 3.4 %collective-permute-start.17 = (f32[32,256]{1,0:T(8,128)S(1)}, f32[32,256]{1,0:T(8,128)S(1)}, u32[]{:S(2)}, u32[]{:S(2)}) collective-permute-start(f32[32,256]{1,0:T(8,128)S(1)} %shard_map.120), channel_id=1, source_target_pairs={{0,64},{64,128},{128,192},{1,65},{65,129},{129,193},{2,66},{66,130... | collective-permute-start | bytes 98312 | tf_op jit(solution)/shard_map/ppermute | solution.py:512
  120.3 4.1 %collective-permute-start.21 = (f32[33,32,256]{2,1,0:T(8,128)S(1)}, f32[33,32,256]{2,1,0:T(8,128)S(1)}, u32[]{:S(2)}, u32[]{:S(2)}) collective-permute-start(f32[33,32,256]{2,1,0:T(8,128)S(1)} %shard_map.123), channel_id=1, source_target_pairs={{0,1},{1,0},{2,3},{3,2},{4,5},{5,4},{6,7},{7,6},{8,9},{9,8},{10,11... | collective-permute-start | bytes 3244040 | tf_op jit(solution)/shard_map/ppermute | solution.py:520
  124.4 2.3 %collective-permute-done.21.refs_8_ = f32[33,32,256]{2,1,0:T(8,128)S(1)} collective-permute-done((f32[33,32,256]{2,1,0:T(8,128)S(1)}, f32[33,32,256]{2,1,0:T(8,128)S(1)}, u32[]{:S(2)}, u32[]{:S(2)}) %collective-permute-start.21) | collective-permute-done | bytes 1081376 | tf_op jit(solution)/shard_map/ppermute | solution.py:520
  126.8 5.0 %shard_map.124 = (f32[16,4,32,256]{3,2,1,0:T(8,128)}, f32[4,32,256]{2,1,0:T(8,128)}) custom-call(f32[16,16]{1,0:T(8,128)S(1)} %copy-done.6, f32[32,256]{1,0:T(8,128)S(1)} %copy-done.5, f32[2,32,256]{2,1,0:T(8,128)S(1)} %get-tuple-element.51.near.near_ref, f32[32,256]{1,0:T(8,128)S(1)} %collective-permute-done.17.one, ...), custom_call_target="tpu_custom_call" | custom-call | flops 6000000 | bytes 6000000 | tf_op jit(solution)/shard_map/pallas_call | solution.py:523
  (48 shorter events, 13.5 us)
Async XLA Ops:
  0.6 12.2 %copy-start = (f32[4,32,256]{2,1,0:T(8,128)S(1)}, f32[4,32,256]{2,1,0:T(8,128)}, u32[]{:S(2)}) copy-start(f32[4,32,256]{2,1,0:T(8,128)} %u_ref.1) | copy-start | bytes 393220
  0.6 12.2 %copy-start.1 = (f32[4,32,256]{2,1,0:T(8,128)S(1)}, f32[4,32,256]{2,1,0:T(8,128)}, u32[]{:S(2)}) copy-start(f32[4,32,256]{2,1,0:T(8,128)} %v_ref.1) | copy-start | bytes 393220
  2.7 6.1 %collective-permute-start = (f32[14,8,256]{2,1,0:T(8,128)S(1)}, f32[14,8,256]{2,1,0:T(8,128)S(1)}, u32[]{:S(2)}, u32[]{:S(2)}) collective-permute-start(f32[14,8,256]{2,1,0:T(8,128)S(1)} %get-tuple-element.35), channel_id=1, source_target_pairs={{0,4},{4,8},{8,12},{12,16},{16,20},{20,24},{24,28},{28,32},{32,36}... | collective-permute-start | bytes 344072 | tf_op jit(solution)/shard_map/ppermute | solution.py:429
  7.1 5.7 %collective-permute-start.1 = (f32[14,8,256]{2,1,0:T(8,128)S(1)}, f32[14,8,256]{2,1,0:T(8,128)S(1)}, u32[]{:S(2)}, u32[]{:S(2)}) collective-permute-start(f32[14,8,256]{2,1,0:T(8,128)S(1)} %get-tuple-element.36), channel_id=1, source_target_pairs={{4,0},{8,4},{12,8},{16,12},{20,16},{24,20},{28,24},{32,28},{36,32}... | collective-permute-start | bytes 344072 | tf_op jit(solution)/shard_map/ppermute | solution.py:430
  14.0 11.2 %collective-permute-start.4 = (f32[3,4,40,256]{3,2,1,0:T(8,128)S(1)}, f32[3,4,40,256]{3,2,1,0:T(8,128)S(1)}, u32[]{:S(2)}, u32[]{:S(2)}) collective-permute-start(f32[3,4,40,256]{3,2,1,0:T(8,128)S(1)} %get-tuple-element.39.own), channel_id=1, source_target_pairs={{3,66},{67,130},{131,194},{64,1},{128,65},{192,129},{7,70},{71,134... | collective-permute-start | bytes 1474568 | tf_op jit(solution)/shard_map/ppermute | solution.py:444
  15.3 19.0 %collective-permute-start.3 = (f32[3,4,40,256]{3,2,1,0:T(8,128)S(1)}, f32[3,4,40,256]{3,2,1,0:T(8,128)S(1)}, u32[]{:S(2)}, u32[]{:S(2)}) collective-permute-start(f32[3,4,40,256]{3,2,1,0:T(8,128)S(1)} %get-tuple-element.39.own), channel_id=1, source_target_pairs={{0,2},{1,3},{2,0},{3,1},{4,6},{5,7},{6,4},{7,5},{8,10},{9,11},{10,... | collective-permute-start | bytes 1474568 | tf_op jit(solution)/shard_map/ppermute | solution.py:450
  25.2 16.6 %collective-permute-start.5 = (f32[3,4,40,256]{3,2,1,0:T(8,128)S(1)}, f32[3,4,40,256]{3,2,1,0:T(8,128)S(1)}, u32[]{:S(2)}, u32[]{:S(2)}) collective-permute-start(f32[3,4,40,256]{3,2,1,0:T(8,128)S(1)} %collective-permute-done.4.near), channel_id=1, source_target_pairs={{2,0},{1,3},{6,4},{5,7},{10,8},{9,11},{14,12},{13,15},{18,16},{17,... | collective-permute-start | bytes 1474568 | tf_op jit(solution)/shard_map/ppermute | solution.py:449
  29.4 14.0 %collective-permute-start.7 = (f32[32,8,256]{2,1,0:T(8,128)S(1)}, f32[32,8,256]{2,1,0:T(8,128)S(1)}, u32[]{:S(2)}, u32[]{:S(2)}) collective-permute-start(f32[32,8,256]{2,1,0:T(8,128)S(1)} %get-tuple-element.40), channel_id=1, source_target_pairs={{0,4},{4,8},{8,12},{12,16},{16,20},{20,24},{24,28},{28,32},{32,36}... | collective-permute-start | bytes 786440 | tf_op jit(solution)/shard_map/ppermute | solution.py:431
  33.0 10.4 %collective-permute-start.8 = (f32[32,8,256]{2,1,0:T(8,128)S(1)}, f32[32,8,256]{2,1,0:T(8,128)S(1)}, u32[]{:S(2)}, u32[]{:S(2)}) collective-permute-start(f32[32,8,256]{2,1,0:T(8,128)S(1)} %get-tuple-element.41), channel_id=1, source_target_pairs={{4,0},{8,4},{12,8},{16,12},{20,16},{24,20},{28,24},{32,28},{36,32}... | collective-permute-start | bytes 786440 | tf_op jit(solution)/shard_map/ppermute | solution.py:432
  41.9 11.0 %collective-permute-start.6 = (f32[2,3,4,40,256]{4,3,2,1,0:T(8,128)S(1)}, f32[2,3,4,40,256]{4,3,2,1,0:T(8,128)S(1)}, u32[]{:S(2)}, u32[]{:S(2)}) collective-permute-start(f32[2,3,4,40,256]{4,3,2,1,0:T(8,128)S(1)} %shard_map.113.pair), channel_id=1, source_target_pairs={{0,1},{1,0},{2,3},{3,2},{4,5},{5,4},{6,7},{7,6},{8,9},{9,8},{10,11... | collective-permute-start | bytes 2949128 | tf_op jit(solution)/shard_map/ppermute | solution.py:474
  44.8 58.1 %collective-permute-start.9 = (f32[24,40,256]{2,1,0:T(8,128)S(1)}, f32[24,40,256]{2,1,0:T(8,128)S(1)}, u32[]{:S(2)}, u32[]{:S(2)}) collective-permute-start(f32[24,40,256]{2,1,0:T(8,128)S(1)} %get-tuple-element.42), channel_id=1, source_target_pairs={{0,192},{1,129},{2,130},{3,131},{64,0},{65,193},{66,194},{67,195},... | collective-permute-start | bytes 2949128 | tf_op jit(solution)/shard_map/ppermute | solution.py:465
  48.4 45.3 %collective-permute-start.10 = (f32[24,32,256]{2,1,0:T(8,128)S(1)}, f32[24,32,256]{2,1,0:T(8,128)S(1)}, u32[]{:S(2)}, u32[]{:S(2)}) collective-permute-start(f32[24,32,256]{2,1,0:T(8,128)S(1)} %get-tuple-element.45), channel_id=1, source_target_pairs={{0,64},{1,65},{2,66},{3,67},{64,128},{65,129},{66,130},{67,131},{1... | collective-permute-start | bytes 2359304 | tf_op jit(solution)/shard_map/ppermute | solution.py:427
  48.4 48.6 %collective-permute-start.12 = (f32[24,32,256]{2,1,0:T(8,128)S(1)}, f32[24,32,256]{2,1,0:T(8,128)S(1)}, u32[]{:S(2)}, u32[]{:S(2)}) collective-permute-start(f32[24,32,256]{2,1,0:T(8,128)S(1)} %get-tuple-element.48), channel_id=1, source_target_pairs={{0,128},{1,193},{2,194},{3,195},{64,192},{65,1},{66,2},{67,3},{128... | collective-permute-start | bytes 2359304 | tf_op jit(solution)/shard_map/ppermute | solution.py:428
  51.0 1.9 %collective-permute-start.2 = (f32[3,4,40,256]{3,2,1,0:T(8,128)S(1)}, f32[3,4,40,256]{3,2,1,0:T(8,128)S(1)}, u32[]{:S(2)}, u32[]{:S(2)}) collective-permute-start(f32[3,4,40,256]{3,2,1,0:T(8,128)S(1)} %get-tuple-element.39.own), channel_id=1, source_target_pairs={{0,1},{1,0},{2,3},{3,2},{4,5},{5,4},{6,7},{7,6},{8,9},{9,8},{10,11... | collective-permute-start | bytes 1474568 | tf_op jit(solution)/shard_map/ppermute | solution.py:451
  52.9 37.1 %collective-permute-start.11 = (f32[24,8,256]{2,1,0:T(8,128)S(1)}, f32[24,8,256]{2,1,0:T(8,128)S(1)}, u32[]{:S(2)}, u32[]{:S(2)}) collective-permute-start(f32[24,8,256]{2,1,0:T(8,128)S(1)} %get-tuple-element.46), channel_id=1, source_target_pairs={{0,64},{1,65},{2,66},{3,67},{64,128},{65,129},{66,130},{67,131},{1... | collective-permute-start | bytes 589832 | tf_op jit(solution)/shard_map/ppermute | solution.py:463
  52.9 44.0 %collective-permute-start.13 = (f32[24,8,256]{2,1,0:T(8,128)S(1)}, f32[24,8,256]{2,1,0:T(8,128)S(1)}, u32[]{:S(2)}, u32[]{:S(2)}) collective-permute-start(f32[24,8,256]{2,1,0:T(8,128)S(1)} %get-tuple-element.49), channel_id=1, source_target_pairs={{0,128},{1,193},{2,194},{3,195},{64,192},{65,1},{66,2},{67,3},{128... | collective-permute-start | bytes 589832 | tf_op jit(solution)/shard_map/ppermute | solution.py:464
  90.0 16.5 %collective-permute-start.14 = (f32[9,32,256]{2,1,0:T(8,128)S(1)}, f32[9,32,256]{2,1,0:T(8,128)S(1)}, u32[]{:S(2)}, u32[]{:S(2)}) collective-permute-start(f32[9,32,256]{2,1,0:T(8,128)S(1)} %get-tuple-element.52.refs_0_), channel_id=1, source_target_pairs={{0,2},{1,3},{2,0},{3,1},{4,6},{5,7},{6,4},{7,5},{8,10},{9,11},{10,... | collective-permute-start | bytes 884744 | tf_op jit(solution)/shard_map/ppermute | solution.py:499
  96.6 9.9 %collective-permute-start.15 = (f32[9,32,256]{2,1,0:T(8,128)S(1)}, f32[9,32,256]{2,1,0:T(8,128)S(1)}, u32[]{:S(2)}, u32[]{:S(2)}) collective-permute-start(f32[9,32,256]{2,1,0:T(8,128)S(1)} %get-tuple-element.53.refs_1_), channel_id=1, source_target_pairs={{0,2},{1,3},{2,0},{3,1},{4,6},{5,7},{6,4},{7,5},{8,10},{9,11},{10,... | collective-permute-start | bytes 884744 | tf_op jit(solution)/shard_map/ppermute | solution.py:499
  99.9 12.9 %collective-permute-start.16 = (f32[9,32,256]{2,1,0:T(8,128)S(1)}, f32[9,32,256]{2,1,0:T(8,128)S(1)}, u32[]{:S(2)}, u32[]{:S(2)}) collective-permute-start(f32[9,32,256]{2,1,0:T(8,128)S(1)} %get-tuple-element.54.refs_2_), channel_id=1, source_target_pairs={{0,2},{1,3},{2,0},{3,1},{4,6},{5,7},{6,4},{7,5},{8,10},{9,11},{10,... | collective-permute-start | bytes 884744 | tf_op jit(solution)/shard_map/ppermute | solution.py:499
  106.4 13.8 %collective-permute-start.20 = (f32[10,32,256]{2,1,0:T(8,128)S(1)}, f32[10,32,256]{2,1,0:T(8,128)S(1)}, u32[]{:S(2)}, u32[]{:S(2)}) collective-permute-start(f32[10,32,256]{2,1,0:T(8,128)S(1)} %get-tuple-element.59), channel_id=1, source_target_pairs={{0,2},{1,3},{2,0},{3,1},{4,6},{5,7},{6,4},{7,5},{8,10},{9,11},{10,... | collective-permute-start | bytes 983048 | tf_op jit(solution)/shard_map/ppermute | solution.py:499
  112.8 6.4 %collective-permute-start.17 = (f32[32,256]{1,0:T(8,128)S(1)}, f32[32,256]{1,0:T(8,128)S(1)}, u32[]{:S(2)}, u32[]{:S(2)}) collective-permute-start(f32[32,256]{1,0:T(8,128)S(1)} %shard_map.120), channel_id=1, source_target_pairs={{0,64},{64,128},{128,192},{1,65},{65,129},{129,193},{2,66},{66,130... | collective-permute-start | bytes 98312 | tf_op jit(solution)/shard_map/ppermute | solution.py:512
  116.3 2.9 %collective-permute-start.18 = (f32[32,256]{1,0:T(8,128)S(1)}, f32[32,256]{1,0:T(8,128)S(1)}, u32[]{:S(2)}, u32[]{:S(2)}) collective-permute-start(f32[32,256]{1,0:T(8,128)S(1)} %shard_map.121), channel_id=1, source_target_pairs={{0,128},{64,192},{1,129},{65,193},{2,130},{66,194},{3,131},{67,195... | collective-permute-start | bytes 98312 | tf_op jit(solution)/shard_map/ppermute | solution.py:512
  117.9 2.3 %collective-permute-start.19 = (f32[32,256]{1,0:T(8,128)S(1)}, f32[32,256]{1,0:T(8,128)S(1)}, u32[]{:S(2)}, u32[]{:S(2)}) collective-permute-start(f32[32,256]{1,0:T(8,128)S(1)} %shard_map.122), channel_id=1, source_target_pairs={{0,192},{1,193},{2,194},{3,195},{4,196},{5,197},{6,198},{7,199},{8... | collective-permute-start | bytes 98312 | tf_op jit(solution)/shard_map/ppermute | solution.py:512
  120.3 6.5 %collective-permute-start.21 = (f32[33,32,256]{2,1,0:T(8,128)S(1)}, f32[33,32,256]{2,1,0:T(8,128)S(1)}, u32[]{:S(2)}, u32[]{:S(2)}) collective-permute-start(f32[33,32,256]{2,1,0:T(8,128)S(1)} %shard_map.123), channel_id=1, source_target_pairs={{0,1},{1,0},{2,3},{3,2},{4,5},{5,4},{6,7},{7,6},{8,9},{9,8},{10,11... | collective-permute-start | bytes 3244040 | tf_op jit(solution)/shard_map/ppermute | solution.py:520
  (5 other events, 57.5 us)

commit v4 on v3

--- a/solution.py
+++ b/solution.py
@@ -326,60 +326,96 @@
     whole[...] = total
 
 
-def gather_kernel(near, one, two, three, *refs):
-    others, across, out = refs[:4], refs[4:8], refs[8]
+def gather_kernel(*refs):
+    others, across, out = refs[:4], refs[4:6], refs[6]
     depth = others[0].shape[0]
+    for index, ref in enumerate(others):
+        out[index * depth : (index + 1) * depth] = ref[...]
+    for index, ref in enumerate(across):
+        out[(4 + index) * depth : (5 + index) * depth] = ref[depth : 2 * depth]
+
+
+def last_kernel(near, one, two, three, third, fourth, out):
+    depth = (out.shape[0] - 1) // 2
     _, t = position()
-    for turn in range(4):
-        out[turn * depth : (turn + 1) * depth] = others[turn][...]
-        out[(4 + turn) * depth : (5 + turn) * depth] = across[turn][depth : 2 * depth]
+    out[:depth] = third[depth : 2 * depth]
+    out[depth : 2 * depth] = fourth[depth : 2 * depth]
     base = one[...] + two[...] + three[...]
-    out[8 * depth] = base + jnp.where(t == 0, near[1], across[3][2 * depth + 1])
-
-
-def reaction_kernel(levels, react_ref, sun_ref, near_ref, one, two, three, *refs):
+    out[2 * depth] = base + jnp.where(t == 0, near[1], fourth[2 * depth + 1])
+
+
+def tracer_of(turn, flip):
+    c, t = position()
+    comps, trcs = lax.axis_size("comp"), lax.axis_size("trc")
+    holder = t ^ flip
+    return trcs * lax.rem(c + comps - shift_of(turn, holder), comps) + holder
+
+
+def growth_kernel(terms, react_ref, *refs):
+    count, depth, width, _ = refs[-1].shape
+    out = refs[-1]
+    arrays = max(term[0] for term in terms) + 1
+    before = refs[arrays:-1]
+    tracers = [tracer_of(turn, flip) for _, _, turn, flip in terms]
+    per_level = width // 8
+
+    def chunk(index, carry):
+        level = lax.div(index, per_level)
+        row = pl.ds(pl.multiple_of(lax.rem(index, per_level) * 8, 8), 8)
+        values = [refs[which][start + level, row, :] for which, start, _, _ in terms]
+        for i in range(count):
+            total = before[0][i, level, row, :] if before else None
+            for tracer, value in zip(tracers, values):
+                part = react_ref[i, tracer] * value
+                total = part if total is None else total + part
+            out[i, level, row, :] = total
+        return carry
+
+    lax.fori_loop(0, depth * per_level, chunk, 0)
+
+
+def reaction_kernel(levels, react_ref, sun_ref, near_ref, one, two, three, growth_ref, *refs):
     mine = refs[0:4]
     across = refs[4:8]
-    core_ref, out_ref, heat_ref, depth, field = refs[8:]
+    core_ref, last_ref, out_ref, heat_ref, depth, field = refs[8:]
     rows = out_ref.shape[2]
     count = out_ref.shape[0]
     level = pl.program_id(0)
     deep = pl.num_programs(0)
-    c, t = position()
+    _, t = position()
 
     @pl.when(level == 0)
     def _():
         base = one[...] + two[...] + three[...]
         inner = base + jnp.where(t == 0, near_ref[0], across[3][2 * HALO])
-        depth[...] = jnp.where(t % 2 == 0, inner, core_ref[8 * deep])
-
-    trcs = lax.axis_size("trc")
-    comps = lax.axis_size("comp")
+        depth[...] = jnp.where(t % 2 == 0, inner, last_ref[2 * deep])
+
     for turn in range(4):
-
-        def tracer(holder, turn=turn):
-            return trcs * lax.rem(c + comps - shift_of(turn, holder), comps) + holder
-
-        field[tracer(t)] = mine[turn][level]
-        field[tracer(t ^ 2)] = across[turn][level]
-        field[tracer(t ^ 1)] = core_ref[turn * deep + level]
-        field[tracer(t ^ 3)] = core_ref[(4 + turn) * deep + level]
+        field[tracer_of(turn, 0)] = mine[turn][level]
+        field[tracer_of(turn, 2)] = across[turn][level]
+        field[tracer_of(turn, 1)] = core_ref[turn * deep + level]
+        if turn < 2:
+            field[tracer_of(turn, 3)] = core_ref[(4 + turn) * deep + level]
+        else:
+            field[tracer_of(turn, 3)] = last_ref[(turn - 2) * deep + level]
+    added = [(tracer_of(2 + part, 3), part) for part in range(2)]
 
     def chunk(index, carry):
         row = pl.ds(pl.multiple_of(index * 8, 8), 8)
-        m = [field[j, row, :] for j in range(count)]
-        tau = (0.5 + m[0] * m[0]) / levels
+        lead = field[0, row, :]
+        tau = (0.5 + lead * lead) / levels
         above = depth[row, :]
         light_top = sun_ref[row, :] * jnp.exp(-above)
         heat_ref[0, row, :] = levels * light_top * (1.0 - jnp.exp(-tau))
         depth[row, :] = above + tau
         light_mid = light_top * jnp.exp(-0.5 * tau)
         limit = light_mid / (light_mid + HALF_LIGHT)
+        values = [(tracer, last_ref[part * deep + level, row, :]) for tracer, part in added]
         for i in range(count):
-            growth = react_ref[i, 0] * m[0]
-            for j in range(1, count):
-                growth = growth + react_ref[i, j] * m[j]
-            out_ref[i, 0, row, :] = m[i] + limit * growth
+            growth = growth_ref[i, level, row, :]
+            for tracer, value in values:
+                growth = growth + react_ref[i, tracer] * value
+            out_ref[i, 0, row, :] = field[i, row, :] + limit * growth
         return carry
 
     lax.fori_loop(0, rows // 8, chunk, 0)
@@ -510,28 +546,55 @@
             out_specs=VMEM,
         )(*in_vmem(*sends[:known], *across[:known]))
         bases.append(lax.ppermute(thick, "comp", [(i, i + k) for i in range(comps - k)]))
+    count = reaction.shape[0]
+
+    def grow(terms, arrays, before=()):
+        return call(
+            functools.partial(growth_kernel, terms),
+            4,
+            out_shape=local(count, depth, width, rows),
+            in_specs=[SMEM] + [VMEM] * (len(arrays) + len(before)),
+            out_specs=VMEM,
+        )(reaction, *in_vmem(*arrays, *before))
+
     cross = call(
         gather_kernel,
         2,
-        out_shape=local(8 * depth + 1, width, rows),
-        in_specs=[VMEM] * 12,
+        out_shape=local(6 * depth, width, rows),
+        in_specs=[VMEM] * 6,
         out_specs=VMEM,
-    )(*in_vmem(near, *bases, *other, *across))
+    )(*in_vmem(*other, *across[:2]))
     cross = lax.ppermute(cross, "trc", flip_core)
-
-    count = reaction.shape[0]
+    growth = grow(
+        tuple((i, 0, i, 0) for i in range(4)) + tuple((4 + i, 0, i, 2) for i in range(2)),
+        (*mine, *across[:2]),
+    )
+    growth = grow(
+        tuple((0, i * depth, i, 1) for i in range(4)) + tuple((0, (4 + i) * depth, i, 3) for i in range(2)),
+        (cross,),
+        (growth,),
+    )
+    final = call(
+        last_kernel,
+        1,
+        out_shape=local(2 * depth + 1, width, rows),
+        in_specs=[VMEM] * 6,
+        out_specs=VMEM,
+    )(*in_vmem(near, *bases, *across[2:]))
+    final = lax.ppermute(final, "trc", flip_core)
+    growth = grow(((0, 0, 2, 2), (1, 0, 3, 2)), tuple(across[2:]), (growth,))
     tracers_out, heating = call(
         functools.partial(reaction_kernel, levels),
         6,
         grid=(depth,),
         out_shape=(array(count, depth, width, rows), array(depth, width, rows)),
-        in_specs=[SMEM] + [VMEM] * 14,
+        in_specs=[SMEM] + [VMEM] * 16,
         out_specs=(
             pl.BlockSpec((count, 1, width, rows), lambda l: (0, l, 0, 0)),
             pl.BlockSpec((1, width, rows), lambda l: (l, 0, 0)),
         ),
         scratch_shapes=[local(width, rows), local(count, width, rows)],
-    )(reaction, *in_vmem(sunlight, near, *bases, *mine, *across, cross))
+    )(reaction, *in_vmem(sunlight, near, *bases, growth, *mine, *across, cross, final))
     return (east_out, north_out, tracers_out, heating)
 
 

time: 132 us -> 143 us (1.083)
  the two profiles are of different devices: /device:TPU:1 before, /device:TPU:7 now
where the time goes in v4:
time: 143 us; the launch traced here: 140 us
  waiting for transfers between devices  59.5 us (42%)
  starting transfers between devices  53 us (37%)
  Pallas kernels  26.5 us (19%)
    ppermute x1, waiting for transfers between devices, per_device(): side_one = lax.ppermute(side_one, both, ring(1))  27.6 us
    pallas_call x4, Pallas kernels, per_device(): call(functools.partial(transport_kernel, levels, turn), 6, out_shape=(loc...  12.3 us
    ppermute x3, starting transfers between devices, per_device(): lax.ppermute(thick, 'comp', [(i, i + k) for i in range(comps - k)])  7.42 us
    ppermute x4, waiting for transfers between devices, per_device(): across.append(lax.ppermute(held, 'trc', flip_x))  7.27 us
    ppermute x4, starting transfers between devices, per_device(): across.append(lax.ppermute(held, 'trc', flip_x))  6.64 us
    ppermute x1, starting transfers between devices, per_device(): side_high = lax.ppermute(side_high, 'horiz', backward)  6.23 us
    ppermute x1, starting transfers between devices, per_device(): high = lax.ppermute(high, 'horiz', backward)  6.12 us
    pallas_call x3, Pallas kernels, grow(): call(functools.partial(growth_kernel, terms), 4, out_shape=local(count, d...  5.67 us
  transfers between devices with their start and end apart: 23, of which 11 were waited for; matrix products, arithmetic and copies ran while one was open for 0% of the time, Pallas kernels for 14%

profile of v4, /device:TPU:7, one launch (start us, length us, event | category | flops | bytes accessed | tf_op | source)
XLA Modules:
  0.0 140.1 jit_solution(18388481124991592694)
XLA Ops:
  2.7 3.5 %collective-permute-start = (f32[14,8,256]{2,1,0:T(8,128)S(1)}, f32[14,8,256]{2,1,0:T(8,128)S(1)}, u32[]{:S(2)}, u32[]{:S(2)}) collective-permute-start(f32[14,8,256]{2,1,0:T(8,128)S(1)} %get-tuple-element.35), channel_id=1, source_target_pairs={{0,4},{4,8},{8,12},{12,16},{16,20},{20,24},{24,28},{28,32},{32,36}... | collective-permute-start | bytes 344072 | tf_op jit(solution)/shard_map/ppermute | solution.py:465
  6.3 6.1 %collective-permute-start.1 = (f32[14,8,256]{2,1,0:T(8,128)S(1)}, f32[14,8,256]{2,1,0:T(8,128)S(1)}, u32[]{:S(2)}, u32[]{:S(2)}) collective-permute-start(f32[14,8,256]{2,1,0:T(8,128)S(1)} %get-tuple-element.36), channel_id=1, source_target_pairs={{4,0},{8,4},{12,8},{16,12},{20,16},{24,20},{28,24},{32,28},{36,32}... | collective-permute-start | bytes 344072 | tf_op jit(solution)/shard_map/ppermute | solution.py:466
  15.3 4.7 %collective-permute-start.4 = (f32[3,4,40,256]{3,2,1,0:T(8,128)S(1)}, f32[3,4,40,256]{3,2,1,0:T(8,128)S(1)}, u32[]{:S(2)}, u32[]{:S(2)}) collective-permute-start(f32[3,4,40,256]{3,2,1,0:T(8,128)S(1)} %get-tuple-element.39.own), channel_id=1, source_target_pairs={{3,66},{67,130},{131,194},{64,1},{128,65},{192,129},{7,70},{71,134... | collective-permute-start | bytes 1474568 | tf_op jit(solution)/shard_map/ppermute | solution.py:480
  20.1 5.6 %collective-permute-done.4.near = f32[3,4,40,256]{3,2,1,0:T(8,128)S(1)} collective-permute-done((f32[3,4,40,256]{3,2,1,0:T(8,128)S(1)}, f32[3,4,40,256]{3,2,1,0:T(8,128)S(1)}, u32[]{:S(2)}, u32[]{:S(2)}) %collective-permute-start.4) | collective-permute-done | bytes 491552 | tf_op jit(solution)/shard_map/ppermute | solution.py:480
  27.0 5.6 %collective-permute-done.3.across = f32[3,4,40,256]{3,2,1,0:T(8,128)S(1)} collective-permute-done((f32[3,4,40,256]{3,2,1,0:T(8,128)S(1)}, f32[3,4,40,256]{3,2,1,0:T(8,128)S(1)}, u32[]{:S(2)}, u32[]{:S(2)}) %collective-permute-start.3) | collective-permute-done | bytes 491552 | tf_op jit(solution)/shard_map/ppermute | solution.py:486
  32.6 5.3 %collective-permute-done.5.far = f32[3,4,40,256]{3,2,1,0:T(8,128)S(1)} collective-permute-done((f32[3,4,40,256]{3,2,1,0:T(8,128)S(1)}, f32[3,4,40,256]{3,2,1,0:T(8,128)S(1)}, u32[]{:S(2)}, u32[]{:S(2)}) %collective-permute-start.5) | collective-permute-done | bytes 491552 | tf_op jit(solution)/shard_map/ppermute | solution.py:485
  40.0 6.2 %collective-permute-start.8 = (f32[32,8,256]{2,1,0:T(8,128)S(1)}, f32[32,8,256]{2,1,0:T(8,128)S(1)}, u32[]{:S(2)}, u32[]{:S(2)}) collective-permute-start(f32[32,8,256]{2,1,0:T(8,128)S(1)} %get-tuple-element.41), channel_id=1, source_target_pairs={{4,0},{8,4},{12,8},{16,12},{20,16},{24,20},{28,24},{32,28},{36,32}... | collective-permute-start | bytes 786440 | tf_op jit(solution)/shard_map/ppermute | solution.py:468
  52.8 3.6 %collective-permute-start.9 = (f32[24,40,256]{2,1,0:T(8,128)S(1)}, f32[24,40,256]{2,1,0:T(8,128)S(1)}, u32[]{:S(2)}, u32[]{:S(2)}) collective-permute-start(f32[24,40,256]{2,1,0:T(8,128)S(1)} %get-tuple-element.42), channel_id=1, source_target_pairs={{0,192},{1,129},{2,130},{3,131},{64,0},{65,193},{66,194},{67,195},... | collective-permute-start | bytes 2949128 | tf_op jit(solution)/shard_map/ppermute | solution.py:501
  58.5 2.9 %shard_map.116 = (f32[4,32,256]{2,1,0:T(8,128)S(1)}, f32[4,32,256]{2,1,0:T(8,128)S(1)}, f32[9,32,256]{2,1,0:T(8,128)S(1)}, f32[4,32,256]{2,1,0:T(8,128)S(1)}) custom-call(f32[6,24,40,256]{3,2,1,0:T(8,128)S(1)} %shard_map.114.weight, f32[24,40,256]{2,1,0:T(8,128)S(1)} %get-tuple-element.43.refs_0_), custom_call_target="tpu_custom_call" | custom-call | flops 6000000 | bytes 6000000 | tf_op jit(solution)/shard_map/pallas_call | solution.py:522
  61.4 2.1 %collective-permute-start.14 = (f32[9,32,256]{2,1,0:T(8,128)S(1)}, f32[9,32,256]{2,1,0:T(8,128)S(1)}, u32[]{:S(2)}, u32[]{:S(2)}) collective-permute-start(f32[9,32,256]{2,1,0:T(8,128)S(1)} %get-tuple-element.52.refs_0_), channel_id=1, source_target_pairs={{0,2},{1,3},{2,0},{3,1},{4,6},{5,7},{6,4},{7,5},{8,10},{9,11},{10,... | collective-permute-start | bytes 884744 | tf_op jit(solution)/shard_map/ppermute | solution.py:535
  63.5 27.6 %collective-permute-done.11.refs_1_ = f32[24,8,256]{2,1,0:T(8,128)S(1)} collective-permute-done((f32[24,8,256]{2,1,0:T(8,128)S(1)}, f32[24,8,256]{2,1,0:T(8,128)S(1)}, u32[]{:S(2)}, u32[]{:S(2)}) %collective-permute-start.11) | collective-permute-done | bytes 196640 | tf_op jit(solution)/shard_map/ppermute | solution.py:499
  91.1 2.9 %shard_map.117 = (f32[4,32,256]{2,1,0:T(8,128)S(1)}, f32[4,32,256]{2,1,0:T(8,128)S(1)}, f32[9,32,256]{2,1,0:T(8,128)S(1)}, f32[4,32,256]{2,1,0:T(8,128)S(1)}) custom-call(f32[6,24,40,256]{3,2,1,0:T(8,128)S(1)} %shard_map.114.weight, f32[24,32,256]{2,1,0:T(8,128)S(1)} %collective-permute-done.10.refs_0_, f32[24,8,256]{2,1,0:T(8,128)S(1)} %collective-permute-done.11.refs_1_), custom_call_target="tpu_custom_call" | custom-call | flops 6000000 | bytes 6000000 | tf_op jit(solution)/shard_map/pallas_call | solution.py:522
  96.0 3.3 %collective-permute-done.13.refs_1_ = f32[24,8,256]{2,1,0:T(8,128)S(1)} collective-permute-done((f32[24,8,256]{2,1,0:T(8,128)S(1)}, f32[24,8,256]{2,1,0:T(8,128)S(1)}, u32[]{:S(2)}, u32[]{:S(2)}) %collective-permute-start.13) | collective-permute-done | bytes 196640 | tf_op jit(solution)/shard_map/ppermute | solution.py:500
  99.2 2.9 %shard_map.118 = (f32[4,32,256]{2,1,0:T(8,128)S(1)}, f32[4,32,256]{2,1,0:T(8,128)S(1)}, f32[9,32,256]{2,1,0:T(8,128)S(1)}, f32[4,32,256]{2,1,0:T(8,128)S(1)}) custom-call(f32[6,24,40,256]{3,2,1,0:T(8,128)S(1)} %shard_map.114.weight, f32[24,32,256]{2,1,0:T(8,128)S(1)} %collective-permute-done.12.refs_0_, f32[24,8,256]{2,1,0:T(8,128)S(1)} %collective-permute-done.13.refs_1_), custom_call_target="tpu_custom_call" | custom-call | flops 6000000 | bytes 6000000 | tf_op jit(solution)/shard_map/pallas_call | solution.py:522
  102.2 3.5 %shard_map.119 = (f32[2,32,256]{2,1,0:T(8,128)S(1)}, f32[4,32,256]{2,1,0:T(8,128)S(1)}, f32[4,32,256]{2,1,0:T(8,128)S(1)}, f32[10,32,256]{2,1,0:T(8,128)S(1)}, f32[4,32,256]{2,1,0:T(8,128)}) custom-call(f32[6,24,40,256]{3,2,1,0:T(8,128)S(1)} %shard_map.114.weight, f32[24,40,256]{2,1,0:T(8,128)S(1)} %collective-permute-done.9.refs_0_, ...), custom_call_target="tpu_custom_call" | custom-call | flops 6000000 | bytes 6000000 | tf_op jit(solution)/shard_map/pallas_call | solution.py:522
  105.8 2.6 %collective-permute-start.21 = (f32[24,32,256]{2,1,0:T(8,128)S(1)}, f32[24,32,256]{2,1,0:T(8,128)S(1)}, u32[]{:S(2)}, u32[]{:S(2)}) collective-permute-start(f32[24,32,256]{2,1,0:T(8,128)S(1)} %shard_map.123), channel_id=1, source_target_pairs={{0,1},{1,0},{2,3},{3,2},{4,5},{5,4},{6,7},{7,6},{8,9},{9,8},{10,11... | collective-permute-start | bytes 2359304 | tf_op jit(solution)/shard_map/ppermute | solution.py:567
  108.4 4.5 %collective-permute-start.16 = (f32[9,32,256]{2,1,0:T(8,128)S(1)}, f32[9,32,256]{2,1,0:T(8,128)S(1)}, u32[]{:S(2)}, u32[]{:S(2)}) collective-permute-start(f32[9,32,256]{2,1,0:T(8,128)S(1)} %get-tuple-element.54.refs_2_), channel_id=1, source_target_pairs={{0,2},{1,3},{2,0},{3,1},{4,6},{5,7},{6,4},{7,5},{8,10},{9,11},{10,... | collective-permute-start | bytes 884744 | tf_op jit(solution)/shard_map/ppermute | solution.py:535
  112.8 7.3 %collective-permute-done.16.refs_5_.refs_0_.third.refs_6_ = f32[9,32,256]{2,1,0:T(8,128)S(1)} collective-permute-done((f32[9,32,256]{2,1,0:T(8,128)S(1)}, f32[9,32,256]{2,1,0:T(8,128)S(1)}, u32[]{:S(2)}, u32[]{:S(2)}) %collective-permute-start.16) | collective-permute-done | bytes 294944 | tf_op jit(solution)/shard_map/ppermute | solution.py:535
  120.1 2.6 %collective-permute-start.17 = (f32[32,256]{1,0:T(8,128)S(1)}, f32[32,256]{1,0:T(8,128)S(1)}, u32[]{:S(2)}, u32[]{:S(2)}) collective-permute-start(f32[32,256]{1,0:T(8,128)S(1)} %shard_map.120), channel_id=1, source_target_pairs={{0,64},{64,128},{128,192},{1,65},{65,129},{129,193},{2,66},{66,130... | collective-permute-start | bytes 98312 | tf_op jit(solution)/shard_map/ppermute | solution.py:548
  122.8 3.5 %collective-permute-start.18 = (f32[32,256]{1,0:T(8,128)S(1)}, f32[32,256]{1,0:T(8,128)S(1)}, u32[]{:S(2)}, u32[]{:S(2)}) collective-permute-start(f32[32,256]{1,0:T(8,128)S(1)} %shard_map.121), channel_id=1, source_target_pairs={{0,128},{64,192},{1,129},{65,193},{2,130},{66,194},{3,131},{67,195... | collective-permute-start | bytes 98312 | tf_op jit(solution)/shard_map/ppermute | solution.py:548
  128.6 2.6 %collective-permute-start.22 = (f32[9,32,256]{2,1,0:T(8,128)S(1)}, f32[9,32,256]{2,1,0:T(8,128)S(1)}, u32[]{:S(2)}, u32[]{:S(2)}) collective-permute-start(f32[9,32,256]{2,1,0:T(8,128)S(1)} %shard_map.127), channel_id=1, source_target_pairs={{0,1},{1,0},{2,3},{3,2},{4,5},{5,4},{6,7},{7,6},{8,9},{9,8},{10,11... | collective-permute-start | bytes 884744 | tf_op jit(solution)/shard_map/ppermute | solution.py:584
  131.2 2.2 %shard_map.124.refs_1_ = f32[16,4,32,256]{3,2,1,0:T(8,128)S(1)} custom-call(f32[16,16]{1,0:T(8,128)S(1)} %copy-done.3, f32[4,32,256]{2,1,0:T(8,128)S(1)} %get-tuple-element.60.refs_0_, f32[4,32,256]{2,1,0:T(8,128)S(1)} %get-tuple-element.61.refs_1_, f32[4,32,256]{2,1,0:T(8,128)S(1)} %get-tuple-element.62.refs_2_, ...), custom_call_target="tpu_custom_call" | custom-call | flops 4000000 | bytes 4000000 | tf_op jit(solution)/shard_map/pallas_call | solution.py:552
  133.5 2.1 %shard_map.125.refs_2_ = f32[16,4,32,256]{3,2,1,0:T(8,128)S(1)} custom-call(f32[16,16]{1,0:T(8,128)S(1)} %copy-done.3, f32[24,32,256]{2,1,0:T(8,128)S(1)} %collective-permute-done.21.refs_0_.refs_8_, f32[16,4,32,256]{3,2,1,0:T(8,128)S(1)} %shard_map.124.refs_1_), custom_call_target="tpu_custom_call" | custom-call | flops 4000000 | bytes 4000000 | tf_op jit(solution)/shard_map/pallas_call | solution.py:552
  137.0 3.1 %shard_map.128 = (f32[16,4,32,256]{3,2,1,0:T(8,128)}, f32[4,32,256]{2,1,0:T(8,128)}) custom-call(f32[16,16]{1,0:T(8,128)S(1)} %copy-done.3, f32[32,256]{1,0:T(8,128)S(1)} %copy-done.6, f32[2,32,256]{2,1,0:T(8,128)S(1)} %get-tuple-element.51.near.near_ref, f32[32,256]{1,0:T(8,128)S(1)} %collective-permute-done.17.one, ...), custom_call_target="tpu_custom_call" | custom-call | flops 6000000 | bytes 6000000 | tf_op jit(solution)/shard_map/pallas_call | solution.py:586
  (54 shorter events, 22.8 us)
Async XLA Ops:
  2.7 10.6 %collective-permute-start = (f32[14,8,256]{2,1,0:T(8,128)S(1)}, f32[14,8,256]{2,1,0:T(8,128)S(1)}, u32[]{:S(2)}, u32[]{:S(2)}) collective-permute-start(f32[14,8,256]{2,1,0:T(8,128)S(1)} %get-tuple-element.35), channel_id=1, source_target_pairs={{0,4},{4,8},{8,12},{12,16},{16,20},{20,24},{24,28},{28,32},{32,36}... | collective-permute-start | bytes 344072 | tf_op jit(solution)/shard_map/ppermute | solution.py:465
  6.3 7.9 %collective-permute-start.1 = (f32[14,8,256]{2,1,0:T(8,128)S(1)}, f32[14,8,256]{2,1,0:T(8,128)S(1)}, u32[]{:S(2)}, u32[]{:S(2)}) collective-permute-start(f32[14,8,256]{2,1,0:T(8,128)S(1)} %get-tuple-element.36), channel_id=1, source_target_pairs={{4,0},{8,4},{12,8},{16,12},{20,16},{24,20},{28,24},{32,28},{36,32}... | collective-permute-start | bytes 344072 | tf_op jit(solution)/shard_map/ppermute | solution.py:466
  15.3 10.4 %collective-permute-start.4 = (f32[3,4,40,256]{3,2,1,0:T(8,128)S(1)}, f32[3,4,40,256]{3,2,1,0:T(8,128)S(1)}, u32[]{:S(2)}, u32[]{:S(2)}) collective-permute-start(f32[3,4,40,256]{3,2,1,0:T(8,128)S(1)} %get-tuple-element.39.own), channel_id=1, source_target_pairs={{3,66},{67,130},{131,194},{64,1},{128,65},{192,129},{7,70},{71,134... | collective-permute-start | bytes 1474568 | tf_op jit(solution)/shard_map/ppermute | solution.py:480
  20.0 12.6 %collective-permute-start.3 = (f32[3,4,40,256]{3,2,1,0:T(8,128)S(1)}, f32[3,4,40,256]{3,2,1,0:T(8,128)S(1)}, u32[]{:S(2)}, u32[]{:S(2)}) collective-permute-start(f32[3,4,40,256]{3,2,1,0:T(8,128)S(1)} %get-tuple-element.39.own), channel_id=1, source_target_pairs={{0,2},{1,3},{2,0},{3,1},{4,6},{5,7},{6,4},{7,5},{8,10},{9,11},{10,... | collective-permute-start | bytes 1474568 | tf_op jit(solution)/shard_map/ppermute | solution.py:486
  25.7 12.1 %collective-permute-start.5 = (f32[3,4,40,256]{3,2,1,0:T(8,128)S(1)}, f32[3,4,40,256]{3,2,1,0:T(8,128)S(1)}, u32[]{:S(2)}, u32[]{:S(2)}) collective-permute-start(f32[3,4,40,256]{3,2,1,0:T(8,128)S(1)} %collective-permute-done.4.near), channel_id=1, source_target_pairs={{2,0},{1,3},{6,4},{5,7},{10,8},{9,11},{14,12},{13,15},{18,16},{17,... | collective-permute-start | bytes 1474568 | tf_op jit(solution)/shard_map/ppermute | solution.py:485
  37.9 19.9 %collective-permute-start.6 = (f32[2,3,4,40,256]{4,3,2,1,0:T(8,128)S(1)}, f32[2,3,4,40,256]{4,3,2,1,0:T(8,128)S(1)}, u32[]{:S(2)}, u32[]{:S(2)}) collective-permute-start(f32[2,3,4,40,256]{4,3,2,1,0:T(8,128)S(1)} %shard_map.113.pair), channel_id=1, source_target_pairs={{0,1},{1,0},{2,3},{3,2},{4,5},{5,4},{6,7},{7,6},{8,9},{9,8},{10,11... | collective-permute-start | bytes 2949128 | tf_op jit(solution)/shard_map/ppermute | solution.py:510
  38.0 12.4 %collective-permute-start.7 = (f32[32,8,256]{2,1,0:T(8,128)S(1)}, f32[32,8,256]{2,1,0:T(8,128)S(1)}, u32[]{:S(2)}, u32[]{:S(2)}) collective-permute-start(f32[32,8,256]{2,1,0:T(8,128)S(1)} %get-tuple-element.40), channel_id=1, source_target_pairs={{0,4},{4,8},{8,12},{12,16},{16,20},{20,24},{24,28},{28,32},{32,36}... | collective-permute-start | bytes 786440 | tf_op jit(solution)/shard_map/ppermute | solution.py:467
  40.0 11.4 %collective-permute-start.8 = (f32[32,8,256]{2,1,0:T(8,128)S(1)}, f32[32,8,256]{2,1,0:T(8,128)S(1)}, u32[]{:S(2)}, u32[]{:S(2)}) collective-permute-start(f32[32,8,256]{2,1,0:T(8,128)S(1)} %get-tuple-element.41), channel_id=1, source_target_pairs={{4,0},{8,4},{12,8},{16,12},{20,16},{24,20},{28,24},{32,28},{36,32}... | collective-permute-start | bytes 786440 | tf_op jit(solution)/shard_map/ppermute | solution.py:468
  46.2 44.9 %collective-permute-start.10 = (f32[24,32,256]{2,1,0:T(8,128)S(1)}, f32[24,32,256]{2,1,0:T(8,128)S(1)}, u32[]{:S(2)}, u32[]{:S(2)}) collective-permute-start(f32[24,32,256]{2,1,0:T(8,128)S(1)} %get-tuple-element.45), channel_id=1, source_target_pairs={{0,64},{1,65},{2,66},{3,67},{64,128},{65,129},{66,130},{67,131},{1... | collective-permute-start | bytes 2359304 | tf_op jit(solution)/shard_map/ppermute | solution.py:463
  48.2 8.9 %collective-permute-start.2 = (f32[3,4,40,256]{3,2,1,0:T(8,128)S(1)}, f32[3,4,40,256]{3,2,1,0:T(8,128)S(1)}, u32[]{:S(2)}, u32[]{:S(2)}) collective-permute-start(f32[3,4,40,256]{3,2,1,0:T(8,128)S(1)} %get-tuple-element.39.own), channel_id=1, source_target_pairs={{0,1},{1,0},{2,3},{3,2},{4,5},{5,4},{6,7},{7,6},{8,9},{9,8},{10,11... | collective-permute-start | bytes 1474568 | tf_op jit(solution)/shard_map/ppermute | solution.py:487
  52.8 49.4 %collective-permute-start.9 = (f32[24,40,256]{2,1,0:T(8,128)S(1)}, f32[24,40,256]{2,1,0:T(8,128)S(1)}, u32[]{:S(2)}, u32[]{:S(2)}) collective-permute-start(f32[24,40,256]{2,1,0:T(8,128)S(1)} %get-tuple-element.42), channel_id=1, source_target_pairs={{0,192},{1,129},{2,130},{3,131},{64,0},{65,193},{66,194},{67,195},... | collective-permute-start | bytes 2949128 | tf_op jit(solution)/shard_map/ppermute | solution.py:501
  56.3 42.9 %collective-permute-start.12 = (f32[24,32,256]{2,1,0:T(8,128)S(1)}, f32[24,32,256]{2,1,0:T(8,128)S(1)}, u32[]{:S(2)}, u32[]{:S(2)}) collective-permute-start(f32[24,32,256]{2,1,0:T(8,128)S(1)} %get-tuple-element.48), channel_id=1, source_target_pairs={{0,128},{1,193},{2,194},{3,195},{64,192},{65,1},{66,2},{67,3},{128... | collective-permute-start | bytes 2359304 | tf_op jit(solution)/shard_map/ppermute | solution.py:464
  57.1 34.0 %collective-permute-start.11 = (f32[24,8,256]{2,1,0:T(8,128)S(1)}, f32[24,8,256]{2,1,0:T(8,128)S(1)}, u32[]{:S(2)}, u32[]{:S(2)}) collective-permute-start(f32[24,8,256]{2,1,0:T(8,128)S(1)} %get-tuple-element.46), channel_id=1, source_target_pairs={{0,64},{1,65},{2,66},{3,67},{64,128},{65,129},{66,130},{67,131},{1... | collective-permute-start | bytes 589832 | tf_op jit(solution)/shard_map/ppermute | solution.py:499
  61.4 44.3 %collective-permute-start.14 = (f32[9,32,256]{2,1,0:T(8,128)S(1)}, f32[9,32,256]{2,1,0:T(8,128)S(1)}, u32[]{:S(2)}, u32[]{:S(2)}) collective-permute-start(f32[9,32,256]{2,1,0:T(8,128)S(1)} %get-tuple-element.52.refs_0_), channel_id=1, source_target_pairs={{0,2},{1,3},{2,0},{3,1},{4,6},{5,7},{6,4},{7,5},{8,10},{9,11},{10,... | collective-permute-start | bytes 884744 | tf_op jit(solution)/shard_map/ppermute | solution.py:535
  94.0 11.7 %collective-permute-start.15 = (f32[9,32,256]{2,1,0:T(8,128)S(1)}, f32[9,32,256]{2,1,0:T(8,128)S(1)}, u32[]{:S(2)}, u32[]{:S(2)}) collective-permute-start(f32[9,32,256]{2,1,0:T(8,128)S(1)} %get-tuple-element.53.refs_1_), channel_id=1, source_target_pairs={{0,2},{1,3},{2,0},{3,1},{4,6},{5,7},{6,4},{7,5},{8,10},{9,11},{10,... | collective-permute-start | bytes 884744 | tf_op jit(solution)/shard_map/ppermute | solution.py:535
  94.1 5.1 %collective-permute-start.13 = (f32[24,8,256]{2,1,0:T(8,128)S(1)}, f32[24,8,256]{2,1,0:T(8,128)S(1)}, u32[]{:S(2)}, u32[]{:S(2)}) collective-permute-start(f32[24,8,256]{2,1,0:T(8,128)S(1)} %get-tuple-element.49), channel_id=1, source_target_pairs={{0,128},{1,193},{2,194},{3,195},{64,192},{65,1},{66,2},{67,3},{128... | collective-permute-start | bytes 589832 | tf_op jit(solution)/shard_map/ppermute | solution.py:500
  105.8 27.7 %collective-permute-start.21 = (f32[24,32,256]{2,1,0:T(8,128)S(1)}, f32[24,32,256]{2,1,0:T(8,128)S(1)}, u32[]{:S(2)}, u32[]{:S(2)}) collective-permute-start(f32[24,32,256]{2,1,0:T(8,128)S(1)} %shard_map.123), channel_id=1, source_target_pairs={{0,1},{1,0},{2,3},{3,2},{4,5},{5,4},{6,7},{7,6},{8,9},{9,8},{10,11... | collective-permute-start | bytes 2359304 | tf_op jit(solution)/shard_map/ppermute | solution.py:567
  108.4 11.7 %collective-permute-start.16 = (f32[9,32,256]{2,1,0:T(8,128)S(1)}, f32[9,32,256]{2,1,0:T(8,128)S(1)}, u32[]{:S(2)}, u32[]{:S(2)}) collective-permute-start(f32[9,32,256]{2,1,0:T(8,128)S(1)} %get-tuple-element.54.refs_2_), channel_id=1, source_target_pairs={{0,2},{1,3},{2,0},{3,1},{4,6},{5,7},{6,4},{7,5},{8,10},{9,11},{10,... | collective-permute-start | bytes 884744 | tf_op jit(solution)/shard_map/ppermute | solution.py:535
  112.8 18.4 %copy-start.3 = (f32[16,16]{1,0:T(8,128)S(1)}, f32[16,16]{1,0:T(8,128)}, u32[]{:S(2)}) copy-start(f32[16,16]{1,0:T(8,128)} %react_ref.7) | copy-start | bytes 3076
  112.8 15.8 %collective-permute-start.20 = (f32[10,32,256]{2,1,0:T(8,128)S(1)}, f32[10,32,256]{2,1,0:T(8,128)S(1)}, u32[]{:S(2)}, u32[]{:S(2)}) collective-permute-start(f32[10,32,256]{2,1,0:T(8,128)S(1)} %get-tuple-element.55), channel_id=1, source_target_pairs={{0,2},{1,3},{2,0},{3,1},{4,6},{5,7},{6,4},{7,5},{8,10},{9,11},{10,... | collective-permute-start | bytes 983048 | tf_op jit(solution)/shard_map/ppermute | solution.py:535
  120.1 7.5 %collective-permute-start.17 = (f32[32,256]{1,0:T(8,128)S(1)}, f32[32,256]{1,0:T(8,128)S(1)}, u32[]{:S(2)}, u32[]{:S(2)}) collective-permute-start(f32[32,256]{1,0:T(8,128)S(1)} %shard_map.120), channel_id=1, source_target_pairs={{0,64},{64,128},{128,192},{1,65},{65,129},{129,193},{2,66},{66,130... | collective-permute-start | bytes 98312 | tf_op jit(solution)/shard_map/ppermute | solution.py:548
  122.8 4.8 %collective-permute-start.18 = (f32[32,256]{1,0:T(8,128)S(1)}, f32[32,256]{1,0:T(8,128)S(1)}, u32[]{:S(2)}, u32[]{:S(2)}) collective-permute-start(f32[32,256]{1,0:T(8,128)S(1)} %shard_map.121), channel_id=1, source_target_pairs={{0,128},{64,192},{1,129},{65,193},{2,130},{66,194},{3,131},{67,195... | collective-permute-start | bytes 98312 | tf_op jit(solution)/shard_map/ppermute | solution.py:548
  126.3 2.3 %collective-permute-start.19 = (f32[32,256]{1,0:T(8,128)S(1)}, f32[32,256]{1,0:T(8,128)S(1)}, u32[]{:S(2)}, u32[]{:S(2)}) collective-permute-start(f32[32,256]{1,0:T(8,128)S(1)} %shard_map.122), channel_id=1, source_target_pairs={{0,192},{1,193},{2,194},{3,195},{4,196},{5,197},{6,198},{7,199},{8... | collective-permute-start | bytes 98312 | tf_op jit(solution)/shard_map/ppermute | solution.py:548
  128.6 8.3 %collective-permute-start.22 = (f32[9,32,256]{2,1,0:T(8,128)S(1)}, f32[9,32,256]{2,1,0:T(8,128)S(1)}, u32[]{:S(2)}, u32[]{:S(2)}) collective-permute-start(f32[9,32,256]{2,1,0:T(8,128)S(1)} %shard_map.127), channel_id=1, source_target_pairs={{0,1},{1,0},{2,3},{3,2},{4,5},{5,4},{6,7},{7,6},{8,9},{9,8},{10,11... | collective-permute-start | bytes 884744 | tf_op jit(solution)/shard_map/ppermute | solution.py:584
  (6 other events, 69.0 us)

commit v5 on v4

--- a/solution.py
+++ b/solution.py
@@ -198,7 +198,7 @@
         emit(2, level, kappa)
 
 
-def weight_kernel(own, core, pair, core_pair, weight_ref):
+def weight_kernel(own, across, core, rim, core_rim, weight_ref):
     depth = own.shape[1]
     _, t = position()
     odd = t & 1
@@ -220,16 +220,20 @@
             weight_ref[5, index] = kappa
 
     fill(1 + t, lambda i, l: own[i, l])
-    fill(1 + (t ^ 1), lambda i, l: core[i, l])
-    fill(1 + (t ^ 2), lambda i, l: pair[0, i, l])
-    fill(1 + (t ^ 3), lambda i, l: core_pair[0, i, l])
-    fill(5 * odd, lambda i, l: pair[1, i, l])
-    fill(5 * (1 - odd), lambda i, l: core_pair[1, i, l])
-
-
-def pair_kernel(across, near, far, out):
-    out[0] = across[...]
-    out[1] = near[...] + far[...]
+    fill(1 + (t ^ 1), lambda i, l: core[0, i, l])
+    fill(1 + (t ^ 2), lambda i, l: across[i, l])
+    fill(1 + (t ^ 3), lambda i, l: core[1, i, l])
+    fill(5 * odd, lambda i, l: rim[i, l])
+    fill(5 * (1 - odd), lambda i, l: core_rim[i, l])
+
+
+def pair_kernel(own, across, out):
+    out[0] = own[...]
+    out[1] = across[...]
+
+
+def rim_kernel(near, far, out):
+    out[...] = near[...] + far[...]
 
 
 def transport_kernel(levels, turn, weight, *refs):
@@ -484,7 +488,6 @@
     )
     far = lax.ppermute(near, "trc", [(trcs - 2, 0), (1, trcs - 1)])
     across_flux = lax.ppermute(flux, "trc", flip_x)
-    core_flux = lax.ppermute(flux, "trc", flip_core)
 
     whole = local(tall, span, rows)
     flank = local(tall, 8, rows)
@@ -504,13 +507,17 @@
         pair_kernel,
         1,
         out_shape=local(2, 3, depth, span, rows),
-        in_specs=[VMEM] * 3,
+        in_specs=[VMEM] * 2,
         out_specs=VMEM,
-    )(across_flux, near, far)
-    core_pair = lax.ppermute(pair, "trc", flip_core)
+    )(*in_vmem(flux, across_flux))
+    core_flux = lax.ppermute(pair, "trc", flip_core)
+    rim = call(
+        rim_kernel, 1, out_shape=local(3, depth, span, rows), in_specs=[VMEM] * 2, out_specs=VMEM
+    )(*in_vmem(near, far))
+    core_rim = lax.ppermute(rim, "trc", flip_core)
     weight = call(
-        weight_kernel, 3, out_shape=local(6, tall, span, rows), in_specs=[VMEM] * 4, out_specs=VMEM
-    )(*in_vmem(flux, core_flux, pair, core_pair))
+        weight_kernel, 3, out_shape=local(6, tall, span, rows), in_specs=[VMEM] * 5, out_specs=VMEM
+    )(*in_vmem(flux, across_flux, core_flux, rim, core_rim))
     piece = local(depth, width, rows)
     mine, other, sends, across, sums = [], [], [], [], []
     for turn in range(4):

time: 143 us -> 137 us (0.958)
  waiting for transfers between devices: 59.5 us -> 48.7 us
  starting transfers between devices: 53 us -> 58.2 us
    ppermute x1, waiting for transfers between devices: 5.63 us -> 0.01 us  [per_device(): lax.ppermute(flux, both, [(trcs * i + last, trcs * i + nxt + 2) for i in...]
    ppermute x1, waiting for transfers between devices: 5.27 us -> 0.01 us  [per_device(): far = lax.ppermute(near, 'trc', [(trcs - 2, 0), (1, trcs - 1)])]
    ppermute x2, starting transfers between devices: 1.14 us -> 5.01 us  [the longest x1 2.51 us: per_device(): core_flux = lax.ppermute(pair, 'trc', flip_core)]
    ppermute x1, waiting for transfers between devices: 27.6 us -> 25.7 us  [per_device(): side_one = lax.ppermute(side_one, both, ring(1))]
  transfers between devices with their start and end apart: 23 -> 23, of which waited for: 11 -> 9; matrix products, arithmetic and copies ran while one was open for 0% -> 0% of each run, Pallas kernels for 14% -> 15%
where the time goes in v5:
time: 137 us; the launch traced here: 134 us
  starting transfers between devices  58.2 us (42%)
  waiting for transfers between devices  48.7 us (36%)
  Pallas kernels  26.5 us (19%)
    ppermute x1, waiting for transfers between devices, per_device(): side_one = lax.ppermute(side_one, both, ring(1))  25.7 us
    pallas_call x4, Pallas kernels, per_device(): call(functools.partial(transport_kernel, levels, turn), 6, out_shape=(loc...  12.3 us
    ppermute x4, starting transfers between devices, per_device(): across.append(lax.ppermute(held, 'trc', flip_x))  7.75 us
    ppermute x3, starting transfers between devices, per_device(): lax.ppermute(thick, 'comp', [(i, i + k) for i in range(comps - k)])  7.68 us
    ppermute x4, waiting for transfers between devices, per_device(): across.append(lax.ppermute(held, 'trc', flip_x))  7.27 us
    ppermute x1, waiting for transfers between devices, per_device(): across_flux = lax.ppermute(flux, 'trc', flip_x)  6.93 us
    ppermute x1, starting transfers between devices, per_device(): side_high = lax.ppermute(side_high, 'horiz', backward)  6.26 us
    ppermute x1, starting transfers between devices, per_device(): high = lax.ppermute(high, 'horiz', backward)  6.12 us
  transfers between devices with their start and end apart: 23, of which 9 were waited for; matrix products, arithmetic and copies ran while one was open for 0% of the time, Pallas kernels for 15%

profile of v5, /device:TPU:7, one launch (start us, length us, event | category | flops | bytes accessed | tf_op | source)
XLA Modules:
  0.0 134.5 jit_solution(16728021243982868378)
XLA Ops:
  2.7 3.5 %collective-permute-start = (f32[14,8,256]{2,1,0:T(8,128)S(1)}, f32[14,8,256]{2,1,0:T(8,128)S(1)}, u32[]{:S(2)}, u32[]{:S(2)}) collective-permute-start(f32[14,8,256]{2,1,0:T(8,128)S(1)} %get-tuple-element.35), channel_id=1, source_target_pairs={{0,4},{4,8},{8,12},{12,16},{16,20},{20,24},{24,28},{28,32},{32,36}... | collective-permute-start | bytes 344072 | tf_op jit(solution)/shard_map/ppermute | solution.py:469
  6.3 6.1 %collective-permute-start.1 = (f32[14,8,256]{2,1,0:T(8,128)S(1)}, f32[14,8,256]{2,1,0:T(8,128)S(1)}, u32[]{:S(2)}, u32[]{:S(2)}) collective-permute-start(f32[14,8,256]{2,1,0:T(8,128)S(1)} %get-tuple-element.36), channel_id=1, source_target_pairs={{4,0},{8,4},{12,8},{16,12},{20,16},{24,20},{28,24},{32,28},{36,32}... | collective-permute-start | bytes 344072 | tf_op jit(solution)/shard_map/ppermute | solution.py:470
  16.2 4.9 %collective-permute-start.4 = (f32[3,4,40,256]{3,2,1,0:T(8,128)S(1)}, f32[3,4,40,256]{3,2,1,0:T(8,128)S(1)}, u32[]{:S(2)}, u32[]{:S(2)}) collective-permute-start(f32[3,4,40,256]{3,2,1,0:T(8,128)S(1)} %get-tuple-element.39.own), channel_id=1, source_target_pairs={{3,66},{67,130},{131,194},{64,1},{128,65},{192,129},{7,70},{71,134... | collective-permute-start | bytes 1474568 | tf_op jit(solution)/shard_map/ppermute | solution.py:484
  21.1 6.9 %collective-permute-done.2.across = f32[3,4,40,256]{3,2,1,0:T(8,128)S(1)} collective-permute-done((f32[3,4,40,256]{3,2,1,0:T(8,128)S(1)}, f32[3,4,40,256]{3,2,1,0:T(8,128)S(1)}, u32[]{:S(2)}, u32[]{:S(2)}) %collective-permute-start.2) | collective-permute-done | bytes 491552 | tf_op jit(solution)/shard_map/ppermute | solution.py:490
  28.1 2.5 %collective-permute-start.3 = (f32[2,3,4,40,256]{4,3,2,1,0:T(8,128)S(1)}, f32[2,3,4,40,256]{4,3,2,1,0:T(8,128)S(1)}, u32[]{:S(2)}, u32[]{:S(2)}) collective-permute-start(f32[2,3,4,40,256]{4,3,2,1,0:T(8,128)S(1)} %shard_map.113), channel_id=1, source_target_pairs={{0,1},{1,0},{2,3},{3,2},{4,5},{5,4},{6,7},{7,6},{8,9},{9,8},{10,11... | collective-permute-start | bytes 2949128 | tf_op jit(solution)/shard_map/ppermute | solution.py:513
  33.9 6.3 %collective-permute-start.8 = (f32[32,8,256]{2,1,0:T(8,128)S(1)}, f32[32,8,256]{2,1,0:T(8,128)S(1)}, u32[]{:S(2)}, u32[]{:S(2)}) collective-permute-start(f32[32,8,256]{2,1,0:T(8,128)S(1)} %get-tuple-element.41), channel_id=1, source_target_pairs={{4,0},{8,4},{12,8},{16,12},{20,16},{24,20},{28,24},{32,28},{36,32}... | collective-permute-start | bytes 786440 | tf_op jit(solution)/shard_map/ppermute | solution.py:472
  41.5 2.1 %collective-permute-done.7.low = f32[32,8,256]{2,1,0:T(8,128)S(1)} collective-permute-done((f32[32,8,256]{2,1,0:T(8,128)S(1)}, f32[32,8,256]{2,1,0:T(8,128)S(1)}, u32[]{:S(2)}, u32[]{:S(2)}) %collective-permute-start.7) | collective-permute-done | bytes 262176 | tf_op jit(solution)/shard_map/ppermute | solution.py:471
  45.9 3.0 %collective-permute-start.9 = (f32[24,40,256]{2,1,0:T(8,128)S(1)}, f32[24,40,256]{2,1,0:T(8,128)S(1)}, u32[]{:S(2)}, u32[]{:S(2)}) collective-permute-start(f32[24,40,256]{2,1,0:T(8,128)S(1)} %get-tuple-element.42), channel_id=1, source_target_pairs={{0,192},{1,129},{2,130},{3,131},{64,0},{65,193},{66,194},{67,195},... | collective-permute-start | bytes 2949128 | tf_op jit(solution)/shard_map/ppermute | solution.py:504
  48.9 2.5 %collective-permute-start.6 = (f32[3,4,40,256]{3,2,1,0:T(8,128)S(1)}, f32[3,4,40,256]{3,2,1,0:T(8,128)S(1)}, u32[]{:S(2)}, u32[]{:S(2)}) collective-permute-start(f32[3,4,40,256]{3,2,1,0:T(8,128)S(1)} %shard_map.114.rim), channel_id=1, source_target_pairs={{0,1},{1,0},{2,3},{3,2},{4,5},{5,4},{6,7},{7,6},{8,9},{9,8},{10,11... | collective-permute-start | bytes 1474568 | tf_op jit(solution)/shard_map/ppermute | solution.py:517
  53.6 2.9 %shard_map.117 = (f32[4,32,256]{2,1,0:T(8,128)S(1)}, f32[4,32,256]{2,1,0:T(8,128)S(1)}, f32[9,32,256]{2,1,0:T(8,128)S(1)}, f32[4,32,256]{2,1,0:T(8,128)S(1)}) custom-call(f32[6,24,40,256]{3,2,1,0:T(8,128)S(1)} %shard_map.115.weight, f32[24,40,256]{2,1,0:T(8,128)S(1)} %get-tuple-element.43.refs_0_), custom_call_target="tpu_custom_call" | custom-call | flops 6000000 | bytes 6000000 | tf_op jit(solution)/shard_map/pallas_call | solution.py:529
  57.7 25.7 %collective-permute-done.11.refs_1_ = f32[24,8,256]{2,1,0:T(8,128)S(1)} collective-permute-done((f32[24,8,256]{2,1,0:T(8,128)S(1)}, f32[24,8,256]{2,1,0:T(8,128)S(1)}, u32[]{:S(2)}, u32[]{:S(2)}) %collective-permute-start.11) | collective-permute-done | bytes 196640 | tf_op jit(solution)/shard_map/ppermute | solution.py:502
  83.4 2.9 %shard_map.118 = (f32[4,32,256]{2,1,0:T(8,128)S(1)}, f32[4,32,256]{2,1,0:T(8,128)S(1)}, f32[9,32,256]{2,1,0:T(8,128)S(1)}, f32[4,32,256]{2,1,0:T(8,128)S(1)}) custom-call(f32[6,24,40,256]{3,2,1,0:T(8,128)S(1)} %shard_map.115.weight, f32[24,32,256]{2,1,0:T(8,128)S(1)} %collective-permute-done.10.refs_0_, f32[24,8,256]{2,1,0:T(8,128)S(1)} %collective-permute-done.11.refs_1_), custom_call_target="tpu_custom_call" | custom-call | flops 6000000 | bytes 6000000 | tf_op jit(solution)/shard_map/pallas_call | solution.py:529
  86.3 2.1 %collective-permute-start.15 = (f32[9,32,256]{2,1,0:T(8,128)S(1)}, f32[9,32,256]{2,1,0:T(8,128)S(1)}, u32[]{:S(2)}, u32[]{:S(2)}) collective-permute-start(f32[9,32,256]{2,1,0:T(8,128)S(1)} %get-tuple-element.53.refs_1_), channel_id=1, source_target_pairs={{0,2},{1,3},{2,0},{3,1},{4,6},{5,7},{6,4},{7,5},{8,10},{9,11},{10,... | collective-permute-start | bytes 884744 | tf_op jit(solution)/shard_map/ppermute | solution.py:542
  90.3 3.1 %collective-permute-done.13.refs_1_ = f32[24,8,256]{2,1,0:T(8,128)S(1)} collective-permute-done((f32[24,8,256]{2,1,0:T(8,128)S(1)}, f32[24,8,256]{2,1,0:T(8,128)S(1)}, u32[]{:S(2)}, u32[]{:S(2)}) %collective-permute-start.13) | collective-permute-done | bytes 196640 | tf_op jit(solution)/shard_map/ppermute | solution.py:503
  93.4 2.9 %shard_map.119 = (f32[4,32,256]{2,1,0:T(8,128)S(1)}, f32[4,32,256]{2,1,0:T(8,128)S(1)}, f32[9,32,256]{2,1,0:T(8,128)S(1)}, f32[4,32,256]{2,1,0:T(8,128)S(1)}) custom-call(f32[6,24,40,256]{3,2,1,0:T(8,128)S(1)} %shard_map.115.weight, f32[24,32,256]{2,1,0:T(8,128)S(1)} %collective-permute-done.12.refs_0_, f32[24,8,256]{2,1,0:T(8,128)S(1)} %collective-permute-done.13.refs_1_), custom_call_target="tpu_custom_call" | custom-call | flops 6000000 | bytes 6000000 | tf_op jit(solution)/shard_map/pallas_call | solution.py:529
  96.4 3.5 %shard_map.120 = (f32[2,32,256]{2,1,0:T(8,128)S(1)}, f32[4,32,256]{2,1,0:T(8,128)S(1)}, f32[4,32,256]{2,1,0:T(8,128)S(1)}, f32[10,32,256]{2,1,0:T(8,128)S(1)}, f32[4,32,256]{2,1,0:T(8,128)}) custom-call(f32[6,24,40,256]{3,2,1,0:T(8,128)S(1)} %shard_map.115.weight, f32[24,40,256]{2,1,0:T(8,128)S(1)} %collective-permute-done.9.refs_0_, ...), custom_call_target="tpu_custom_call" | custom-call | flops 6000000 | bytes 6000000 | tf_op jit(solution)/shard_map/pallas_call | solution.py:529
  100.0 2.4 %collective-permute-start.21 = (f32[24,32,256]{2,1,0:T(8,128)S(1)}, f32[24,32,256]{2,1,0:T(8,128)S(1)}, u32[]{:S(2)}, u32[]{:S(2)}) collective-permute-start(f32[24,32,256]{2,1,0:T(8,128)S(1)} %shard_map.124), channel_id=1, source_target_pairs={{0,1},{1,0},{2,3},{3,2},{4,5},{5,4},{6,7},{7,6},{8,9},{9,8},{10,11... | collective-permute-start | bytes 2359304 | tf_op jit(solution)/shard_map/ppermute | solution.py:574
  102.4 4.4 %collective-permute-start.16 = (f32[9,32,256]{2,1,0:T(8,128)S(1)}, f32[9,32,256]{2,1,0:T(8,128)S(1)}, u32[]{:S(2)}, u32[]{:S(2)}) collective-permute-start(f32[9,32,256]{2,1,0:T(8,128)S(1)} %get-tuple-element.54.refs_2_), channel_id=1, source_target_pairs={{0,2},{1,3},{2,0},{3,1},{4,6},{5,7},{6,4},{7,5},{8,10},{9,11},{10,... | collective-permute-start | bytes 884744 | tf_op jit(solution)/shard_map/ppermute | solution.py:542
  106.8 7.3 %collective-permute-done.16.refs_5_.refs_0_.third.refs_6_ = f32[9,32,256]{2,1,0:T(8,128)S(1)} collective-permute-done((f32[9,32,256]{2,1,0:T(8,128)S(1)}, f32[9,32,256]{2,1,0:T(8,128)S(1)}, u32[]{:S(2)}, u32[]{:S(2)}) %collective-permute-start.16) | collective-permute-done | bytes 294944 | tf_op jit(solution)/shard_map/ppermute | solution.py:542
  116.1 4.4 %collective-permute-start.18 = (f32[32,256]{1,0:T(8,128)S(1)}, f32[32,256]{1,0:T(8,128)S(1)}, u32[]{:S(2)}, u32[]{:S(2)}) collective-permute-start(f32[32,256]{1,0:T(8,128)S(1)} %shard_map.122), channel_id=1, source_target_pairs={{0,128},{64,192},{1,129},{65,193},{2,130},{66,194},{3,131},{67,195... | collective-permute-start | bytes 98312 | tf_op jit(solution)/shard_map/ppermute | solution.py:555
  122.9 2.7 %collective-permute-start.22 = (f32[9,32,256]{2,1,0:T(8,128)S(1)}, f32[9,32,256]{2,1,0:T(8,128)S(1)}, u32[]{:S(2)}, u32[]{:S(2)}) collective-permute-start(f32[9,32,256]{2,1,0:T(8,128)S(1)} %shard_map.128), channel_id=1, source_target_pairs={{0,1},{1,0},{2,3},{3,2},{4,5},{5,4},{6,7},{7,6},{8,9},{9,8},{10,11... | collective-permute-start | bytes 884744 | tf_op jit(solution)/shard_map/ppermute | solution.py:591
  125.6 2.2 %shard_map.125.refs_1_ = f32[16,4,32,256]{3,2,1,0:T(8,128)S(1)} custom-call(f32[16,16]{1,0:T(8,128)S(1)} %copy-done.3, f32[4,32,256]{2,1,0:T(8,128)S(1)} %get-tuple-element.60.refs_0_, f32[4,32,256]{2,1,0:T(8,128)S(1)} %get-tuple-element.61.refs_1_, f32[4,32,256]{2,1,0:T(8,128)S(1)} %get-tuple-element.62.refs_2_, ...), custom_call_target="tpu_custom_call" | custom-call | flops 4000000 | bytes 4000000 | tf_op jit(solution)/shard_map/pallas_call | solution.py:559
  127.9 2.1 %shard_map.126.refs_2_ = f32[16,4,32,256]{3,2,1,0:T(8,128)S(1)} custom-call(f32[16,16]{1,0:T(8,128)S(1)} %copy-done.3, f32[24,32,256]{2,1,0:T(8,128)S(1)} %collective-permute-done.21.refs_0_.refs_8_, f32[16,4,32,256]{3,2,1,0:T(8,128)S(1)} %shard_map.125.refs_1_), custom_call_target="tpu_custom_call" | custom-call | flops 4000000 | bytes 4000000 | tf_op jit(solution)/shard_map/pallas_call | solution.py:559
  131.4 3.1 %shard_map.129 = (f32[16,4,32,256]{3,2,1,0:T(8,128)}, f32[4,32,256]{2,1,0:T(8,128)}) custom-call(f32[16,16]{1,0:T(8,128)S(1)} %copy-done.3, f32[32,256]{1,0:T(8,128)S(1)} %copy-done.6, f32[2,32,256]{2,1,0:T(8,128)S(1)} %get-tuple-element.51.near.near_ref, f32[32,256]{1,0:T(8,128)S(1)} %collective-permute-done.17.one, ...), custom_call_target="tpu_custom_call" | custom-call | flops 6000000 | bytes 6000000 | tf_op jit(solution)/shard_map/pallas_call | solution.py:593
  (55 shorter events, 23.8 us)
Async XLA Ops:
  2.7 10.6 %collective-permute-start = (f32[14,8,256]{2,1,0:T(8,128)S(1)}, f32[14,8,256]{2,1,0:T(8,128)S(1)}, u32[]{:S(2)}, u32[]{:S(2)}) collective-permute-start(f32[14,8,256]{2,1,0:T(8,128)S(1)} %get-tuple-element.35), channel_id=1, source_target_pairs={{0,4},{4,8},{8,12},{12,16},{16,20},{20,24},{24,28},{28,32},{32,36}... | collective-permute-start | bytes 344072 | tf_op jit(solution)/shard_map/ppermute | solution.py:469
  6.3 7.9 %collective-permute-start.1 = (f32[14,8,256]{2,1,0:T(8,128)S(1)}, f32[14,8,256]{2,1,0:T(8,128)S(1)}, u32[]{:S(2)}, u32[]{:S(2)}) collective-permute-start(f32[14,8,256]{2,1,0:T(8,128)S(1)} %get-tuple-element.36), channel_id=1, source_target_pairs={{4,0},{8,4},{12,8},{16,12},{20,16},{24,20},{28,24},{32,28},{36,32}... | collective-permute-start | bytes 344072 | tf_op jit(solution)/shard_map/ppermute | solution.py:470
  15.3 12.7 %collective-permute-start.2 = (f32[3,4,40,256]{3,2,1,0:T(8,128)S(1)}, f32[3,4,40,256]{3,2,1,0:T(8,128)S(1)}, u32[]{:S(2)}, u32[]{:S(2)}) collective-permute-start(f32[3,4,40,256]{3,2,1,0:T(8,128)S(1)} %get-tuple-element.39.own), channel_id=1, source_target_pairs={{0,2},{1,3},{2,0},{3,1},{4,6},{5,7},{6,4},{7,5},{8,10},{9,11},{10,... | collective-permute-start | bytes 1474568 | tf_op jit(solution)/shard_map/ppermute | solution.py:490
  16.2 14.5 %collective-permute-start.4 = (f32[3,4,40,256]{3,2,1,0:T(8,128)S(1)}, f32[3,4,40,256]{3,2,1,0:T(8,128)S(1)}, u32[]{:S(2)}, u32[]{:S(2)}) collective-permute-start(f32[3,4,40,256]{3,2,1,0:T(8,128)S(1)} %get-tuple-element.39.own), channel_id=1, source_target_pairs={{3,66},{67,130},{131,194},{64,1},{128,65},{192,129},{7,70},{71,134... | collective-permute-start | bytes 1474568 | tf_op jit(solution)/shard_map/ppermute | solution.py:484
  28.1 24.1 %collective-permute-start.3 = (f32[2,3,4,40,256]{4,3,2,1,0:T(8,128)S(1)}, f32[2,3,4,40,256]{4,3,2,1,0:T(8,128)S(1)}, u32[]{:S(2)}, u32[]{:S(2)}) collective-permute-start(f32[2,3,4,40,256]{4,3,2,1,0:T(8,128)S(1)} %shard_map.113), channel_id=1, source_target_pairs={{0,1},{1,0},{2,3},{3,2},{4,5},{5,4},{6,7},{7,6},{8,9},{9,8},{10,11... | collective-permute-start | bytes 2949128 | tf_op jit(solution)/shard_map/ppermute | solution.py:513
  30.6 18.2 %collective-permute-start.5 = (f32[3,4,40,256]{3,2,1,0:T(8,128)S(1)}, f32[3,4,40,256]{3,2,1,0:T(8,128)S(1)}, u32[]{:S(2)}, u32[]{:S(2)}) collective-permute-start(f32[3,4,40,256]{3,2,1,0:T(8,128)S(1)} %collective-permute-done.4.near), channel_id=1, source_target_pairs={{2,0},{1,3},{6,4},{5,7},{10,8},{9,11},{14,12},{13,15},{18,16},{17,... | collective-permute-start | bytes 1474568 | tf_op jit(solution)/shard_map/ppermute | solution.py:489
  31.9 11.7 %collective-permute-start.7 = (f32[32,8,256]{2,1,0:T(8,128)S(1)}, f32[32,8,256]{2,1,0:T(8,128)S(1)}, u32[]{:S(2)}, u32[]{:S(2)}) collective-permute-start(f32[32,8,256]{2,1,0:T(8,128)S(1)} %get-tuple-element.40), channel_id=1, source_target_pairs={{0,4},{4,8},{8,12},{12,16},{16,20},{20,24},{24,28},{28,32},{32,36}... | collective-permute-start | bytes 786440 | tf_op jit(solution)/shard_map/ppermute | solution.py:471
  33.9 10.6 %collective-permute-start.8 = (f32[32,8,256]{2,1,0:T(8,128)S(1)}, f32[32,8,256]{2,1,0:T(8,128)S(1)}, u32[]{:S(2)}, u32[]{:S(2)}) collective-permute-start(f32[32,8,256]{2,1,0:T(8,128)S(1)} %get-tuple-element.41), channel_id=1, source_target_pairs={{4,0},{8,4},{12,8},{16,12},{20,16},{24,20},{28,24},{32,28},{36,32}... | collective-permute-start | bytes 786440 | tf_op jit(solution)/shard_map/ppermute | solution.py:472
  40.1 43.2 %collective-permute-start.10 = (f32[24,32,256]{2,1,0:T(8,128)S(1)}, f32[24,32,256]{2,1,0:T(8,128)S(1)}, u32[]{:S(2)}, u32[]{:S(2)}) collective-permute-start(f32[24,32,256]{2,1,0:T(8,128)S(1)} %get-tuple-element.45), channel_id=1, source_target_pairs={{0,64},{1,65},{2,66},{3,67},{64,128},{65,129},{66,130},{67,131},{1... | collective-permute-start | bytes 2359304 | tf_op jit(solution)/shard_map/ppermute | solution.py:467
  45.9 50.5 %collective-permute-start.9 = (f32[24,40,256]{2,1,0:T(8,128)S(1)}, f32[24,40,256]{2,1,0:T(8,128)S(1)}, u32[]{:S(2)}, u32[]{:S(2)}) collective-permute-start(f32[24,40,256]{2,1,0:T(8,128)S(1)} %get-tuple-element.42), channel_id=1, source_target_pairs={{0,192},{1,129},{2,130},{3,131},{64,0},{65,193},{66,194},{67,195},... | collective-permute-start | bytes 2949128 | tf_op jit(solution)/shard_map/ppermute | solution.py:504
  48.9 4.0 %collective-permute-start.6 = (f32[3,4,40,256]{3,2,1,0:T(8,128)S(1)}, f32[3,4,40,256]{3,2,1,0:T(8,128)S(1)}, u32[]{:S(2)}, u32[]{:S(2)}) collective-permute-start(f32[3,4,40,256]{3,2,1,0:T(8,128)S(1)} %shard_map.114.rim), channel_id=1, source_target_pairs={{0,1},{1,0},{2,3},{3,2},{4,5},{5,4},{6,7},{7,6},{8,9},{9,8},{10,11... | collective-permute-start | bytes 1474568 | tf_op jit(solution)/shard_map/ppermute | solution.py:517
  51.4 42.0 %collective-permute-start.12 = (f32[24,32,256]{2,1,0:T(8,128)S(1)}, f32[24,32,256]{2,1,0:T(8,128)S(1)}, u32[]{:S(2)}, u32[]{:S(2)}) collective-permute-start(f32[24,32,256]{2,1,0:T(8,128)S(1)} %get-tuple-element.48), channel_id=1, source_target_pairs={{0,128},{1,193},{2,194},{3,195},{64,192},{65,1},{66,2},{67,3},{128... | collective-permute-start | bytes 2359304 | tf_op jit(solution)/shard_map/ppermute | solution.py:468
  52.2 31.2 %collective-permute-start.11 = (f32[24,8,256]{2,1,0:T(8,128)S(1)}, f32[24,8,256]{2,1,0:T(8,128)S(1)}, u32[]{:S(2)}, u32[]{:S(2)}) collective-permute-start(f32[24,8,256]{2,1,0:T(8,128)S(1)} %get-tuple-element.46), channel_id=1, source_target_pairs={{0,64},{1,65},{2,66},{3,67},{64,128},{65,129},{66,130},{67,131},{1... | collective-permute-start | bytes 589832 | tf_op jit(solution)/shard_map/ppermute | solution.py:502
  56.5 43.4 %collective-permute-start.14 = (f32[9,32,256]{2,1,0:T(8,128)S(1)}, f32[9,32,256]{2,1,0:T(8,128)S(1)}, u32[]{:S(2)}, u32[]{:S(2)}) collective-permute-start(f32[9,32,256]{2,1,0:T(8,128)S(1)} %get-tuple-element.52.refs_0_), channel_id=1, source_target_pairs={{0,2},{1,3},{2,0},{3,1},{4,6},{5,7},{6,4},{7,5},{8,10},{9,11},{10,... | collective-permute-start | bytes 884744 | tf_op jit(solution)/shard_map/ppermute | solution.py:542
  86.3 13.6 %collective-permute-start.15 = (f32[9,32,256]{2,1,0:T(8,128)S(1)}, f32[9,32,256]{2,1,0:T(8,128)S(1)}, u32[]{:S(2)}, u32[]{:S(2)}) collective-permute-start(f32[9,32,256]{2,1,0:T(8,128)S(1)} %get-tuple-element.53.refs_1_), channel_id=1, source_target_pairs={{0,2},{1,3},{2,0},{3,1},{4,6},{5,7},{6,4},{7,5},{8,10},{9,11},{10,... | collective-permute-start | bytes 884744 | tf_op jit(solution)/shard_map/ppermute | solution.py:542
  88.4 5.0 %collective-permute-start.13 = (f32[24,8,256]{2,1,0:T(8,128)S(1)}, f32[24,8,256]{2,1,0:T(8,128)S(1)}, u32[]{:S(2)}, u32[]{:S(2)}) collective-permute-start(f32[24,8,256]{2,1,0:T(8,128)S(1)} %get-tuple-element.49), channel_id=1, source_target_pairs={{0,128},{1,193},{2,194},{3,195},{64,192},{65,1},{66,2},{67,3},{128... | collective-permute-start | bytes 589832 | tf_op jit(solution)/shard_map/ppermute | solution.py:503
  100.0 27.9 %collective-permute-start.21 = (f32[24,32,256]{2,1,0:T(8,128)S(1)}, f32[24,32,256]{2,1,0:T(8,128)S(1)}, u32[]{:S(2)}, u32[]{:S(2)}) collective-permute-start(f32[24,32,256]{2,1,0:T(8,128)S(1)} %shard_map.124), channel_id=1, source_target_pairs={{0,1},{1,0},{2,3},{3,2},{4,5},{5,4},{6,7},{7,6},{8,9},{9,8},{10,11... | collective-permute-start | bytes 2359304 | tf_op jit(solution)/shard_map/ppermute | solution.py:574
  102.4 11.7 %collective-permute-start.16 = (f32[9,32,256]{2,1,0:T(8,128)S(1)}, f32[9,32,256]{2,1,0:T(8,128)S(1)}, u32[]{:S(2)}, u32[]{:S(2)}) collective-permute-start(f32[9,32,256]{2,1,0:T(8,128)S(1)} %get-tuple-element.54.refs_2_), channel_id=1, source_target_pairs={{0,2},{1,3},{2,0},{3,1},{4,6},{5,7},{6,4},{7,5},{8,10},{9,11},{10,... | collective-permute-start | bytes 884744 | tf_op jit(solution)/shard_map/ppermute | solution.py:542
  106.8 18.8 %copy-start.3 = (f32[16,16]{1,0:T(8,128)S(1)}, f32[16,16]{1,0:T(8,128)}, u32[]{:S(2)}) copy-start(f32[16,16]{1,0:T(8,128)} %react_ref.7) | copy-start | bytes 3076
  106.8 16.1 %collective-permute-start.20 = (f32[10,32,256]{2,1,0:T(8,128)S(1)}, f32[10,32,256]{2,1,0:T(8,128)S(1)}, u32[]{:S(2)}, u32[]{:S(2)}) collective-permute-start(f32[10,32,256]{2,1,0:T(8,128)S(1)} %get-tuple-element.55), channel_id=1, source_target_pairs={{0,2},{1,3},{2,0},{3,1},{4,6},{5,7},{6,4},{7,5},{8,10},{9,11},{10,... | collective-permute-start | bytes 983048 | tf_op jit(solution)/shard_map/ppermute | solution.py:542
  114.1 7.8 %collective-permute-start.17 = (f32[32,256]{1,0:T(8,128)S(1)}, f32[32,256]{1,0:T(8,128)S(1)}, u32[]{:S(2)}, u32[]{:S(2)}) collective-permute-start(f32[32,256]{1,0:T(8,128)S(1)} %shard_map.121), channel_id=1, source_target_pairs={{0,64},{64,128},{128,192},{1,65},{65,129},{129,193},{2,66},{66,130... | collective-permute-start | bytes 98312 | tf_op jit(solution)/shard_map/ppermute | solution.py:555
  116.1 5.8 %collective-permute-start.18 = (f32[32,256]{1,0:T(8,128)S(1)}, f32[32,256]{1,0:T(8,128)S(1)}, u32[]{:S(2)}, u32[]{:S(2)}) collective-permute-start(f32[32,256]{1,0:T(8,128)S(1)} %shard_map.122), channel_id=1, source_target_pairs={{0,128},{64,192},{1,129},{65,193},{2,130},{66,194},{3,131},{67,195... | collective-permute-start | bytes 98312 | tf_op jit(solution)/shard_map/ppermute | solution.py:555
  120.6 2.3 %collective-permute-start.19 = (f32[32,256]{1,0:T(8,128)S(1)}, f32[32,256]{1,0:T(8,128)S(1)}, u32[]{:S(2)}, u32[]{:S(2)}) collective-permute-start(f32[32,256]{1,0:T(8,128)S(1)} %shard_map.123), channel_id=1, source_target_pairs={{0,192},{1,193},{2,194},{3,195},{4,196},{5,197},{6,198},{7,199},{8... | collective-permute-start | bytes 98312 | tf_op jit(solution)/shard_map/ppermute | solution.py:555
  122.9 8.5 %collective-permute-start.22 = (f32[9,32,256]{2,1,0:T(8,128)S(1)}, f32[9,32,256]{2,1,0:T(8,128)S(1)}, u32[]{:S(2)}, u32[]{:S(2)}) collective-permute-start(f32[9,32,256]{2,1,0:T(8,128)S(1)} %shard_map.128), channel_id=1, source_target_pairs={{0,1},{1,0},{2,3},{3,2},{4,5},{5,4},{6,7},{7,6},{8,9},{9,8},{10,11... | collective-permute-start | bytes 884744 | tf_op jit(solution)/shard_map/ppermute | solution.py:591
  (6 other events, 69.0 us)

commit v6 on v5

--- a/solution.py
+++ b/solution.py
@@ -198,8 +198,9 @@
         emit(2, level, kappa)
 
 
-def weight_kernel(own, across, core, rim, core_rim, weight_ref):
-    depth = own.shape[1]
+def weight_kernel(*refs):
+    pieces, weight_ref = refs[:-1], refs[-1]
+    depth = pieces[-1].shape[-3]
     _, t = position()
     odd = t & 1
 
@@ -219,12 +220,16 @@
             weight_ref[4, index] = jnp.maximum(fs, 0.0)
             weight_ref[5, index] = kappa
 
-    fill(1 + t, lambda i, l: own[i, l])
-    fill(1 + (t ^ 1), lambda i, l: core[0, i, l])
-    fill(1 + (t ^ 2), lambda i, l: across[i, l])
-    fill(1 + (t ^ 3), lambda i, l: core[1, i, l])
-    fill(5 * odd, lambda i, l: rim[i, l])
-    fill(5 * (1 - odd), lambda i, l: core_rim[i, l])
+    if len(pieces) == 2:
+        own, core = pieces
+        fill(1 + t, lambda i, l: own[0, i, l])
+        fill(1 + (t ^ 2), lambda i, l: own[1, i, l])
+        fill(1 + (t ^ 1), lambda i, l: core[0, i, l])
+        fill(1 + (t ^ 3), lambda i, l: core[1, i, l])
+    else:
+        _, rim, core_rim = pieces
+        fill(5 * odd, lambda i, l: rim[i, l])
+        fill(5 * (1 - odd), lambda i, l: core_rim[i, l])
 
 
 def pair_kernel(own, across, out):
@@ -515,9 +520,18 @@
         rim_kernel, 1, out_shape=local(3, depth, span, rows), in_specs=[VMEM] * 2, out_specs=VMEM
     )(*in_vmem(near, far))
     core_rim = lax.ppermute(rim, "trc", flip_core)
+    weight = local(6, tall, span, rows)
+    weight_inner = call(
+        weight_kernel, 2, out_shape=weight, in_specs=[VMEM] * 2, out_specs=VMEM
+    )(*in_vmem(pair, core_flux))
     weight = call(
-        weight_kernel, 3, out_shape=local(6, tall, span, rows), in_specs=[VMEM] * 5, out_specs=VMEM
-    )(*in_vmem(flux, across_flux, core_flux, rim, core_rim))
+        weight_kernel,
+        1,
+        out_shape=weight,
+        in_specs=[VMEM] * 3,
+        out_specs=VMEM,
+        input_output_aliases={0: 0},
+    )(*in_vmem(weight_inner, rim, core_rim))
     piece = local(depth, width, rows)
     mine, other, sends, across, sums = [], [], [], [], []
     for turn in range(4):

time: 137 us -> 137 us (level)
  no operation moved by 1% of the time
where the time goes in v6:
time: 137 us; the launch traced here: 134 us
  starting transfers between devices  58 us (42%)
  waiting for transfers between devices  49 us (36%)
  Pallas kernels  26.5 us (19%)
    ppermute x1, waiting for transfers between devices, per_device(): side_one = lax.ppermute(side_one, both, ring(1))  26 us
    pallas_call x4, Pallas kernels, per_device(): call(functools.partial(transport_kernel, levels, turn), 6, out_shape=(loc...  12.3 us
    ppermute x3, starting transfers between devices, per_device(): lax.ppermute(thick, 'comp', [(i, i + k) for i in range(comps - k)])  7.68 us
    ppermute x4, starting transfers between devices, per_device(): across.append(lax.ppermute(held, 'trc', flip_x))  7.46 us
    ppermute x4, waiting for transfers between devices, per_device(): across.append(lax.ppermute(held, 'trc', flip_x))  7.27 us
    ppermute x1, waiting for transfers between devices, per_device(): across_flux = lax.ppermute(flux, 'trc', flip_x)  6.93 us
    ppermute x1, starting transfers between devices, per_device(): side_high = lax.ppermute(side_high, 'horiz', backward)  6.26 us
    ppermute x1, starting transfers between devices, per_device(): high = lax.ppermute(high, 'horiz', backward)  6.12 us
  transfers between devices with their start and end apart: 23, of which 9 were waited for; matrix products, arithmetic and copies ran while one was open for 0% of the time, Pallas kernels for 15%

profile of v6, /device:TPU:7, one launch (start us, length us, event | category | flops | bytes accessed | tf_op | source)
XLA Modules:
  0.0 134.5 jit_solution(16977889495641663738)
XLA Ops:
  2.7 3.5 %collective-permute-start = (f32[14,8,256]{2,1,0:T(8,128)S(1)}, f32[14,8,256]{2,1,0:T(8,128)S(1)}, u32[]{:S(2)}, u32[]{:S(2)}) collective-permute-start(f32[14,8,256]{2,1,0:T(8,128)S(1)} %get-tuple-element.35), channel_id=1, source_target_pairs={{0,4},{4,8},{8,12},{12,16},{16,20},{20,24},{24,28},{28,32},{32,36}... | collective-permute-start | bytes 344072 | tf_op jit(solution)/shard_map/ppermute | solution.py:474
  6.3 6.1 %collective-permute-start.1 = (f32[14,8,256]{2,1,0:T(8,128)S(1)}, f32[14,8,256]{2,1,0:T(8,128)S(1)}, u32[]{:S(2)}, u32[]{:S(2)}) collective-permute-start(f32[14,8,256]{2,1,0:T(8,128)S(1)} %get-tuple-element.36), channel_id=1, source_target_pairs={{4,0},{8,4},{12,8},{16,12},{20,16},{24,20},{28,24},{32,28},{36,32}... | collective-permute-start | bytes 344072 | tf_op jit(solution)/shard_map/ppermute | solution.py:475
  16.2 4.9 %collective-permute-start.4 = (f32[3,4,40,256]{3,2,1,0:T(8,128)S(1)}, f32[3,4,40,256]{3,2,1,0:T(8,128)S(1)}, u32[]{:S(2)}, u32[]{:S(2)}) collective-permute-start(f32[3,4,40,256]{3,2,1,0:T(8,128)S(1)} %get-tuple-element.39.own), channel_id=1, source_target_pairs={{3,66},{67,130},{131,194},{64,1},{128,65},{192,129},{7,70},{71,134... | collective-permute-start | bytes 1474568 | tf_op jit(solution)/shard_map/ppermute | solution.py:489
  21.1 6.9 %collective-permute-done.2.across = f32[3,4,40,256]{3,2,1,0:T(8,128)S(1)} collective-permute-done((f32[3,4,40,256]{3,2,1,0:T(8,128)S(1)}, f32[3,4,40,256]{3,2,1,0:T(8,128)S(1)}, u32[]{:S(2)}, u32[]{:S(2)}) %collective-permute-start.2) | collective-permute-done | bytes 491552 | tf_op jit(solution)/shard_map/ppermute | solution.py:495
  28.1 2.5 %collective-permute-start.3 = (f32[2,3,4,40,256]{4,3,2,1,0:T(8,128)S(1)}, f32[2,3,4,40,256]{4,3,2,1,0:T(8,128)S(1)}, u32[]{:S(2)}, u32[]{:S(2)}) collective-permute-start(f32[2,3,4,40,256]{4,3,2,1,0:T(8,128)S(1)} %shard_map.113.refs_0_), channel_id=1, source_target_pairs={{0,1},{1,0},{2,3},{3,2},{4,5},{5,4},{6,7},{7,6},{8,9},{9,8},{10,11... | collective-permute-start | bytes 2949128 | tf_op jit(solution)/shard_map/ppermute | solution.py:518
  33.9 6.3 %collective-permute-start.8 = (f32[32,8,256]{2,1,0:T(8,128)S(1)}, f32[32,8,256]{2,1,0:T(8,128)S(1)}, u32[]{:S(2)}, u32[]{:S(2)}) collective-permute-start(f32[32,8,256]{2,1,0:T(8,128)S(1)} %get-tuple-element.41), channel_id=1, source_target_pairs={{4,0},{8,4},{12,8},{16,12},{20,16},{24,20},{28,24},{32,28},{36,32}... | collective-permute-start | bytes 786440 | tf_op jit(solution)/shard_map/ppermute | solution.py:477
  41.5 2.1 %collective-permute-done.7.low = f32[32,8,256]{2,1,0:T(8,128)S(1)} collective-permute-done((f32[32,8,256]{2,1,0:T(8,128)S(1)}, f32[32,8,256]{2,1,0:T(8,128)S(1)}, u32[]{:S(2)}, u32[]{:S(2)}) %collective-permute-start.7) | collective-permute-done | bytes 262176 | tf_op jit(solution)/shard_map/ppermute | solution.py:476
  45.9 3.0 %collective-permute-start.9 = (f32[24,40,256]{2,1,0:T(8,128)S(1)}, f32[24,40,256]{2,1,0:T(8,128)S(1)}, u32[]{:S(2)}, u32[]{:S(2)}) collective-permute-start(f32[24,40,256]{2,1,0:T(8,128)S(1)} %get-tuple-element.42), channel_id=1, source_target_pairs={{0,192},{1,129},{2,130},{3,131},{64,0},{65,193},{66,194},{67,195},... | collective-permute-start | bytes 2949128 | tf_op jit(solution)/shard_map/ppermute | solution.py:509
  48.9 2.5 %collective-permute-start.6 = (f32[3,4,40,256]{3,2,1,0:T(8,128)S(1)}, f32[3,4,40,256]{3,2,1,0:T(8,128)S(1)}, u32[]{:S(2)}, u32[]{:S(2)}) collective-permute-start(f32[3,4,40,256]{3,2,1,0:T(8,128)S(1)} %shard_map.115.refs_1_), channel_id=1, source_target_pairs={{0,1},{1,0},{2,3},{3,2},{4,5},{5,4},{6,7},{7,6},{8,9},{9,8},{10,11... | collective-permute-start | bytes 1474568 | tf_op jit(solution)/shard_map/ppermute | solution.py:522
  53.6 2.9 %shard_map.118 = (f32[4,32,256]{2,1,0:T(8,128)S(1)}, f32[4,32,256]{2,1,0:T(8,128)S(1)}, f32[9,32,256]{2,1,0:T(8,128)S(1)}, f32[4,32,256]{2,1,0:T(8,128)S(1)}) custom-call(f32[6,24,40,256]{3,2,1,0:T(8,128)S(1)} %shard_map.116.weight, f32[24,40,256]{2,1,0:T(8,128)S(1)} %get-tuple-element.43.refs_0_), custom_call_target="tpu_custom_call" | custom-call | flops 6000000 | bytes 6000000 | tf_op jit(solution)/shard_map/pallas_call | solution.py:543
  57.4 26.0 %collective-permute-done.11.refs_1_ = f32[24,8,256]{2,1,0:T(8,128)S(1)} collective-permute-done((f32[24,8,256]{2,1,0:T(8,128)S(1)}, f32[24,8,256]{2,1,0:T(8,128)S(1)}, u32[]{:S(2)}, u32[]{:S(2)}) %collective-permute-start.11) | collective-permute-done | bytes 196640 | tf_op jit(solution)/shard_map/ppermute | solution.py:507
  83.4 2.9 %shard_map.119 = (f32[4,32,256]{2,1,0:T(8,128)S(1)}, f32[4,32,256]{2,1,0:T(8,128)S(1)}, f32[9,32,256]{2,1,0:T(8,128)S(1)}, f32[4,32,256]{2,1,0:T(8,128)S(1)}) custom-call(f32[6,24,40,256]{3,2,1,0:T(8,128)S(1)} %shard_map.116.weight, f32[24,32,256]{2,1,0:T(8,128)S(1)} %collective-permute-done.10.refs_0_, f32[24,8,256]{2,1,0:T(8,128)S(1)} %collective-permute-done.11.refs_1_), custom_call_target="tpu_custom_call" | custom-call | flops 6000000 | bytes 6000000 | tf_op jit(solution)/shard_map/pallas_call | solution.py:543
  86.3 2.1 %collective-permute-start.15 = (f32[9,32,256]{2,1,0:T(8,128)S(1)}, f32[9,32,256]{2,1,0:T(8,128)S(1)}, u32[]{:S(2)}, u32[]{:S(2)}) collective-permute-start(f32[9,32,256]{2,1,0:T(8,128)S(1)} %get-tuple-element.53.refs_1_), channel_id=1, source_target_pairs={{0,2},{1,3},{2,0},{3,1},{4,6},{5,7},{6,4},{7,5},{8,10},{9,11},{10,... | collective-permute-start | bytes 884744 | tf_op jit(solution)/shard_map/ppermute | solution.py:556
  90.3 3.1 %collective-permute-done.13.refs_1_ = f32[24,8,256]{2,1,0:T(8,128)S(1)} collective-permute-done((f32[24,8,256]{2,1,0:T(8,128)S(1)}, f32[24,8,256]{2,1,0:T(8,128)S(1)}, u32[]{:S(2)}, u32[]{:S(2)}) %collective-permute-start.13) | collective-permute-done | bytes 196640 | tf_op jit(solution)/shard_map/ppermute | solution.py:508
  93.4 2.9 %shard_map.120 = (f32[4,32,256]{2,1,0:T(8,128)S(1)}, f32[4,32,256]{2,1,0:T(8,128)S(1)}, f32[9,32,256]{2,1,0:T(8,128)S(1)}, f32[4,32,256]{2,1,0:T(8,128)S(1)}) custom-call(f32[6,24,40,256]{3,2,1,0:T(8,128)S(1)} %shard_map.116.weight, f32[24,32,256]{2,1,0:T(8,128)S(1)} %collective-permute-done.12.refs_0_, f32[24,8,256]{2,1,0:T(8,128)S(1)} %collective-permute-done.13.refs_1_), custom_call_target="tpu_custom_call" | custom-call | flops 6000000 | bytes 6000000 | tf_op jit(solution)/shard_map/pallas_call | solution.py:543
  96.4 3.5 %shard_map.121 = (f32[2,32,256]{2,1,0:T(8,128)S(1)}, f32[4,32,256]{2,1,0:T(8,128)S(1)}, f32[4,32,256]{2,1,0:T(8,128)S(1)}, f32[10,32,256]{2,1,0:T(8,128)S(1)}, f32[4,32,256]{2,1,0:T(8,128)}) custom-call(f32[6,24,40,256]{3,2,1,0:T(8,128)S(1)} %shard_map.116.weight, f32[24,40,256]{2,1,0:T(8,128)S(1)} %collective-permute-done.9.refs_0_, ...), custom_call_target="tpu_custom_call" | custom-call | flops 6000000 | bytes 6000000 | tf_op jit(solution)/shard_map/pallas_call | solution.py:543
  100.0 2.4 %collective-permute-start.21 = (f32[24,32,256]{2,1,0:T(8,128)S(1)}, f32[24,32,256]{2,1,0:T(8,128)S(1)}, u32[]{:S(2)}, u32[]{:S(2)}) collective-permute-start(f32[24,32,256]{2,1,0:T(8,128)S(1)} %shard_map.125), channel_id=1, source_target_pairs={{0,1},{1,0},{2,3},{3,2},{4,5},{5,4},{6,7},{7,6},{8,9},{9,8},{10,11... | collective-permute-start | bytes 2359304 | tf_op jit(solution)/shard_map/ppermute | solution.py:588
  102.4 4.4 %collective-permute-start.16 = (f32[9,32,256]{2,1,0:T(8,128)S(1)}, f32[9,32,256]{2,1,0:T(8,128)S(1)}, u32[]{:S(2)}, u32[]{:S(2)}) collective-permute-start(f32[9,32,256]{2,1,0:T(8,128)S(1)} %get-tuple-element.54.refs_2_), channel_id=1, source_target_pairs={{0,2},{1,3},{2,0},{3,1},{4,6},{5,7},{6,4},{7,5},{8,10},{9,11},{10,... | collective-permute-start | bytes 884744 | tf_op jit(solution)/shard_map/ppermute | solution.py:556
  106.8 7.3 %collective-permute-done.16.refs_5_.refs_0_.third.refs_6_ = f32[9,32,256]{2,1,0:T(8,128)S(1)} collective-permute-done((f32[9,32,256]{2,1,0:T(8,128)S(1)}, f32[9,32,256]{2,1,0:T(8,128)S(1)}, u32[]{:S(2)}, u32[]{:S(2)}) %collective-permute-start.16) | collective-permute-done | bytes 294944 | tf_op jit(solution)/shard_map/ppermute | solution.py:556
  116.1 4.4 %collective-permute-start.18 = (f32[32,256]{1,0:T(8,128)S(1)}, f32[32,256]{1,0:T(8,128)S(1)}, u32[]{:S(2)}, u32[]{:S(2)}) collective-permute-start(f32[32,256]{1,0:T(8,128)S(1)} %shard_map.123), channel_id=1, source_target_pairs={{0,128},{64,192},{1,129},{65,193},{2,130},{66,194},{3,131},{67,195... | collective-permute-start | bytes 98312 | tf_op jit(solution)/shard_map/ppermute | solution.py:569
  122.9 2.7 %collective-permute-start.22 = (f32[9,32,256]{2,1,0:T(8,128)S(1)}, f32[9,32,256]{2,1,0:T(8,128)S(1)}, u32[]{:S(2)}, u32[]{:S(2)}) collective-permute-start(f32[9,32,256]{2,1,0:T(8,128)S(1)} %shard_map.129), channel_id=1, source_target_pairs={{0,1},{1,0},{2,3},{3,2},{4,5},{5,4},{6,7},{7,6},{8,9},{9,8},{10,11... | collective-permute-start | bytes 884744 | tf_op jit(solution)/shard_map/ppermute | solution.py:605
  125.6 2.2 %shard_map.126.refs_1_ = f32[16,4,32,256]{3,2,1,0:T(8,128)S(1)} custom-call(f32[16,16]{1,0:T(8,128)S(1)} %copy-done.3, f32[4,32,256]{2,1,0:T(8,128)S(1)} %get-tuple-element.60.refs_0_, f32[4,32,256]{2,1,0:T(8,128)S(1)} %get-tuple-element.61.refs_1_, f32[4,32,256]{2,1,0:T(8,128)S(1)} %get-tuple-element.62.refs_2_, ...), custom_call_target="tpu_custom_call" | custom-call | flops 4000000 | bytes 4000000 | tf_op jit(solution)/shard_map/pallas_call | solution.py:573
  127.9 2.1 %shard_map.127.refs_2_ = f32[16,4,32,256]{3,2,1,0:T(8,128)S(1)} custom-call(f32[16,16]{1,0:T(8,128)S(1)} %copy-done.3, f32[24,32,256]{2,1,0:T(8,128)S(1)} %collective-permute-done.21.refs_0_.refs_8_, f32[16,4,32,256]{3,2,1,0:T(8,128)S(1)} %shard_map.126.refs_1_), custom_call_target="tpu_custom_call" | custom-call | flops 4000000 | bytes 4000000 | tf_op jit(solution)/shard_map/pallas_call | solution.py:573
  131.4 3.1 %shard_map.130 = (f32[16,4,32,256]{3,2,1,0:T(8,128)}, f32[4,32,256]{2,1,0:T(8,128)}) custom-call(f32[16,16]{1,0:T(8,128)S(1)} %copy-done.3, f32[32,256]{1,0:T(8,128)S(1)} %copy-done.6, f32[2,32,256]{2,1,0:T(8,128)S(1)} %get-tuple-element.51.near.near_ref, f32[32,256]{1,0:T(8,128)S(1)} %collective-permute-done.17.one, ...), custom_call_target="tpu_custom_call" | custom-call | flops 6000000 | bytes 6000000 | tf_op jit(solution)/shard_map/pallas_call | solution.py:607
  (56 shorter events, 23.5 us)
Async XLA Ops:
  2.7 10.6 %collective-permute-start = (f32[14,8,256]{2,1,0:T(8,128)S(1)}, f32[14,8,256]{2,1,0:T(8,128)S(1)}, u32[]{:S(2)}, u32[]{:S(2)}) collective-permute-start(f32[14,8,256]{2,1,0:T(8,128)S(1)} %get-tuple-element.35), channel_id=1, source_target_pairs={{0,4},{4,8},{8,12},{12,16},{16,20},{20,24},{24,28},{28,32},{32,36}... | collective-permute-start | bytes 344072 | tf_op jit(solution)/shard_map/ppermute | solution.py:474
  6.3 7.9 %collective-permute-start.1 = (f32[14,8,256]{2,1,0:T(8,128)S(1)}, f32[14,8,256]{2,1,0:T(8,128)S(1)}, u32[]{:S(2)}, u32[]{:S(2)}) collective-permute-start(f32[14,8,256]{2,1,0:T(8,128)S(1)} %get-tuple-element.36), channel_id=1, source_target_pairs={{4,0},{8,4},{12,8},{16,12},{20,16},{24,20},{28,24},{32,28},{36,32}... | collective-permute-start | bytes 344072 | tf_op jit(solution)/shard_map/ppermute | solution.py:475
  15.3 12.7 %collective-permute-start.2 = (f32[3,4,40,256]{3,2,1,0:T(8,128)S(1)}, f32[3,4,40,256]{3,2,1,0:T(8,128)S(1)}, u32[]{:S(2)}, u32[]{:S(2)}) collective-permute-start(f32[3,4,40,256]{3,2,1,0:T(8,128)S(1)} %get-tuple-element.39.own), channel_id=1, source_target_pairs={{0,2},{1,3},{2,0},{3,1},{4,6},{5,7},{6,4},{7,5},{8,10},{9,11},{10,... | collective-permute-start | bytes 1474568 | tf_op jit(solution)/shard_map/ppermute | solution.py:495
  16.2 14.5 %collective-permute-start.4 = (f32[3,4,40,256]{3,2,1,0:T(8,128)S(1)}, f32[3,4,40,256]{3,2,1,0:T(8,128)S(1)}, u32[]{:S(2)}, u32[]{:S(2)}) collective-permute-start(f32[3,4,40,256]{3,2,1,0:T(8,128)S(1)} %get-tuple-element.39.own), channel_id=1, source_target_pairs={{3,66},{67,130},{131,194},{64,1},{128,65},{192,129},{7,70},{71,134... | collective-permute-start | bytes 1474568 | tf_op jit(solution)/shard_map/ppermute | solution.py:489
  28.1 24.1 %collective-permute-start.3 = (f32[2,3,4,40,256]{4,3,2,1,0:T(8,128)S(1)}, f32[2,3,4,40,256]{4,3,2,1,0:T(8,128)S(1)}, u32[]{:S(2)}, u32[]{:S(2)}) collective-permute-start(f32[2,3,4,40,256]{4,3,2,1,0:T(8,128)S(1)} %shard_map.113.refs_0_), channel_id=1, source_target_pairs={{0,1},{1,0},{2,3},{3,2},{4,5},{5,4},{6,7},{7,6},{8,9},{9,8},{10,11... | collective-permute-start | bytes 2949128 | tf_op jit(solution)/shard_map/ppermute | solution.py:518
  30.6 18.2 %collective-permute-start.5 = (f32[3,4,40,256]{3,2,1,0:T(8,128)S(1)}, f32[3,4,40,256]{3,2,1,0:T(8,128)S(1)}, u32[]{:S(2)}, u32[]{:S(2)}) collective-permute-start(f32[3,4,40,256]{3,2,1,0:T(8,128)S(1)} %collective-permute-done.4.near), channel_id=1, source_target_pairs={{2,0},{1,3},{6,4},{5,7},{10,8},{9,11},{14,12},{13,15},{18,16},{17,... | collective-permute-start | bytes 1474568 | tf_op jit(solution)/shard_map/ppermute | solution.py:494
  31.9 11.7 %collective-permute-start.7 = (f32[32,8,256]{2,1,0:T(8,128)S(1)}, f32[32,8,256]{2,1,0:T(8,128)S(1)}, u32[]{:S(2)}, u32[]{:S(2)}) collective-permute-start(f32[32,8,256]{2,1,0:T(8,128)S(1)} %get-tuple-element.40), channel_id=1, source_target_pairs={{0,4},{4,8},{8,12},{12,16},{16,20},{20,24},{24,28},{28,32},{32,36}... | collective-permute-start | bytes 786440 | tf_op jit(solution)/shard_map/ppermute | solution.py:476
  33.9 10.6 %collective-permute-start.8 = (f32[32,8,256]{2,1,0:T(8,128)S(1)}, f32[32,8,256]{2,1,0:T(8,128)S(1)}, u32[]{:S(2)}, u32[]{:S(2)}) collective-permute-start(f32[32,8,256]{2,1,0:T(8,128)S(1)} %get-tuple-element.41), channel_id=1, source_target_pairs={{4,0},{8,4},{12,8},{16,12},{20,16},{24,20},{28,24},{32,28},{36,32}... | collective-permute-start | bytes 786440 | tf_op jit(solution)/shard_map/ppermute | solution.py:477
  40.1 43.2 %collective-permute-start.10 = (f32[24,32,256]{2,1,0:T(8,128)S(1)}, f32[24,32,256]{2,1,0:T(8,128)S(1)}, u32[]{:S(2)}, u32[]{:S(2)}) collective-permute-start(f32[24,32,256]{2,1,0:T(8,128)S(1)} %get-tuple-element.45), channel_id=1, source_target_pairs={{0,64},{1,65},{2,66},{3,67},{64,128},{65,129},{66,130},{67,131},{1... | collective-permute-start | bytes 2359304 | tf_op jit(solution)/shard_map/ppermute | solution.py:472
  45.9 50.5 %collective-permute-start.9 = (f32[24,40,256]{2,1,0:T(8,128)S(1)}, f32[24,40,256]{2,1,0:T(8,128)S(1)}, u32[]{:S(2)}, u32[]{:S(2)}) collective-permute-start(f32[24,40,256]{2,1,0:T(8,128)S(1)} %get-tuple-element.42), channel_id=1, source_target_pairs={{0,192},{1,129},{2,130},{3,131},{64,0},{65,193},{66,194},{67,195},... | collective-permute-start | bytes 2949128 | tf_op jit(solution)/shard_map/ppermute | solution.py:509
  48.9 4.5 %collective-permute-start.6 = (f32[3,4,40,256]{3,2,1,0:T(8,128)S(1)}, f32[3,4,40,256]{3,2,1,0:T(8,128)S(1)}, u32[]{:S(2)}, u32[]{:S(2)}) collective-permute-start(f32[3,4,40,256]{3,2,1,0:T(8,128)S(1)} %shard_map.115.refs_1_), channel_id=1, source_target_pairs={{0,1},{1,0},{2,3},{3,2},{4,5},{5,4},{6,7},{7,6},{8,9},{9,8},{10,11... | collective-permute-start | bytes 1474568 | tf_op jit(solution)/shard_map/ppermute | solution.py:522
  51.4 42.0 %collective-permute-start.12 = (f32[24,32,256]{2,1,0:T(8,128)S(1)}, f32[24,32,256]{2,1,0:T(8,128)S(1)}, u32[]{:S(2)}, u32[]{:S(2)}) collective-permute-start(f32[24,32,256]{2,1,0:T(8,128)S(1)} %get-tuple-element.48), channel_id=1, source_target_pairs={{0,128},{1,193},{2,194},{3,195},{64,192},{65,1},{66,2},{67,3},{128... | collective-permute-start | bytes 2359304 | tf_op jit(solution)/shard_map/ppermute | solution.py:473
  52.2 31.2 %collective-permute-start.11 = (f32[24,8,256]{2,1,0:T(8,128)S(1)}, f32[24,8,256]{2,1,0:T(8,128)S(1)}, u32[]{:S(2)}, u32[]{:S(2)}) collective-permute-start(f32[24,8,256]{2,1,0:T(8,128)S(1)} %get-tuple-element.46), channel_id=1, source_target_pairs={{0,64},{1,65},{2,66},{3,67},{64,128},{65,129},{66,130},{67,131},{1... | collective-permute-start | bytes 589832 | tf_op jit(solution)/shard_map/ppermute | solution.py:507
  56.5 43.4 %collective-permute-start.14 = (f32[9,32,256]{2,1,0:T(8,128)S(1)}, f32[9,32,256]{2,1,0:T(8,128)S(1)}, u32[]{:S(2)}, u32[]{:S(2)}) collective-permute-start(f32[9,32,256]{2,1,0:T(8,128)S(1)} %get-tuple-element.52.refs_0_), channel_id=1, source_target_pairs={{0,2},{1,3},{2,0},{3,1},{4,6},{5,7},{6,4},{7,5},{8,10},{9,11},{10,... | collective-permute-start | bytes 884744 | tf_op jit(solution)/shard_map/ppermute | solution.py:556
  86.3 13.6 %collective-permute-start.15 = (f32[9,32,256]{2,1,0:T(8,128)S(1)}, f32[9,32,256]{2,1,0:T(8,128)S(1)}, u32[]{:S(2)}, u32[]{:S(2)}) collective-permute-start(f32[9,32,256]{2,1,0:T(8,128)S(1)} %get-tuple-element.53.refs_1_), channel_id=1, source_target_pairs={{0,2},{1,3},{2,0},{3,1},{4,6},{5,7},{6,4},{7,5},{8,10},{9,11},{10,... | collective-permute-start | bytes 884744 | tf_op jit(solution)/shard_map/ppermute | solution.py:556
  88.4 5.0 %collective-permute-start.13 = (f32[24,8,256]{2,1,0:T(8,128)S(1)}, f32[24,8,256]{2,1,0:T(8,128)S(1)}, u32[]{:S(2)}, u32[]{:S(2)}) collective-permute-start(f32[24,8,256]{2,1,0:T(8,128)S(1)} %get-tuple-element.49), channel_id=1, source_target_pairs={{0,128},{1,193},{2,194},{3,195},{64,192},{65,1},{66,2},{67,3},{128... | collective-permute-start | bytes 589832 | tf_op jit(solution)/shard_map/ppermute | solution.py:508
  100.0 27.9 %collective-permute-start.21 = (f32[24,32,256]{2,1,0:T(8,128)S(1)}, f32[24,32,256]{2,1,0:T(8,128)S(1)}, u32[]{:S(2)}, u32[]{:S(2)}) collective-permute-start(f32[24,32,256]{2,1,0:T(8,128)S(1)} %shard_map.125), channel_id=1, source_target_pairs={{0,1},{1,0},{2,3},{3,2},{4,5},{5,4},{6,7},{7,6},{8,9},{9,8},{10,11... | collective-permute-start | bytes 2359304 | tf_op jit(solution)/shard_map/ppermute | solution.py:588
  102.4 11.7 %collective-permute-start.16 = (f32[9,32,256]{2,1,0:T(8,128)S(1)}, f32[9,32,256]{2,1,0:T(8,128)S(1)}, u32[]{:S(2)}, u32[]{:S(2)}) collective-permute-start(f32[9,32,256]{2,1,0:T(8,128)S(1)} %get-tuple-element.54.refs_2_), channel_id=1, source_target_pairs={{0,2},{1,3},{2,0},{3,1},{4,6},{5,7},{6,4},{7,5},{8,10},{9,11},{10,... | collective-permute-start | bytes 884744 | tf_op jit(solution)/shard_map/ppermute | solution.py:556
  106.8 18.8 %copy-start.3 = (f32[16,16]{1,0:T(8,128)S(1)}, f32[16,16]{1,0:T(8,128)}, u32[]{:S(2)}) copy-start(f32[16,16]{1,0:T(8,128)} %react_ref.7) | copy-start | bytes 3076
  106.8 16.1 %collective-permute-start.20 = (f32[10,32,256]{2,1,0:T(8,128)S(1)}, f32[10,32,256]{2,1,0:T(8,128)S(1)}, u32[]{:S(2)}, u32[]{:S(2)}) collective-permute-start(f32[10,32,256]{2,1,0:T(8,128)S(1)} %get-tuple-element.55), channel_id=1, source_target_pairs={{0,2},{1,3},{2,0},{3,1},{4,6},{5,7},{6,4},{7,5},{8,10},{9,11},{10,... | collective-permute-start | bytes 983048 | tf_op jit(solution)/shard_map/ppermute | solution.py:556
  114.1 7.8 %collective-permute-start.17 = (f32[32,256]{1,0:T(8,128)S(1)}, f32[32,256]{1,0:T(8,128)S(1)}, u32[]{:S(2)}, u32[]{:S(2)}) collective-permute-start(f32[32,256]{1,0:T(8,128)S(1)} %shard_map.122), channel_id=1, source_target_pairs={{0,64},{64,128},{128,192},{1,65},{65,129},{129,193},{2,66},{66,130... | collective-permute-start | bytes 98312 | tf_op jit(solution)/shard_map/ppermute | solution.py:569
  116.1 5.8 %collective-permute-start.18 = (f32[32,256]{1,0:T(8,128)S(1)}, f32[32,256]{1,0:T(8,128)S(1)}, u32[]{:S(2)}, u32[]{:S(2)}) collective-permute-start(f32[32,256]{1,0:T(8,128)S(1)} %shard_map.123), channel_id=1, source_target_pairs={{0,128},{64,192},{1,129},{65,193},{2,130},{66,194},{3,131},{67,195... | collective-permute-start | bytes 98312 | tf_op jit(solution)/shard_map/ppermute | solution.py:569
  120.6 2.3 %collective-permute-start.19 = (f32[32,256]{1,0:T(8,128)S(1)}, f32[32,256]{1,0:T(8,128)S(1)}, u32[]{:S(2)}, u32[]{:S(2)}) collective-permute-start(f32[32,256]{1,0:T(8,128)S(1)} %shard_map.124), channel_id=1, source_target_pairs={{0,192},{1,193},{2,194},{3,195},{4,196},{5,197},{6,198},{7,199},{8... | collective-permute-start | bytes 98312 | tf_op jit(solution)/shard_map/ppermute | solution.py:569
  122.9 8.5 %collective-permute-start.22 = (f32[9,32,256]{2,1,0:T(8,128)S(1)}, f32[9,32,256]{2,1,0:T(8,128)S(1)}, u32[]{:S(2)}, u32[]{:S(2)}) collective-permute-start(f32[9,32,256]{2,1,0:T(8,128)S(1)} %shard_map.129), channel_id=1, source_target_pairs={{0,1},{1,0},{2,3},{3,2},{4,5},{5,4},{6,7},{7,6},{8,9},{9,8},{10,11... | collective-permute-start | bytes 884744 | tf_op jit(solution)/shard_map/ppermute | solution.py:605
  (6 other events, 69.0 us)
